TPU v7x, 32 devices: a whole 2x2x4 slice. The times are simulated.
32 devices in a mesh: expert: 4 (over z), fsdp: 8 (over y, x, core).
Axes of the slice: x: 2, y: 2, z: 4, core: 2. Of those that a mesh axis runs over, the one named last changes fastest.
Arguments:
- tokens: bfloat16 [25216, 512], P(('expert', 'fsdp')), may hold values from -6 to 6
- routes: int32 [25216, 2], P(('expert', 'fsdp')), may hold values from 0 to 7, all different within a row; in each aligned block of 788 rows (0 to 787, 788 to 1575, ...) at most 394 rows name the same one
- cotangent: bfloat16 [25216, 512], P(('expert', 'fsdp')), may hold values from -6 to 6
- attend_gain: float32 [512], P('fsdp'), may hold values from 0.5 to 1.5
- attend_bias: float32 [512], P('fsdp'), may hold values from -1.25 to 1.25
- triple_weight: float32 [512, 1536], P('fsdp'), may hold values from -0.25 to 0.25
- merge_weight: float32 [512, 512], P('fsdp'), may hold values from -2 to 2
- mixture_gain: float32 [512], P('fsdp'), may hold values from 0.5 to 1.5
- mixture_bias: float32 [512], P('fsdp'), may hold values from -1.25 to 1.25
- router_weight: float32 [512, 8], P('fsdp'), may hold values from -0.125 to 0.125
- expert_up: float32 [8, 512, 2048], P('expert', 'fsdp'), may hold values from -0.25 to 0.25
- expert_down: float32 [8, 2048, 512], P('expert', 'fsdp'), may hold values from -0.75 to 0.75
Outputs:
- block_out: bfloat16 [25216, 512], P(('expert', 'fsdp'))
- tokens_grad: float32 [25216, 512], P(('expert', 'fsdp'))
- attendgain_grad: float32 [512], P('fsdp')
- attendbias_grad: float32 [512], P('fsdp')
- triple_grad: float32 [512, 1536], P('fsdp')
- merge_grad: float32 [512, 512], P('fsdp')
- mixturegain_grad: float32 [512], P('fsdp')
- mixturebias_grad: float32 [512], P('fsdp')
- router_grad: float32 [512, 8], P('fsdp')
- expertup_grad: float32 [8, 512, 2048], P('expert', 'fsdp')
- expertdown_grad: float32 [8, 2048, 512], P('expert', 'fsdp')
Inputs may be any that keep to these rules, and one draw needn't show every extreme that they name: `routes`: each token names 2 different experts. Among the 788 tokens of one device no expert is named by more than 394 tokens, a bound that some block reaches of them; every expert is named by some token.
All inputs are finite; a program needn't handle non-finite values.
Results may differ from a plain program's by a relative error of at most 0.02.
Values may be sent and summed in bfloat16 or wider, within the bound.
A program may use at most 192 MiB of HBM per device.

v0:
```python
from functools import partial

import jax
import jax.numpy as jnp
from jax import lax
from jax.sharding import PartitionSpec as P

HEAD_DIM = 64
TOP = 2
SEQ = 197


EPSILON = 1e-06


def layer_norm(values, gain, bias):
    center = values - jnp.mean(values, -1, keepdims=True)
    spread = jnp.mean(center * center, -1, keepdims=True)
    return center * lax.rsqrt(spread + EPSILON) * gain + bias


def local(
    tokens,
    routes,
    cotangent,
    attend_gain,
    attend_bias,
    triple_weight,
    merge_weight,
    mixture_gain,
    mixture_bias,
    router_weight,
    expert_up,
    expert_down,
):
    local_rows = tokens.shape[0]
    width = tokens.shape[1]
    experts = router_weight.shape[1]
    owners = lax.axis_size("expert")
    per_owner = expert_up.shape[0]
    capacity = 2 * TOP * local_rows // experts
    images = local_rows // SEQ
    heads = width // HEAD_DIM
    scale = 1.0 / HEAD_DIM**0.5
    spread_rows = owners * capacity
    gain_one, bias_one, triple, merge_full, gain_two, bias_two, router = (
        lax.all_gather(attend_gain.astype(jnp.bfloat16), "fsdp", axis=0, tiled=True),
        lax.all_gather(attend_bias.astype(jnp.bfloat16), "fsdp", axis=0, tiled=True),
        lax.all_gather(triple_weight.astype(jnp.bfloat16), "fsdp", axis=0, tiled=True),
        lax.all_gather(merge_weight.astype(jnp.bfloat16), "fsdp", axis=0, tiled=True),
        lax.all_gather(mixture_gain.astype(jnp.bfloat16), "fsdp", axis=0, tiled=True),
        lax.all_gather(mixture_bias.astype(jnp.bfloat16), "fsdp", axis=0, tiled=True),
        lax.all_gather(router_weight.astype(jnp.bfloat16), "fsdp", axis=0, tiled=True),
    )
    up_full, down_full = (
        lax.all_gather(expert_up.astype(jnp.bfloat16), "fsdp", axis=1, tiled=True),
        lax.all_gather(expert_down.astype(jnp.bfloat16), "fsdp", axis=1, tiled=True),
    )
    inputs = tokens.astype(jnp.float32)
    normed_one, norm_back_one = jax.vjp(
        layer_norm, inputs, gain_one.astype(jnp.float32), bias_one.astype(jnp.float32)
    )
    normed_low = normed_one.astype(jnp.bfloat16)
    joined = jnp.dot(normed_low, triple, preferred_element_type=jnp.float32).astype(jnp.bfloat16)
    joined = joined.reshape(images, SEQ, 3, heads, HEAD_DIM)
    query_rows = joined[:, :, 0]
    key_rows = joined[:, :, 1]
    value_rows = joined[:, :, 2]
    scores = (
        jnp.einsum("bqhd,bkhd->bhqk", query_rows, key_rows, preferred_element_type=jnp.float32)
        * scale
    )
    top_score = jnp.max(scores, -1, keepdims=True)
    log_total = top_score + jnp.log(jnp.sum(jnp.exp(scores - top_score), -1, keepdims=True))
    weights_low = jnp.exp(scores - log_total).astype(jnp.bfloat16)
    mixed = jnp.einsum(
        "bhqk,bkhd->bqhd", weights_low, value_rows, preferred_element_type=jnp.float32
    )
    mixed = mixed.astype(jnp.bfloat16).reshape(local_rows, width)
    branch = jnp.dot(mixed, merge_full, preferred_element_type=jnp.float32)
    hidden_one = inputs + branch
    normed_two, norm_back_two = jax.vjp(
        layer_norm, hidden_one, gain_two.astype(jnp.float32), bias_two.astype(jnp.float32)
    )
    send_rows = normed_two.astype(jnp.bfloat16)
    logits = jnp.dot(send_rows, router, preferred_element_type=jnp.float32)
    probs = jax.nn.softmax(logits, -1)
    expert_ids = jnp.arange(experts, dtype=jnp.int32)
    picked = (routes[:, :, None] == expert_ids).astype(jnp.float32)
    gates = jnp.sum(picked * probs[:, None, :], 2)
    chosen = routes.reshape(-1)
    onehot = (chosen[:, None] == expert_ids).astype(jnp.int32)
    before = jnp.cumsum(onehot, 0) - onehot
    ranking = jnp.sum(before * onehot, 1)
    slots = chosen * capacity + ranking
    pair_ids = jnp.arange(chosen.shape[0], dtype=jnp.int32)
    filler = jnp.zeros((experts * capacity,), jnp.int32).at[slots].set(pair_ids + 1)
    token_source = jnp.where(filler > 0, (filler - 1) // TOP + 1, 0)
    padded = jnp.concatenate([jnp.zeros((1, width), jnp.bfloat16), send_rows], 0)
    outgoing = padded[token_source].reshape(owners, per_owner, capacity, width)
    arrived = lax.all_to_all(outgoing, "expert", split_axis=0, concat_axis=2, tiled=True).reshape(
        per_owner, spread_rows, width
    )
    hidden_list = []
    active_list = []
    result_list = []
    for member in range(per_owner):
        hidden_pre = jnp.dot(arrived[member], up_full[member], preferred_element_type=jnp.float32)
        activated = jax.nn.gelu(hidden_pre, approximate=False).astype(jnp.bfloat16)
        hidden_list.append(hidden_pre)
        active_list.append(activated)
        result_list.append(
            jnp.dot(activated, down_full[member], preferred_element_type=jnp.float32).astype(
                jnp.bfloat16
            )
        )
    expert_out = jnp.stack(result_list, 0).reshape(1, per_owner, spread_rows, width)
    returned = lax.all_to_all(expert_out, "expert", split_axis=2, concat_axis=0, tiled=True)
    pair_out = (
        returned.reshape(experts * capacity, width)[slots]
        .reshape(local_rows, TOP, width)
        .astype(jnp.float32)
    )
    mixture = jnp.sum(gates[:, :, None] * pair_out, 1)
    block_out = (hidden_one + mixture).astype(jnp.bfloat16)
    upstream = cotangent.astype(jnp.float32)
    gate_grad = jnp.sum(upstream[:, None, :] * pair_out, 2)
    pair_grad = (
        (gates[:, :, None] * upstream[:, None, :])
        .astype(jnp.bfloat16)
        .reshape(local_rows * TOP, width)
    )
    padded_grad = jnp.concatenate([jnp.zeros((1, width), jnp.bfloat16), pair_grad], 0)
    outgoing_grad = padded_grad[filler].reshape(owners, per_owner, capacity, width)
    arrived_grad = lax.all_to_all(
        outgoing_grad, "expert", split_axis=0, concat_axis=2, tiled=True
    ).reshape(per_owner, spread_rows, width)
    up_back, down_back = (
        lax.all_gather(expert_up.astype(jnp.bfloat16), "fsdp", axis=1, tiled=True),
        lax.all_gather(expert_down.astype(jnp.bfloat16), "fsdp", axis=1, tiled=True),
    )
    up_list = []
    down_list = []
    row_list = []
    for member in range(per_owner):
        act_grad = jnp.dot(
            arrived_grad[member], down_back[member].T, preferred_element_type=jnp.float32
        )
        down_list.append(
            jnp.dot(active_list[member].T, arrived_grad[member], preferred_element_type=jnp.float32)
        )
        gelu_back = jax.vjp(partial(jax.nn.gelu, approximate=False), hidden_list[member])[1]
        pre_grad = gelu_back(act_grad)[0].astype(jnp.bfloat16)
        up_list.append(jnp.dot(arrived[member].T, pre_grad, preferred_element_type=jnp.float32))
        row_list.append(
            jnp.dot(pre_grad, up_back[member].T, preferred_element_type=jnp.float32).astype(
                jnp.bfloat16
            )
        )
    row_grad = jnp.stack(row_list, 0).reshape(1, per_owner, spread_rows, width)
    back_rows = lax.all_to_all(row_grad, "expert", split_axis=2, concat_axis=0, tiled=True)
    send_grad = jnp.sum(
        back_rows.reshape(experts * capacity, width)[slots]
        .reshape(local_rows, TOP, width)
        .astype(jnp.float32),
        1,
    )
    up_total = jnp.stack(up_list, 0)
    down_total = jnp.stack(down_list, 0)
    expertup_grad, expertdown_grad = (
        lax.psum_scatter(
            up_total.astype(jnp.bfloat16), "fsdp", scatter_dimension=1, tiled=True
        ).astype(jnp.float32),
        lax.psum_scatter(
            down_total.astype(jnp.bfloat16), "fsdp", scatter_dimension=1, tiled=True
        ).astype(jnp.float32),
    )
    prob_grad = jnp.sum(picked * gate_grad[:, :, None], 1)
    logit_grad = (probs * (prob_grad - jnp.sum(probs * prob_grad, -1, keepdims=True))).astype(
        jnp.bfloat16
    )
    router_term = jnp.dot(send_rows.T, logit_grad, preferred_element_type=jnp.float32)
    normed_grad = send_grad + jnp.dot(logit_grad, router.T, preferred_element_type=jnp.float32)
    hidden_grad, gain_two_term, bias_two_term = norm_back_two(normed_grad)
    hidden_grad = hidden_grad + upstream
    branch_grad = hidden_grad.astype(jnp.bfloat16)
    merge_term = jnp.dot(mixed.T, branch_grad, preferred_element_type=jnp.float32)
    mixed_grad = jnp.dot(branch_grad, merge_full.T, preferred_element_type=jnp.float32).astype(
        jnp.bfloat16
    )
    mixed_grad = mixed_grad.reshape(images, SEQ, heads, HEAD_DIM)
    scores_again = (
        jnp.einsum("bqhd,bkhd->bhqk", query_rows, key_rows, preferred_element_type=jnp.float32)
        * scale
    )
    probs_again = jnp.exp(scores_again - log_total)
    weight_grad = jnp.einsum(
        "bqhd,bkhd->bhqk", mixed_grad, value_rows, preferred_element_type=jnp.float32
    )
    score_grad = (
        probs_again * (weight_grad - jnp.sum(probs_again * weight_grad, -1, keepdims=True))
    ).astype(jnp.bfloat16)
    query_grad = (
        jnp.einsum("bhqk,bkhd->bqhd", score_grad, key_rows, preferred_element_type=jnp.float32)
        * scale
    )
    key_grad = (
        jnp.einsum("bhqk,bqhd->bkhd", score_grad, query_rows, preferred_element_type=jnp.float32)
        * scale
    )
    value_grad = jnp.einsum(
        "bhqk,bqhd->bkhd",
        probs_again.astype(jnp.bfloat16),
        mixed_grad,
        preferred_element_type=jnp.float32,
    )
    joined_grad = (
        jnp.stack([query_grad, key_grad, value_grad], 2)
        .astype(jnp.bfloat16)
        .reshape(local_rows, 3 * width)
    )
    triple_term = jnp.dot(normed_low.T, joined_grad, preferred_element_type=jnp.float32)
    normed_one_grad = jnp.dot(joined_grad, triple.T, preferred_element_type=jnp.float32)
    input_grad, gain_one_term, bias_one_term = norm_back_one(normed_one_grad)
    tokens_grad = input_grad + hidden_grad
    shares = (
        lax.psum_scatter(
            gain_one_term.astype(jnp.bfloat16), "fsdp", scatter_dimension=0, tiled=True
        ).astype(jnp.float32),
        lax.psum_scatter(
            bias_one_term.astype(jnp.bfloat16), "fsdp", scatter_dimension=0, tiled=True
        ).astype(jnp.float32),
        lax.psum_scatter(
            triple_term.astype(jnp.bfloat16), "fsdp", scatter_dimension=0, tiled=True
        ).astype(jnp.float32),
        lax.psum_scatter(
            merge_term.astype(jnp.bfloat16), "fsdp", scatter_dimension=0, tiled=True
        ).astype(jnp.float32),
        lax.psum_scatter(
            gain_two_term.astype(jnp.bfloat16), "fsdp", scatter_dimension=0, tiled=True
        ).astype(jnp.float32),
        lax.psum_scatter(
            bias_two_term.astype(jnp.bfloat16), "fsdp", scatter_dimension=0, tiled=True
        ).astype(jnp.float32),
        lax.psum_scatter(
            router_term.astype(jnp.bfloat16), "fsdp", scatter_dimension=0, tiled=True
        ).astype(jnp.float32),
    )
    totals = (
        lax.psum(shares[0].astype(jnp.bfloat16), "expert").astype(jnp.float32),
        lax.psum(shares[1].astype(jnp.bfloat16), "expert").astype(jnp.float32),
        lax.psum(shares[2].astype(jnp.bfloat16), "expert").astype(jnp.float32),
        lax.psum(shares[3].astype(jnp.bfloat16), "expert").astype(jnp.float32),
        lax.psum(shares[4].astype(jnp.bfloat16), "expert").astype(jnp.float32),
        lax.psum(shares[5].astype(jnp.bfloat16), "expert").astype(jnp.float32),
        lax.psum(shares[6].astype(jnp.bfloat16), "expert").astype(jnp.float32),
    )
    return (
        block_out,
        tokens_grad,
        totals[0],
        totals[1],
        totals[2],
        totals[3],
        totals[4],
        totals[5],
        totals[6],
        expertup_grad,
        expertdown_grad,
    )


def solution(mesh):
    return jax.shard_map(
        local,
        mesh=mesh,
        in_specs=(
            P(("expert", "fsdp"), None),
            P(("expert", "fsdp"), None),
            P(("expert", "fsdp"), None),
            P("fsdp"),
            P("fsdp"),
            P("fsdp", None),
            P("fsdp", None),
            P("fsdp"),
            P("fsdp"),
            P("fsdp", None),
            P("expert", "fsdp", None),
            P("expert", "fsdp", None),
        ),
        out_specs=(
            P(("expert", "fsdp"), None),
            P(("expert", "fsdp"), None),
            P("fsdp"),
            P("fsdp"),
            P("fsdp", None),
            P("fsdp", None),
            P("fsdp"),
            P("fsdp"),
            P("fsdp", None),
            P("expert", "fsdp", None),
            P("expert", "fsdp", None),
        ),
        check_vma=False,
    )
```

profile of v0, /device:TPU:0, one launch (start us, length us, event | category | flops | bytes accessed | tf_op | source)
XLA Modules:
  0.0 934.5 jit_solution(5010760115874107428)
XLA Ops:
  15.2 15.2 %all-reduce.12 = (bf16[512]{0:T(512)(128)(2,1)S(1)}, bf16[512]{0:T(512)(128)(2,1)S(1)}, bf16[512]{0:T(512)(128)(2,1)S(1)}, bf16[512]{0:T(512)(128)(2,1)S(1)}) all-reduce(bf16[512]{0:T(512)(128)(2,1)S(1)} %dynamic-update-slice.1, bf16[512]{0:T(512)(128)(2,1)S(1)} %dynamic-update-slice, ...), channel_id=1, replica_groups=mesh['expert'=4,'fsdp'=8] {'fsdp'}, use_global_device_ids=true, to_apply=%add.4 | all-reduce | flops 2048 | bytes 8192
  62.7 10.8 %all_gather.32 = bf16[512,512]{1,0:T(8,128)(2,1)} all-gather(bf16[64,512]{1,0:T(8,128)(2,1)S(1)} %convert_element_type.210), channel_id=1, replica_groups=mesh['expert'=4,'fsdp'=8] {'fsdp'}, dimensions={0}, use_global_device_ids=true | all-gather | bytes 589824 | tf_op jit(solution)/shard_map/all_gather | solution.py:50
  108.7 10.3 %gather_fusion.2 = bf16[3152,512]{1,0:T(8,128)(2,1)} fusion(bf16[1577,512]{1,0:T(8,128)(2,1)S(1)} %concatenate.7, s32[4096]{0:T(1024)S(1)} %get-tuple-element.65), kind=kCustom, calls=%fused_computation.2 | custom fusion | bytes 6467904 | tf_op jit(solution)/shard_map/gather | solution.py:134
  132.7 10.2 %gather_fusion = bf16[3152,512]{1,0:T(8,128)(2,1)} fusion(bf16[789,512]{1,0:T(8,128)(2,1)S(1)} %concatenate.6, s32[4096]{0:T(1024)S(1)} %get-tuple-element.66), kind=kCustom, calls=%fused_computation | custom fusion | bytes 6467904 | tf_op jit(solution)/shard_map/gather | solution.py:100
  150.5 54.2 %all-to-all-done.2 = bf16[4,2,394,512]{3,1,2,0:T(2,128)(2,1)} async-done(((bf16[4,2,394,512]{3,1,2,0:T(2,128)(2,1)}), bf16[4,2,394,512]{3,1,2,0:T(2,128)(2,1)}, u32[]{:S(2)}, u32[]{:S(2)}) %all-to-all-start.2) | async-done | bytes 3227680 | tf_op jit(solution)/shard_map/all_to_all | solution.py:135
  210.6 37.3 %slice_reduce_fusion.1 = (bf16[4,394,512]{2,1,0:T(8,128)(2,1)}, bf16[4,394,512]{2,1,0:T(8,128)(2,1)}) fusion(bf16[1,2,4,394,512]{4,1,3,2,0:T(2,128)(2,1)} %bitcast.21), kind=kLoop, calls=%fused_computation.51 | loop fusion | bytes 6455296 | tf_op jit(solution)/shard_map/slice | solution.py:147
  254.0 26.5 %all-to-all-done = bf16[4,2,394,512]{3,1,2,0:T(2,128)(2,1)S(1)} async-done(((bf16[4,2,394,512]{3,1,2,0:T(2,128)(2,1)}), bf16[4,2,394,512]{3,1,2,0:T(2,128)(2,1)S(1)}, u32[]{:S(2)}, u32[]{:S(2)}) %all-to-all-start) | async-done | bytes 3227680 | tf_op jit(solution)/shard_map/all_to_all | solution.py:101
  280.6 36.0 %slice_reduce_fusion.3 = (bf16[4,394,512]{2,1,0:T(8,128)(2,1)}, bf16[4,394,512]{2,1,0:T(8,128)(2,1)}) fusion(bf16[1,2,4,394,512]{4,1,3,2,0:T(2,128)(2,1)S(1)} %bitcast.150), kind=kLoop, calls=%fused_computation.53 | loop fusion | bytes 6455296 | tf_op jit(solution)/shard_map/slice | solution.py:108
  320.2 32.9 %multiply_convert_fusion = (bf16[1576,2048]{1,0:T(8,128)(2,1)}, f32[1576,2048]{1,0:T(8,128)}, f32[1576,2048]{1,0:T(8,128)}) fusion(bf16[1576,512]{1,0:T(8,128)(2,1)} %squeeze.47, bf16[2,512,2048]{2,1,0:T(8,128)(2,1)} %all-gather.7.cloned.1.call-done), kind=kOutput, calls=%fused_computation.11 | convolution fusion | flops 3514908672 | bytes 35987456 | tf_op jit(solution)/shard_map/dot_general | solution.py:108
  353.2 15.5 %add_convert_fusion = bf16[1576,2048]{1,0:T(8,128)(2,1)} fusion(f32[1576,2048]{1,0:T(8,128)} %get-tuple-element.44, f32[1576,2048]{1,0:T(8,128)} %get-tuple-element.57, bf16[1576,512]{1,0:T(8,128)(2,1)S(1)} %copy-done.26, bf16[2,2048,512]{2,1,0:T(8,128)(2,1)} %all-gather.9.cloned.1.call-done), kind=kOutput, calls=%fused_computation.9 | convolution fusion | flops 3350298624 | bytes 35987456 | tf_op jit(solution)/shard_map/dot_general | solution.py:146
  375.1 32.5 %multiply_convert_fusion.1 = (bf16[1576,2048]{1,0:T(8,128)(2,1)}, f32[1576,2048]{1,0:T(8,128)}, f32[1576,2048]{1,0:T(8,128)}) fusion(bf16[1576,512]{1,0:T(8,128)(2,1)S(1)} %squeeze.44, bf16[2,512,2048]{2,1,0:T(8,128)(2,1)S(1)} %copy-done.62), kind=kOutput, calls=%fused_computation.24 | convolution fusion | flops 3514908672 | bytes 35987456 | tf_op jit(solution)/shard_map/dot_general | solution.py:108
  407.6 15.6 %add_convert_fusion.1 = bf16[1576,2048]{1,0:T(8,128)(2,1)} fusion(f32[1576,2048]{1,0:T(8,128)} %get-tuple-element.42, f32[1576,2048]{1,0:T(8,128)} %get-tuple-element.60, bf16[1576,512]{1,0:T(8,128)(2,1)S(1)} %copy-done.24, bf16[2,2048,512]{2,1,0:T(8,128)(2,1)} %all-gather.9.cloned.1.call-done), kind=kOutput, calls=%fused_computation.10 | convolution fusion | flops 3350298624 | bytes 35987456 | tf_op jit(solution)/shard_map/dot_general | solution.py:146
  429.9 11.9 %copy.128 = bf16[1,2,1576,512]{3,1,0,2:T(2,128)(2,1)} copy(bf16[1,2,1576,512]{3,2,1,0:T(8,128)(2,1)S(1)} %maximum_bitcast_fusion.1) | data formatting | bytes 6455296 | tf_op jit(solution)/shard_map/reshape | solution.py:160
  459.5 11.9 %copy.123 = bf16[1,2,1576,512]{3,1,0,2:T(2,128)(2,1)} copy(bf16[1,2,1576,512]{3,2,1,0:T(8,128)(2,1)S(1)} %maximum_bitcast_fusion) | data formatting | bytes 6455296 | tf_op jit(solution)/shard_map/reshape | solution.py:117
  471.4 46.3 %all-to-all-done.3 = bf16[1,2,1576,512]{3,1,0,2:T(2,128)(2,1)S(1)} async-done(((bf16[1,2,1576,512]{3,1,0,2:T(2,128)(2,1)}), bf16[1,2,1576,512]{3,1,0,2:T(2,128)(2,1)S(1)}, u32[]{:S(2)}, u32[]{:S(2)}) %all-to-all-start.3) | async-done | bytes 3227680 | tf_op jit(solution)/shard_map/all_to_all | solution.py:161
  530.0 64.4 %all-to-all-done.1 = bf16[1,2,1576,512]{3,1,0,2:T(2,128)(2,1)} async-done(((bf16[1,2,1576,512]{3,1,0,2:T(2,128)(2,1)}), bf16[1,2,1576,512]{3,1,0,2:T(2,128)(2,1)}, u32[]{:S(2)}, u32[]{:S(2)}) %all-to-all-start.1) | async-done | bytes 3227680 | tf_op jit(solution)/shard_map/all_to_all | solution.py:118
  620.5 9.9 %multiply_reduce_fusion.2 = (f32[788,2]{1,0:T(8,128)}, f32[788,512]{1,0:T(8,128)}) fusion(f32[788,2,512]{2,1,0:T(2,128)S(1)} %reshape.221, f32[788,512]{1,0:T(8,128)} %convert_element_type.227, f32[788,2]{1,0:T(8,128)} %copy.118), kind=kLoop, calls=%fused_computation.56 | loop fusion | flops 2822616 | bytes 6467904 | tf_op jit(solution)/shard_map/reduce_sum | solution.py:127
  692.4 8.9 fusion.18
  740.1 12.1 %all-reduce.11 = (bf16[512]{0:T(512)(128)(2,1)S(1)}, bf16[512]{0:T(512)(128)(2,1)S(1)}, bf16[512]{0:T(512)(128)(2,1)S(1)}, bf16[512]{0:T(512)(128)(2,1)S(1)}) all-reduce(bf16[512]{0:T(512)(128)(2,1)S(1)} %get-tuple-element.19, bf16[512]{0:T(512)(128)(2,1)S(1)} %get-tuple-element.22, ...), channel_id=2, replica_groups=mesh['expert'=4,'fsdp'=8] {'fsdp'}, use_global_device_ids=true, to_apply=%region_24.25.clone | all-reduce | flops 2048 | bytes 8192
  755.7 21.6 %reduce-scatter.16.cloned.1.call-done = bf16[64,8]{1,0:T(8,128)(2,1)} async-done(((bf16[512,8]{1,0:T(8,128)(2,1)}), bf16[64,8]{1,0:T(8,128)(2,1)}) %reduce-scatter.16.cloned.1.call-update) | async-done | bytes 1040
  778.1 11.7 %all-reduce.13 = (bf16[64]{0:T(256)(128)(2,1)S(1)}, bf16[64]{0:T(256)(128)(2,1)S(1)}, bf16[64]{0:T(256)(128)(2,1)S(1)}, bf16[64]{0:T(256)(128)(2,1)S(1)}, bf16[64,8]{0,1:T(8,128)(2,1)S(1)}) all-reduce(bf16[64]{0:T(256)(128)(2,1)S(1)} %dynamic-slice.5, ...), channel_id=1, replica_groups=mesh['expert'=4,'fsdp'=8] {'expert'}, use_global_device_ids=true, to_apply=%region_25.26 | all-reduce | flops 768 | bytes 3072 | tf_op jit(solution)/shard_map/psum | solution.py:250
  792.5 39.4 %reduce-scatter.12.cloned.1.call-done = bf16[2,64,2048]{2,1,0:T(8,128)(2,1)} async-done(((bf16[2,512,2048]{2,1,0:T(8,128)(2,1)}), bf16[2,64,2048]{2,1,0:T(8,128)(2,1)}) %reduce-scatter.12.cloned.1.call-update) | async-done | bytes 524304 | tf_op jit(solution)/shard_map/reduce_scatter | solution.py:171
  834.0 52.4 %reduce-scatter.14.cloned.1.call-done = bf16[2,256,512]{2,1,0:T(8,128)(2,1)} async-done(((bf16[2,2048,512]{2,1,0:T(8,128)(2,1)}), bf16[2,256,512]{2,1,0:T(8,128)(2,1)}) %reduce-scatter.14.cloned.1.call-update) | async-done | bytes 524304 | tf_op jit(solution)/shard_map/reduce_scatter | solution.py:174
  888.5 35.9 %all-reduce.17.cloned.1.call-done = (bf16[64,1536]{1,0:T(8,128)(2,1)}, bf16[64,512]{1,0:T(8,128)(2,1)}) async-done(((bf16[64,1536]{1,0:T(8,128)(2,1)}, bf16[64,512]{1,0:T(8,128)(2,1)}), (bf16[64,1536]{1,0:T(8,128)(2,1)}, bf16[64,512]{1,0:T(8,128)(2,1)})) %all-reduce.17.cloned.1.call-update) | async-done | bytes 262160 | tf_op jit(solution)/shard_map/psum | solution.py:252
  (305 shorter events, 294.4 us)
Async XLA Ops:
  7.2 67.1 %all-gather.5.cloned.1.call-start = ((), (), s32[]{:S(2)}) async-start(), calls=%async_computation.9 | async-start | bytes 1769472 | tf_op jit(solution)/shard_map/all_gather | solution.py:49
  30.4 43.9 %copy-start.60 = (f32[512]{0:T(512)}, f32[512]{0:T(512)S(1)}, u32[]{:S(2)}) copy-start(f32[512]{0:T(512)S(1)} %convert_element_type.203) | copy-start | bytes 6148
  30.4 43.9 %copy-start.58 = (f32[512]{0:T(512)}, f32[512]{0:T(512)S(1)}, u32[]{:S(2)}) copy-start(f32[512]{0:T(512)S(1)} %convert_element_type.201) | copy-start | bytes 6148
  30.4 72.3 %copy-start.54 = (f32[512]{0:T(512)}, f32[512]{0:T(512)S(1)}, u32[]{:S(2)}) copy-start(f32[512]{0:T(512)S(1)} %convert_element_type.212) | copy-start | bytes 6148
  38.6 65.2 %copy-start.40 = (bf16[512,8]{0,1:T(8,128)(2,1)}, bf16[512,8]{0,1:T(8,128)(2,1)S(1)}, u32[]{:S(2)}) copy-start(bf16[512,8]{0,1:T(8,128)(2,1)S(1)} %reshape.278) | copy-start | bytes 24580
  48.4 25.2 %copy-start.3 = (bf16[788,512]{1,0:T(8,128)(2,1)S(1)}, bf16[788,512]{1,0:T(8,128)(2,1)}, u32[]{:S(2)}) copy-start(bf16[788,512]{1,0:T(8,128)(2,1)} %param.12) | copy-start | bytes 2420740
  126.7 78.1 %all-to-all-start.2 = ((bf16[4,2,394,512]{3,1,2,0:T(2,128)(2,1)}), bf16[4,2,394,512]{3,1,2,0:T(2,128)(2,1)}, u32[]{:S(2)}, u32[]{:S(2)}) async-start(bf16[4,2,394,512]{3,1,2,0:T(2,128)(2,1)} %copy.127), calls=%async_computation.2 | async-start | bytes 6455296 | tf_op jit(solution)/shard_map/all_to_all | solution.py:135
  131.6 188.6 %all-gather.7.cloned.1.call-start = ((), (), s32[]{:S(2)}) async-start(), calls=%async_computation.10 | async-start | bytes 4718592 | tf_op jit(solution)/shard_map/all_gather | solution.py:56
  204.7 75.8 %all-to-all-start = ((bf16[4,2,394,512]{3,1,2,0:T(2,128)(2,1)}), bf16[4,2,394,512]{3,1,2,0:T(2,128)(2,1)S(1)}, u32[]{:S(2)}, u32[]{:S(2)}) async-start(bf16[4,2,394,512]{3,1,2,0:T(2,128)(2,1)} %copy.122), calls=%async_computation | async-start | bytes 6455296 | tf_op jit(solution)/shard_map/all_to_all | solution.py:101
  208.5 144.7 %all-gather.9.cloned.1.call-start = ((), (), s32[]{:S(2)}) async-start(), calls=%async_computation.11 | async-start | bytes 4718592 | tf_op jit(solution)/shard_map/all_gather | solution.py:57
  318.5 56.5 %copy-start.27 = (bf16[1576,512]{1,0:T(8,128)(2,1)}, bf16[1576,512]{1,0:T(8,128)(2,1)S(1)}, u32[]{:S(2)}) copy-start(bf16[1576,512]{1,0:T(8,128)(2,1)S(1)} %squeeze.44) | copy-start | bytes 4841476
  320.2 32.9 %copy-start.26 = (bf16[1576,512]{1,0:T(8,128)(2,1)S(1)}, bf16[1576,512]{1,0:T(8,128)(2,1)}, u32[]{:S(2)}) copy-start(bf16[1576,512]{1,0:T(8,128)(2,1)} %squeeze.51) | copy-start | bytes 4841476
  353.1 15.5 %copy-start.62 = (bf16[2,512,2048]{2,1,0:T(8,128)(2,1)S(1)}, bf16[2,512,2048]{2,1,0:T(8,128)(2,1)}, u32[]{:S(2)}) copy-start(bf16[2,512,2048]{2,1,0:T(8,128)(2,1)} %all-gather.7.cloned.1.call-done) | copy-start | bytes 12582916
  375.1 32.5 %copy-start.24 = (bf16[1576,512]{1,0:T(8,128)(2,1)S(1)}, bf16[1576,512]{1,0:T(8,128)(2,1)}, u32[]{:S(2)}) copy-start(bf16[1576,512]{1,0:T(8,128)(2,1)} %squeeze.50) | copy-start | bytes 4841476
  441.8 75.9 %all-to-all-start.3 = ((bf16[1,2,1576,512]{3,1,0,2:T(2,128)(2,1)}), bf16[1,2,1576,512]{3,1,0,2:T(2,128)(2,1)S(1)}, u32[]{:S(2)}, u32[]{:S(2)}) async-start(bf16[1,2,1576,512]{3,1,0,2:T(2,128)(2,1)} %copy.128), calls=%async_computation.3 | async-start | bytes 6455296 | tf_op jit(solution)/shard_map/all_to_all | solution.py:161
  471.4 53.5 %copy-start.57 = (s32[1576]{0:T(1024)S(1)}, s32[1576]{0:T(1024)}, u32[]{:S(2)}) copy-start(s32[1576]{0:T(1024)} %copy-done.56) | copy-start | bytes 18916
  517.7 76.7 %all-to-all-start.1 = ((bf16[1,2,1576,512]{3,1,0,2:T(2,128)(2,1)}), bf16[1,2,1576,512]{3,1,0,2:T(2,128)(2,1)}, u32[]{:S(2)}, u32[]{:S(2)}) async-start(bf16[1,2,1576,512]{3,1,0,2:T(2,128)(2,1)} %copy.123), calls=%async_computation.1 | async-start | bytes 6455296 | tf_op jit(solution)/shard_map/all_to_all | solution.py:118
  522.3 230.2 %reduce-scatter.10.cloned.1.call-start = ((), (), s32[]{:S(2)}) async-start(), calls=%async_computation.13 | async-start | bytes 589824 | tf_op jit(solution)/shard_map/reduce_scatter | solution.py:236
  631.6 11.2 %copy-start.2 = (f32[788,512]{1,0:T(8,128)S(1)}, f32[788,512]{1,0:T(8,128)}, u32[]{:S(2)}) copy-start(f32[788,512]{1,0:T(8,128)} %copy-done.1) | copy-start | bytes 4841476
  666.5 86.0 %reduce-scatter.8.cloned.1.call-start = ((), (), s32[]{:S(2)}) async-start(), calls=%async_computation.12 | async-start | bytes 1769472 | tf_op jit(solution)/shard_map/reduce_scatter | solution.py:233
  692.4 85.0 %reduce-scatter.16.cloned.1.call-start = ((), (), s32[]{:S(2)}) async-start(), calls=%async_computation.16 | async-start | bytes 147456
  710.5 121.3 %reduce-scatter.12.cloned.1.call-start = ((), (), s32[]{:S(2)}) async-start(), calls=%async_computation.14 | async-start | bytes 4718592 | tf_op jit(solution)/shard_map/reduce_scatter | solution.py:171
  715.3 171.0 %reduce-scatter.14.cloned.1.call-start = ((), (), s32[]{:S(2)}) async-start(), calls=%async_computation.15 | async-start | bytes 4718592 | tf_op jit(solution)/shard_map/reduce_scatter | solution.py:174
  732.9 191.5 %all-reduce.17.cloned.1.call-start = ((), (), s32[]{:S(2)}) async-start(), calls=%async_computation.17 | async-start | bytes 524288 | tf_op jit(solution)/shard_map/psum | solution.py:252
  (53 other events, 274.7 us)
Sparse Core Ops, SparseCore 0:
  10.4 28.3 all-gather.4
  134.9 37.0 all-gather.6
  211.2 37.0 all-gather.8
  666.6 32.2 reduce-scatter.9
  702.0 38.3 reduce-scatter.7
  743.8 33.5 reduce-scatter.15
  780.7 51.1 reduce-scatter.11
  835.2 51.0 reduce-scatter.13
  888.7 35.6 all-reduce.16
where the time goes:
time: 945 us; the launch traced here: 935 us
  waiting for transfers between devices  341 us (36%)
  local copies, waits for them, and re-layouts  248 us (26%)
  matrix products  189 us (20%)
  other arithmetic  64 us (7%)
  blocking collectives  57.9 us (6%)
  starting transfers between devices  18 us (2%)
  between operations  16.7 us (2%)
    dot_general x2, matrix products, local(): jnp.dot(arrived[member], up_full[member], preferred_element_type=jnp.floa...  65.4 us
    all_to_all x1, waiting for transfers between devices, local(): lax.all_to_all(expert_out, 'expert', split_axis=2, concat_axis=0, tiled=T...  64.4 us
    all_to_all x1, waiting for transfers between devices, local(): lax.all_to_all(outgoing_grad, 'expert', split_axis=0, concat_axis=2, tile...  54.2 us
    reduce_scatter x1, waiting for transfers between devices, local(): lax.psum_scatter(down_total.astype(jnp.bfloat16), 'fsdp', scatter_dimensi...  52.4 us
    all_to_all x1, waiting for transfers between devices, local(): lax.all_to_all(row_grad, 'expert', split_axis=2, concat_axis=0, tiled=True)  46.3 us
    reduce_scatter x1, waiting for transfers between devices, local(): lax.psum_scatter(up_total.astype(jnp.bfloat16), 'fsdp', scatter_dimension...  39.4 us
    slice x1, local copies, waits for them, and re-layouts, local(): arrived_grad[member]  37.3 us
    slice x1, local copies, waits for them, and re-layouts, local(): arrived[member]  36 us
  transfers between devices with their start and end apart: 13, of which 8 were waited for; matrix products, arithmetic and copies ran while one was open for 30% of the time, Pallas kernels for 0%

commit v1 on v0

v1 whole, which is shorter than its diff:
```python
from functools import partial

import jax
import jax.numpy as jnp
from jax import lax
from jax.experimental import pallas as pl
from jax.experimental.pallas import tpu as pltpu
from jax.sharding import PartitionSpec as P

HEAD_DIM = 64
TOP = 2
SEQ = 197
EPSILON = 1e-06
LANES = 128
TILE = 256
STRIP = 64
SUB = 128
FAR = -1e30
BF = jnp.bfloat16
F32 = jnp.float32
VMEM_LIMIT = 60 * 1024 * 1024

ERFC = (
    0.2820843458175659,
    0.282412052154541,
    0.24283546209335327,
    0.2037508189678192,
    -0.029143672436475754,
    0.2817249596118927,
    -0.49039793014526367,
    0.2861193120479584,
    -0.05938538536429405,
)


def ceil_to(value, unit):
    return -(-value // unit) * unit


def dot_nn(a, b):
    return lax.dot_general(a, b, (((1,), (0,)), ((), ())), preferred_element_type=F32)


def dot_nt(a, b):
    return lax.dot_general(a, b, (((1,), (1,)), ((), ())), preferred_element_type=F32)


def dot_tn(a, b):
    return lax.dot_general(a, b, (((0,), (0,)), ((), ())), preferred_element_type=F32)


def gelu_both(hidden):
    bell = jnp.exp(hidden * hidden * -0.5)
    t = 1.0 / (1.0 + jnp.abs(hidden) * (0.5 * 0.5**0.5))
    series = jnp.full_like(t, ERFC[-1])
    for factor in ERFC[-2::-1]:
        series = series * t + factor
    tail = (0.5 * t) * series * bell
    share = jnp.where(hidden >= 0, 1.0 - tail, tail)
    return hidden * share, share + hidden * bell * 0.3989422804014327


def normalize(values):
    center = values - jnp.mean(values, -1, keepdims=True)
    spread = jnp.mean(center * center, -1, keepdims=True)
    inverse = lax.rsqrt(spread + EPSILON)
    return center * inverse, inverse


def window(image):
    start = image * SEQ // 16 * 16
    offset = image * SEQ - start
    return pl.multiple_of(start, 16), offset


WINDOW = ceil_to(SEQ + 15, 32)


def attend_kernel(
    experts, tokens, routes, packed, qkv, mixed, hidden, normed, probs, gates, first, small
):
    rows, width = tokens.shape
    images = rows // SEQ
    half = rows // 2
    small[...] = packed[:, 4 * width :].astype(F32).T
    gain_one, bias_one = small[experts : experts + 1, :], small[experts + 1 : experts + 2, :]
    gain_two, bias_two = small[experts + 2 : experts + 3, :], small[experts + 3 : experts + 4, :]

    def norm_one(j, carry):
        part = pl.ds(pl.multiple_of(j * STRIP, STRIP), STRIP)
        unit, _ = normalize(tokens[part, :].astype(F32))
        first[part, :] = (unit * gain_one + bias_one).astype(BF)
        mixed[part, :] = jnp.zeros((STRIP, width), BF)
        return carry

    lax.fori_loop(0, rows // STRIP, norm_one, 0)
    for third in range(3):
        columns = slice(third * width, (third + 1) * width)

        def project(j, carry):
            part = pl.ds(pl.multiple_of(j * half, 16), half)
            qkv[part, columns] = dot_nn(first[part, :], packed[:, columns]).astype(BF)
            return carry

        lax.fori_loop(0, 2, project, 0)

    lane = lax.broadcasted_iota(jnp.int32, (1, LANES), 1)
    low = lane < HEAD_DIM
    scale = 1.0 / HEAD_DIM**0.5

    def attend(image, carry):
        start, offset = window(image)
        part = pl.ds(start, WINDOW)
        place = lax.broadcasted_iota(jnp.int32, (WINDOW, 1), 0) - offset
        mine = (place >= 0) & (place < SEQ)
        across = lax.broadcasted_iota(jnp.int32, (1, WINDOW), 1) - offset
        keys_mine = (across >= 0) & (across < SEQ)
        for pair in range(width // LANES):
            at = pair * LANES
            query = qkv[part, at : at + LANES]
            key = qkv[part, width + at : width + at + LANES]
            value = qkv[part, 2 * width + at : 2 * width + at + LANES]
            both = []
            for side in (low, ~low):
                chosen = jnp.where(side, query, jnp.zeros_like(query))
                scores = jnp.where(keys_mine, dot_nt(chosen, key) * scale, FAR)
                top = jnp.max(scores, -1, keepdims=True)
                raised = jnp.exp(scores - top)
                weights = raised * (1.0 / jnp.sum(raised, -1, keepdims=True))
                both.append(dot_nn(weights.astype(BF), value))
            out = jnp.where(low, both[0], both[1]).astype(BF)
            mixed[part, at : at + LANES] = jnp.where(mine, out, mixed[part, at : at + LANES])
        return carry

    lax.fori_loop(0, images, attend, 0)

    def merge(j, carry):
        part = pl.ds(pl.multiple_of(j * half, 16), half)
        hidden[part, :] = dot_nn(mixed[part, :], packed[:, 3 * width : 4 * width])
        return carry

    lax.fori_loop(0, 2, merge, 0)

    def norm_two(j, carry):
        part = pl.ds(pl.multiple_of(j * STRIP, STRIP), STRIP)
        total = tokens[part, :].astype(F32) + hidden[part, :]
        hidden[part, :] = total
        unit, _ = normalize(total)
        normed[part, :] = (unit * gain_two + bias_two).astype(BF)
        return carry

    lax.fori_loop(0, rows // STRIP, norm_two, 0)
    router = small[0 : max(experts, 16), :].astype(BF)
    logits = dot_nt(router, normed[...])[:experts]
    raised = jnp.exp(logits - jnp.max(logits, 0, keepdims=True))
    share = raised / jnp.sum(raised, 0, keepdims=True)
    probs[...] = share
    ids = lax.broadcasted_iota(jnp.int32, (experts, rows), 0)
    picked = (routes[0:1, :] == ids) | (routes[1:2, :] == ids)
    gates[...] = jnp.where(picked, share, 0.0)


def attend(tokens, routes, packed, experts):
    rows, width = tokens.shape
    shape = jax.ShapeDtypeStruct
    return pl.pallas_call(
        partial(attend_kernel, experts),
        out_shape=(
            shape((rows, 3 * width), BF),
            shape((rows, width), BF),
            shape((rows, width), F32),
            shape((rows, width), BF),
            shape((experts, rows), F32),
            shape((experts, rows), F32),
        ),
        in_specs=[pl.BlockSpec(memory_space=pltpu.VMEM)] * 3,
        out_specs=[pl.BlockSpec(memory_space=pltpu.VMEM)] * 6,
        scratch_shapes=[pltpu.VMEM((rows, width), BF), pltpu.VMEM((LANES, width), F32)],
        compiler_params=pltpu.CompilerParams(vmem_limit_bytes=VMEM_LIMIT),
        name="attend",
    )(tokens, routes, packed)


def expert_kernel(
    tiles,
    parts,
    room,
    meta,
    info,
    up,
    down,
    rows,
    upstream,
    mixture,
    row_grad,
    gate_grad,
    up_grad,
    down_grad,
    packed_rows,
    packed_grads,
    out_sum,
    back_sum,
    out_low,
    back_low,
    up_sum,
    down_sum,
):
    width = rows.shape[1]
    step = pl.program_id(0)
    member = jnp.minimum(step // parts, 1)
    part = step - member * parts
    span = up_sum.shape[1]
    stride = meta.shape[0] // 2

    @pl.when(step == 0)
    def _():
        def clear(j, carry):
            at = pl.ds(pl.multiple_of(j * TILE, TILE), TILE)
            for which in range(2):
                out_low[which, at, :] = jnp.zeros((TILE, width), BF)
                back_low[which, at, :] = jnp.zeros((TILE, width), BF)
            return carry

        lax.fori_loop(0, room // TILE, clear, 0)

    @pl.when((step < 2 * parts) & (part == 0))
    def _():
        def clear(j, carry):
            at = pl.ds(pl.multiple_of(j * TILE, TILE), TILE)
            packed_rows[at, :] = jnp.zeros((TILE, width), BF)
            packed_grads[at, :] = jnp.zeros((TILE, width), BF)
            return carry

        lax.fori_loop(0, room // TILE, clear, 0)

        def gather(tile, carry):
            begin = meta[member * stride + tile]
            end = meta[member * stride + tile + 1]
            base = begin // 16 * 16
            count = jnp.where(end > begin, (end - base + SUB - 1) // SUB, 0)
            at = pl.ds(pl.multiple_of(tile * TILE, TILE), TILE)
            known = info[tile]
            order = jnp.where(member == 0, known[0:1, :], known[1:2, :])
            columns = known.T
            gate = jnp.where(member == 0, columns[:, 2:3], columns[:, 3:4])
            source = rows[at, :]
            gated = (upstream[at, :].astype(F32) * gate).astype(BF)

            def place(j, inner):
                origin = pl.multiple_of(base + j * SUB, 16)
                wanted = lax.broadcasted_iota(jnp.int32, (SUB, 1), 0) + origin
                chosen = jnp.where(order == wanted.astype(F32), 1.0, 0.0).astype(BF)
                to = pl.ds(origin, SUB)
                packed_rows[to, :] += dot_nn(chosen, source).astype(BF)
                packed_grads[to, :] += dot_nn(chosen, gated).astype(BF)
                return inner

            return lax.fori_loop(0, count, place, carry)

        lax.fori_loop(0, tiles, gather, 0)

    @pl.when(step < 2 * parts)
    def _():
        up_part = up[...].reshape(width, span)
        down_part = down[...].reshape(span, width)
        chunks = (meta[member * stride + tiles] + TILE - 1) // TILE
        up_sum[...] = jnp.zeros(up_sum.shape, F32)
        down_sum[...] = jnp.zeros(down_sum.shape, F32)

        def chunk(j, carry):
            at = pl.ds(pl.multiple_of(j * TILE, TILE), TILE)
            source = packed_rows[at, :]
            grads = packed_grads[at, :]
            active, slope = gelu_both(dot_nn(source, up_part))
            active = active.astype(BF)
            out = dot_nn(active, down_part)
            pre_grad = (dot_nt(grads, down_part) * slope).astype(BF)
            back = dot_nt(pre_grad, up_part)

            @pl.when(part == 0)
            def _():
                out_sum[at, :] = out
                back_sum[at, :] = back

            @pl.when((part > 0) & (part < parts - 1))
            def _():
                out_sum[at, :] += out
                back_sum[at, :] += back

            @pl.when(part == parts - 1)
            def _():
                out_low[member, at, :] = (out_sum[at, :] + out).astype(BF)
                back_low[member, at, :] = (back_sum[at, :] + back).astype(BF)

            down_sum[...] += dot_tn(active, grads)
            up_sum[...] += dot_tn(source, pre_grad)
            return carry

        lax.fori_loop(0, chunks, chunk, 0)
        up_grad[...] = up_sum[...].astype(BF).reshape(up_grad.shape)
        down_grad[...] = down_sum[...].astype(BF).reshape(down_grad.shape)

    @pl.when(step >= 2 * parts)
    def _():
        tile = step - 2 * parts
        at = pl.ds(pl.multiple_of(tile * TILE, TILE), TILE)
        columns = info[tile].T
        grads = upstream[at, :].astype(F32)
        mixture[...] = jnp.zeros(mixture.shape, mixture.dtype)
        lane = lax.broadcasted_iota(jnp.int32, (1, LANES), 1)
        zero = jnp.zeros((TILE, width), F32)
        mix, back, dots = zero, zero, jnp.zeros((TILE, LANES), F32)
        for which in range(2):
            begin = meta[which * stride + tile]
            end = meta[which * stride + tile + 1]
            base = begin // 16 * 16
            count = jnp.where(end > begin, (end - base + TILE - 1) // TILE, 0)
            order = columns[:, which : which + 1]

            def fetch(j, carry, which=which, base=base, order=order):
                out, back = carry
                origin = pl.multiple_of(base + j * TILE, 16)
                wanted = lax.broadcasted_iota(jnp.int32, (1, TILE), 1) + origin
                chosen = jnp.where(order == wanted.astype(F32), 1.0, 0.0).astype(BF)
                source = pl.ds(origin, TILE)
                out += dot_nn(chosen, out_low[which, source, :])
                back += dot_nn(chosen, back_low[which, source, :])
                return out, back

            out, back = lax.fori_loop(0, count, fetch, (zero, back))
            mix += out * columns[:, 2 + which : 3 + which]
            dots += jnp.where(lane == which, jnp.sum(out * grads, -1, keepdims=True), 0.0)
        mixture[...] = mix.astype(BF)
        row_grad[...] = back.astype(BF)
        gate_grad[...] = dots.T[:8]


def expert_block(meta, info, up, down, rows, upstream, most):
    shards, members, rows_up, hidden_units = up.shape
    rows_down = down.shape[2]
    count, width = rows.shape
    tiles = count // TILE
    parts = hidden_units // 512
    span = hidden_units // parts
    room = ceil_to(most, TILE) + TILE
    shape = jax.ShapeDtypeStruct
    last = 2 * parts - 1

    def member_of(i):
        return jnp.minimum(i, last) // parts

    def part_of(i):
        return jnp.minimum(i, last) % parts

    up_spec = pl.BlockSpec(
        (shards, 1, rows_up, span), lambda i, *_: (0, member_of(i), 0, part_of(i))
    )
    down_spec = pl.BlockSpec(
        (span // rows_down, 1, rows_down, width), lambda i, *_: (part_of(i), member_of(i), 0, 0)
    )
    tile_spec = pl.BlockSpec((TILE, width), lambda i, *_: (jnp.maximum(i - last - 1, 0), 0))
    whole = pl.BlockSpec(memory_space=pltpu.VMEM)
    return pl.pallas_call(
        partial(expert_kernel, tiles, parts, room),
        grid_spec=pltpu.PrefetchScalarGridSpec(
            num_scalar_prefetch=1,
            grid=(2 * parts + tiles,),
            in_specs=[whole, up_spec, down_spec, whole, whole],
            out_specs=[
                tile_spec,
                tile_spec,
                pl.BlockSpec((8, TILE), lambda i, *_: (0, jnp.maximum(i - last - 1, 0))),
                up_spec,
                down_spec,
            ],
            scratch_shapes=[
                pltpu.VMEM((room, width), BF),
                pltpu.VMEM((room, width), BF),
                pltpu.VMEM((room, width), F32),
                pltpu.VMEM((room, width), F32),
                pltpu.VMEM((2, room, width), BF),
                pltpu.VMEM((2, room, width), BF),
                pltpu.VMEM((width, span), F32),
                pltpu.VMEM((span, width), F32),
            ],
        ),
        out_shape=(
            shape((count, width), BF),
            shape((count, width), BF),
            shape((8, count), F32),
            shape(up.shape, BF),
            shape(down.shape, BF),
        ),
        compiler_params=pltpu.CompilerParams(
            vmem_limit_bytes=VMEM_LIMIT, dimension_semantics=("arbitrary",)
        ),
        name="experts",
    )(meta, info, up, down, rows, upstream)


def retreat_kernel(
    experts,
    tokens,
    cotangent,
    hidden,
    normed,
    qkv,
    mixed,
    probs,
    gate_grad,
    returned,
    packed,
    token_grad,
    grads,
    first,
    hidden_grad,
    branch_grad,
    joined_grad,
    small,
    sums,
    totals,
):
    rows, width = tokens.shape
    real = token_grad.shape[0]
    images = rows // SEQ
    half = rows // 2
    small[...] = packed[:, 4 * width :].astype(F32).T
    gain_one, bias_one = small[experts : experts + 1, :], small[experts + 1 : experts + 2, :]
    gain_two = small[experts + 2 : experts + 3, :]
    sums[...] = jnp.zeros(sums.shape, F32)
    totals[...] = jnp.zeros(totals.shape, F32)

    share = probs[...]
    change = gate_grad[...]
    tilt = share * (change - jnp.sum(share * change, 0, keepdims=True))
    if experts < 16:
        tilt = jnp.concatenate([tilt, jnp.zeros((16 - experts, rows), F32)], 0)
    tilt = tilt.astype(BF)
    router = small[0 : tilt.shape[0], :].astype(BF)
    keep = lax.broadcasted_iota(jnp.int32, (tilt.shape[0], 1), 0) < experts
    router = jnp.where(keep, router, jnp.zeros_like(router))
    sums[0 : tilt.shape[0], :] = dot_nn(tilt, normed[...])
    hidden_grad[...] = dot_tn(tilt, router)

    def norm_two(j, carry):
        part = pl.ds(pl.multiple_of(j * STRIP, STRIP), STRIP)
        change = hidden_grad[part, :]
        for owner in range(returned.shape[0]):
            change += returned[owner, part, :].astype(F32)
        unit, inverse = normalize(hidden[part, :])
        tail = change * unit
        totals[0] += jnp.sum(tail.reshape(STRIP // 8, 8, width), 0)
        totals[1] += jnp.sum(change.reshape(STRIP // 8, 8, width), 0)
        change = change * gain_two
        mean = jnp.mean(change, -1, keepdims=True)
        lean = jnp.mean(change * unit, -1, keepdims=True)
        total = cotangent[part, :].astype(F32) + inverse * (change - mean - unit * lean)
        hidden_grad[part, :] = total
        branch_grad[part, :] = total.astype(BF)
        unit, _ = normalize(tokens[part, :].astype(F32))
        first[part, :] = (unit * gain_one + bias_one).astype(BF)
        joined_grad[part, :] = jnp.zeros((STRIP, 3 * width), BF)
        return carry

    lax.fori_loop(0, rows // STRIP, norm_two, 0)
    merge = slice(3 * width, 4 * width)
    grads[:, merge] = dot_tn(mixed[...], branch_grad[...]).astype(BF)

    def project(j, carry):
        part = pl.ds(pl.multiple_of(j * half, 16), half)
        branch_grad[part, :] = dot_nt(branch_grad[part, :], packed[:, merge]).astype(BF)
        return carry

    lax.fori_loop(0, 2, project, 0)

    lane = lax.broadcasted_iota(jnp.int32, (1, LANES), 1)
    low = lane < HEAD_DIM
    scale = 1.0 / HEAD_DIM**0.5

    def attend(image, carry):
        start, offset = window(image)
        part = pl.ds(start, WINDOW)
        place = lax.broadcasted_iota(jnp.int32, (WINDOW, 1), 0) - offset
        mine = (place >= 0) & (place < SEQ)
        for pair in range(width // LANES):
            at = pair * LANES
            query = qkv[part, at : at + LANES]
            key = qkv[part, width + at : width + at + LANES]
            value = qkv[part, 2 * width + at : 2 * width + at + LANES]
            change = branch_grad[part, at : at + LANES]
            change = jnp.where(mine, change, jnp.zeros_like(change))
            sides = []
            for side in (low, ~low):
                chosen = jnp.where(side, query, jnp.zeros_like(query))
                scores = jnp.where(mine, dot_nt(key, chosen) * scale, FAR)
                raised = jnp.exp(scores - jnp.max(scores, 0, keepdims=True))
                weights = raised * (1.0 / jnp.sum(raised, 0, keepdims=True))
                slope = dot_nt(value, jnp.where(side, change, jnp.zeros_like(change)))
                lean = jnp.sum(weights * slope, 0, keepdims=True)
                slope = (weights * (slope - lean)).astype(BF)
                sides.append(
                    (
                        dot_tn(slope, key) * scale,
                        dot_nn(slope, query) * scale,
                        dot_nn(weights.astype(BF), change),
                    )
                )
            for third in range(3):
                to = third * width + at
                joined_grad[part, to : to + LANES] += jnp.where(
                    low, sides[0][third], sides[1][third]
                ).astype(BF)
        return carry

    lax.fori_loop(0, images, attend, 0)
    for third in range(3):
        columns = slice(third * width, (third + 1) * width)
        grads[:, columns] = dot_tn(first[...], joined_grad[:, columns]).astype(BF)

    def finish(start, size):
        part = pl.ds(start, size)
        change = dot_nt(joined_grad[part, :], packed[:, : 3 * width])
        unit, inverse = normalize(tokens[part, :].astype(F32))
        tail = change * unit
        totals[2] += jnp.sum(tail.reshape(size // 8, 8, width), 0)
        totals[3] += jnp.sum(change.reshape(size // 8, 8, width), 0)
        change = change * gain_one
        mean = jnp.mean(change, -1, keepdims=True)
        lean = jnp.mean(change * unit, -1, keepdims=True)
        return hidden_grad[part, :] + inverse * (change - mean - unit * lean)

    block = 2 * STRIP

    def finish_loop(j, carry):
        start = pl.multiple_of(j * block, block)
        token_grad[pl.ds(start, block), :] = finish(start, block)
        return carry

    lax.fori_loop(0, real // block, finish_loop, 0)
    done = real // block * block
    if done < real:
        token_grad[done:real, :] = finish(done, ceil_to(real - done, 16))[: real - done]
    for which, row in ((2, experts), (3, experts + 1), (0, experts + 2), (1, experts + 3)):
        sums[row : row + 1, :] = jnp.sum(totals[which], 0, keepdims=True)
    grads[:, 4 * width :] = sums[...].T.astype(BF)


def retreat(
    tokens, cotangent, hidden, normed, qkv, mixed, probs, gate_grad, returned, packed, real
):
    rows, width = tokens.shape
    experts = probs.shape[0]
    shape = jax.ShapeDtypeStruct
    return pl.pallas_call(
        partial(retreat_kernel, experts),
        out_shape=(shape((real, width), F32), shape(packed.shape, BF)),
        in_specs=[pl.BlockSpec(memory_space=pltpu.VMEM)] * 10,
        out_specs=[pl.BlockSpec(memory_space=pltpu.VMEM)] * 2,
        scratch_shapes=[
            pltpu.VMEM((rows, width), BF),
            pltpu.VMEM((rows, width), F32),
            pltpu.VMEM((rows, width), BF),
            pltpu.VMEM((rows, 3 * width), BF),
            pltpu.VMEM((LANES, width), F32),
            pltpu.VMEM((LANES, width), F32),
            pltpu.VMEM((4, 8, width), F32),
        ],
        compiler_params=pltpu.CompilerParams(vmem_limit_bytes=VMEM_LIMIT),
        name="retreat",
    )(tokens, cotangent, hidden, normed, qkv, mixed, probs, gate_grad, returned, packed)


def plan_rows(routes, first_expert):
    owners, _, padded = routes.shape
    tiles = owners * padded // TILE
    mine = first_expert + jnp.arange(2, dtype=jnp.int32)[:, None, None]
    chosen = (routes[None, :, 0] == mine) | (routes[None, :, 1] == mine)
    chosen = chosen.reshape(2, tiles, TILE)
    flags = chosen.astype(BF)
    upper = jnp.triu(jnp.ones((TILE, TILE), BF))
    within = jnp.dot(flags.reshape(2 * tiles, TILE), upper, preferred_element_type=F32)
    within = within.reshape(2, tiles, TILE)
    counts = within[:, :, -1]
    below = jnp.tril(jnp.ones((tiles + 1, tiles), F32), -1)
    begins = jnp.sum(below[None] * counts[:, None, :], 2)
    order = jnp.where(chosen, begins[:, :tiles, None] + within - 1.0, -1.0)
    return order, begins.astype(jnp.int32).reshape(-1)


def local(
    tokens,
    routes,
    cotangent,
    attend_gain,
    attend_bias,
    triple_weight,
    merge_weight,
    mixture_gain,
    mixture_bias,
    router_weight,
    expert_up,
    expert_down,
):
    real, width = tokens.shape
    experts = router_weight.shape[1]
    owners = lax.axis_size("expert")
    capacity = 2 * TOP * real // experts
    padded = ceil_to(real, STRIP)
    spare = LANES - experts - 4
    here = lax.axis_index("expert")

    small = jnp.concatenate(
        [
            router_weight,
            attend_gain[:, None],
            attend_bias[:, None],
            mixture_gain[:, None],
            mixture_bias[:, None],
            jnp.zeros((router_weight.shape[0], spare), F32),
        ],
        1,
    )
    packed = jnp.concatenate([triple_weight, merge_weight, small], 1).astype(BF)
    packed = lax.all_gather(packed, "fsdp", axis=0, tiled=True)
    up_full = lax.all_gather(expert_up.astype(BF), "fsdp", axis=0)
    down_full = lax.all_gather(expert_down.astype(BF), "fsdp", axis=0)

    token_rows = jnp.pad(tokens, ((0, padded - real), (0, 0)))
    upstream = jnp.pad(cotangent, ((0, padded - real), (0, 0)))
    route_rows = jnp.pad(routes.T, ((0, 0), (0, padded - real)), constant_values=-1)
    all_routes = lax.all_gather(route_rows, "expert", axis=0)
    order, meta = plan_rows(all_routes, here * 2)
    tiles = owners * padded // TILE
    all_upstream = lax.all_gather(upstream, "expert", axis=0, tiled=True)

    qkv, mixed, hidden, normed, probs, gates = attend(token_rows, route_rows, packed, experts)
    all_rows = lax.all_gather(normed, "expert", axis=0, tiled=True)
    all_gates = lax.all_gather(gates, "expert", axis=0)
    own_gates = lax.dynamic_slice_in_dim(all_gates, here * 2, 2, 1)
    own_gates = own_gates.transpose(1, 0, 2).reshape(2, tiles, TILE)
    info = jnp.concatenate([order, own_gates, jnp.zeros((4, tiles, TILE), F32)], 0)
    info = info.transpose(1, 0, 2)

    mixture, row_grad, gate_grad, up_grad, down_grad = expert_block(
        meta, info, up_full, down_full, all_rows, all_upstream, owners * capacity
    )
    gate_grad = gate_grad[:2].reshape(2, owners, padded).transpose(1, 0, 2)
    gate_grad = lax.all_to_all(gate_grad, "expert", 0, 0).reshape(experts, padded)
    row_grad = lax.psum_scatter(
        row_grad.reshape(owners, padded, width), "expert", scatter_dimension=0, tiled=True
    )
    mixture = lax.psum_scatter(
        mixture.reshape(owners, padded, width), "expert", scatter_dimension=0, tiled=True
    )
    block_out = (hidden[:real] + mixture[0, :real].astype(F32)).astype(BF)
    up_grad = lax.psum_scatter(up_grad, "fsdp", scatter_dimension=0, tiled=True)
    down_grad = lax.psum_scatter(down_grad, "fsdp", scatter_dimension=0, tiled=True)

    token_grad, grads = retreat(
        token_rows,
        upstream,
        hidden,
        normed,
        qkv,
        mixed,
        probs,
        gate_grad,
        row_grad,
        packed,
        real,
    )
    grads = lax.psum_scatter(grads, "fsdp", scatter_dimension=0, tiled=True)
    grads = lax.psum(grads, "expert").astype(F32)
    rest = grads[:, 4 * width :]
    return (
        block_out,
        token_grad,
        rest[:, experts],
        rest[:, experts + 1],
        grads[:, : 3 * width],
        grads[:, 3 * width : 4 * width],
        rest[:, experts + 2],
        rest[:, experts + 3],
        rest[:, :experts],
        up_grad[0].astype(F32),
        down_grad[0].astype(F32),
    )


def solution(mesh):
    return jax.shard_map(
        local,
        mesh=mesh,
        in_specs=(
            P(("expert", "fsdp"), None),
            P(("expert", "fsdp"), None),
            P(("expert", "fsdp"), None),
            P("fsdp"),
            P("fsdp"),
            P("fsdp", None),
            P("fsdp", None),
            P("fsdp"),
            P("fsdp"),
            P("fsdp", None),
            P("expert", "fsdp", None),
            P("expert", "fsdp", None),
        ),
        out_specs=(
            P(("expert", "fsdp"), None),
            P(("expert", "fsdp"), None),
            P("fsdp"),
            P("fsdp"),
            P("fsdp", None),
            P("fsdp", None),
            P("fsdp"),
            P("fsdp"),
            P("fsdp", None),
            P("expert", "fsdp", None),
            P("expert", "fsdp", None),
        ),
        check_vma=False,
    )
```

time: 945 us -> 715 us (0.76)
  local copies, waits for them, and re-layouts: 248 us -> 13.6 us
  matrix products: 189 us -> 0.21 us
  Pallas kernels: 0 us -> 144 us
  waiting for transfers between devices: 341 us -> 466 us
  other arithmetic: 64 us -> 15.6 us
  starting transfers between devices: 18 us -> 0.44 us
    all_gather x3 -> x5, waiting for transfers between devices: 0.02 us -> 193 us  [the longest x1 69.2 us: local(): all_rows = lax.all_gather(normed, 'expert', axis=0, tiled=True)]
    all_to_all x4 -> x0, waiting for transfers between devices: 191 us -> none  [the longest x1 64.4 us: local(): lax.all_to_all(expert_out, 'expert', split_axis=2, concat_axis=0, tiled=T...]
    dot_general x27 -> x1, matrix products: 189 us -> 0.21 us  [plan_rows(): jnp.dot(flags.reshape(2 * tiles, TILE), upper, preferred_element_type=F32)]
    pallas_call x0 -> x3, Pallas kernels: none -> 144 us  [the longest x1 93.4 us: expert_block(): pl.pallas_call(partial(expert_kernel, tiles, parts, room), grid_spec=pltp...]
    reduce_scatter x4 -> x5, waiting for transfers between devices: 91.7 us -> 235 us  [the longest x1 66.6 us: local(): lax.psum_scatter(mixture.reshape(owners, padded, width), 'expert', scatte...]
    slice x4 -> x8, local copies, waits for them, and re-layouts: 78.3 us -> 5.83 us  [the longest x1 1.7 us: local(): grads[:, :3 * width]]
    reshape x12 -> x5, local copies, waits for them, and re-layouts: 54.8 us -> 0.86 us  [the longest x1 0.63 us: local(): lax.all_to_all(gate_grad, 'expert', 0, 0).reshape(experts, padded)]
    gather x4 -> x0, local copies, waits for them, and re-layouts: 35 us -> none  [the longest x1 10.3 us: local(): padded_grad[filler].reshape(owners, per_owner, capacity, width)]
  transfers between devices with their start and end apart: 13 -> 11, of which waited for: 8 -> 11; matrix products, arithmetic and copies ran while one was open for 30% -> 2% of each run, Pallas kernels for 0% -> 7%
where the time goes in v1:
time: 715 us; the launch traced here: 706 us
  waiting for transfers between devices  466 us (65%)
  Pallas kernels  144 us (20%)
  blocking collectives  52 us (7%)
  other arithmetic  15.6 us (2%)
  between operations  14 us (2%)
  local copies, waits for them, and re-layouts  13.6 us (2%)
    pallas_call x1, Pallas kernels, expert_block(): pl.pallas_call(partial(expert_kernel, tiles, parts, room), grid_spec=pltp...  93.4 us
    all_gather x1, waiting for transfers between devices, local(): all_rows = lax.all_gather(normed, 'expert', axis=0, tiled=True)  69.2 us
    reduce_scatter x1, waiting for transfers between devices, local(): lax.psum_scatter(mixture.reshape(owners, padded, width), 'expert', scatte...  66.6 us
    reduce_scatter x1, waiting for transfers between devices, local(): up_grad = lax.psum_scatter(up_grad, 'fsdp', scatter_dimension=0, tiled=True)  52.4 us
    reduce_scatter x1, waiting for transfers between devices, local(): lax.psum_scatter(row_grad.reshape(owners, padded, width), 'expert', scatt...  51.4 us
    reduce_scatter x1, waiting for transfers between devices, local(): grads = lax.psum_scatter(grads, 'fsdp', scatter_dimension=0, tiled=True)  43 us
    all_gather x1, waiting for transfers between devices, local(): down_full = lax.all_gather(expert_down.astype(BF), 'fsdp', axis=0)  38.9 us
    all_gather x1, waiting for transfers between devices, local(): up_full = lax.all_gather(expert_up.astype(BF), 'fsdp', axis=0)  37.7 us
  transfers between devices with their start and end apart: 11, of which 11 were waited for; matrix products, arithmetic and copies ran while one was open for 2% of the time, Pallas kernels for 7%

profile of v1, /device:TPU:0, one launch (start us, length us, event | category | flops | bytes accessed | tf_op | source)
XLA Modules:
  0.0 706.1 jit_solution(17132369915715249744)
XLA Ops:
  12.1 1.0 convert.30
  14.0 2.2 pad.13.cotangent
  19.8 25.4 %all-gather.11.cloned.1.call-done.packed = bf16[512,2176]{1,0:T(8,128)(2,1)} async-done(((bf16[64,2176]{1,0:T(8,128)(2,1)}), bf16[512,2176]{1,0:T(8,128)(2,1)}) %all-gather.11.cloned.1.call-update) | async-done | bytes 2228240 | tf_op jit(solution)/shard_map/all_gather | solution.py:624
  45.2 18.4 %attend.1 = (bf16[832,1536]{1,0:T(8,128)(2,1)}, bf16[832,512]{1,0:T(8,128)(2,1)}, f32[832,512]{1,0:T(8,128)}, bf16[832,512]{1,0:T(8,128)(2,1)}, f32[8,832]{1,0:T(8,128)}, /*index=5*/f32[8,832]{1,0:T(8,128)}) custom-call(bf16[832,512]{1,0:T(8,128)(2,1)} %pad.11.tokens, s32[2,832]{1,0:T(2,128)} %get-tuple-element.88.routes, ...), custom_call_target="tpu_custom_call" | custom-call | tf_op jit(solution)/shard_map/attend/pallas_call | solution.py:166
  63.7 13.7 %all-gather.4 = s32[4,2,832]{2,1,0:T(2,128)S(1)} all-gather(s32[1,2,832]{2,1,0:T(2,128)S(1)} %get-tuple-element.87), channel_id=2, replica_groups=mesh['expert'=4,'fsdp'=8] {'expert'}, dimensions={0}, use_global_device_ids=true | all-gather | bytes 33280 | tf_op jit(solution)/shard_map/all_gather | solution.py:631
  79.2 14.8 %all-gather.1 = f32[32,832]{1,0:T(8,128)S(1)} all-gather(f32[8,832]{1,0:T(8,128)} %get-tuple-element.25), channel_id=3, replica_groups=mesh['expert'=4,'fsdp'=8] {'expert'}, dimensions={0}, use_global_device_ids=true | all-gather | bytes 133120 | tf_op jit(solution)/shard_map/all_gather | solution.py:638
  94.9 21.8 %all-gather.15.cloned.1.call-done.upstream = bf16[3328,512]{1,0:T(8,128)(2,1)} async-done(((bf16[832,512]{1,0:T(8,128)(2,1)}), bf16[3328,512]{1,0:T(8,128)(2,1)}) %all-gather.15.cloned.1.call-update) | async-done | bytes 3407888 | tf_op jit(solution)/shard_map/all_gather | solution.py:634
  116.7 37.7 %all-gather.17.cloned.1.call-done = bf16[16,64,2048]{2,1,0:T(8,128)(2,1)} async-done(((bf16[2,64,2048]{2,1,0:T(8,128)(2,1)}), bf16[16,64,2048]{2,1,0:T(8,128)(2,1)}) %all-gather.17.cloned.1.call-update) | async-done | bytes 4194320 | tf_op jit(solution)/shard_map/all_gather | solution.py:625
  154.4 38.9 %all-gather.19.cloned.1.call-done = bf16[16,256,512]{2,1,0:T(8,128)(2,1)} async-done(((bf16[2,256,512]{2,1,0:T(8,128)(2,1)}), bf16[16,256,512]{2,1,0:T(8,128)(2,1)}) %all-gather.19.cloned.1.call-update) | async-done | bytes 4194320 | tf_op jit(solution)/shard_map/all_gather | solution.py:626
  193.3 69.2 %all-gather.13.cloned.1.call-done.rows = bf16[3328,512]{1,0:T(8,128)(2,1)} async-done(((bf16[832,512]{1,0:T(8,128)(2,1)}), bf16[3328,512]{1,0:T(8,128)(2,1)}) %all-gather.13.cloned.1.call-update) | async-done | bytes 3407888 | tf_op jit(solution)/shard_map/all_gather | solution.py:637
  262.6 93.4 %experts.1 = (bf16[3328,512]{1,0:T(8,128)(2,1)}, bf16[3328,512]{1,0:T(8,128)(2,1)}, f32[8,3328]{1,0:T(8,128)}, bf16[8,2,64,2048]{3,2,1,0:T(8,128)(2,1)}, bf16[8,2,256,512]{3,2,1,0:T(8,128)(2,1)}) custom-call(s32[28]{0:T(128)} %convert_element_type.43.meta, f32[13,8,256]{2,1,0:T(8,128)} %maximum_bitcast_fusion.info, bf16[8,2,64,2048]{3,2,1,0:T(8,128)(2,1)} %bitcast.40, ...), custom_call_target="tpu_custom_call" | custom-call | tf_op jit(solution)/shard_map/experts/pallas_call | solution.py:363
  358.6 23.4 %all_to_all.5 = f32[4,2,832]{2,1,0:T(2,128)S(1)} all-to-all(f32[4,2,832]{2,1,0:T(2,128)S(1)} %bitcast.45), channel_id=1, replica_groups=mesh['expert'=4,'fsdp'=8] {'expert'}, dimensions={0} | all-to-all | bytes 53248 | tf_op jit(solution)/shard_map/all_to_all | solution.py:648
  382.6 51.4 %reduce-scatter.8.cloned.1.call-done.returned = bf16[1,832,512]{2,1,0:T(8,128)(2,1)} async-done(((bf16[4,832,512]{2,1,0:T(8,128)(2,1)}), bf16[1,832,512]{2,1,0:T(8,128)(2,1)}) %reduce-scatter.8.cloned.1.call-update) | async-done | bytes 851984 | tf_op jit(solution)/shard_map/reduce_scatter | solution.py:649
  434.0 32.1 %retreat.1 = (f32[788,512]{1,0:T(8,128)}, bf16[512,2176]{1,0:T(8,128)(2,1)}) custom-call(bf16[832,512]{1,0:T(8,128)(2,1)} %pad.11.tokens, bf16[832,512]{1,0:T(8,128)(2,1)} %pad.13.cotangent, f32[832,512]{1,0:T(8,128)} %get-tuple-element.24.hidden, bf16[832,512]{1,0:T(8,128)(2,1)} %get-tuple-element.26.normed, bf16[832,1536]{1,0:T(8,128)(2,1)} %get-tuple-element.28.qkv, ...), custom_call_target="tpu_custom_call" | custom-call | tf_op jit(solution)/shard_map/retreat/pallas_call | solution.py:554
  466.7 21.9 %reduce-scatter.14.cloned.1.call-done = bf16[1,2,256,512]{3,2,1,0:T(8,128)(2,1)} async-done(((bf16[8,2,256,512]{3,2,1,0:T(8,128)(2,1)}), bf16[1,2,256,512]{3,2,1,0:T(8,128)(2,1)}) %reduce-scatter.14.cloned.1.call-update) | async-done | bytes 524304 | tf_op jit(solution)/shard_map/reduce_scatter | solution.py:657
  488.6 2.1 bitcast_convert_fusion
  490.8 52.4 %reduce-scatter.12.cloned.1.call-done = bf16[1,2,64,2048]{3,2,1,0:T(8,128)(2,1)} async-done(((bf16[8,2,64,2048]{3,2,1,0:T(8,128)(2,1)}), bf16[1,2,64,2048]{3,2,1,0:T(8,128)(2,1)}) %reduce-scatter.12.cloned.1.call-update) | async-done | bytes 524304 | tf_op jit(solution)/shard_map/reduce_scatter | solution.py:656
  543.1 2.1 bitcast_convert_fusion.1
  545.3 43.0 %reduce-scatter.10.cloned.1.call-done = bf16[64,2176]{1,0:T(8,128)(2,1)} async-done(((bf16[512,2176]{1,0:T(8,128)(2,1)}), bf16[64,2176]{1,0:T(8,128)(2,1)}) %reduce-scatter.10.cloned.1.call-update) | async-done | bytes 278544 | tf_op jit(solution)/shard_map/reduce_scatter | solution.py:672
  588.3 66.6 %reduce-scatter.6.cloned.1.call-done = bf16[1,832,512]{2,1,0:T(8,128)(2,1)} async-done(((bf16[4,832,512]{2,1,0:T(8,128)(2,1)}), bf16[1,832,512]{2,1,0:T(8,128)(2,1)}) %reduce-scatter.6.cloned.1.call-update) | async-done | bytes 851984 | tf_op jit(solution)/shard_map/reduce_scatter | solution.py:652
  654.9 2.3 fusion
  657.2 36.0 %all-reduce.5.cloned.1.call-done = bf16[64,2176]{1,0:T(8,128)(2,1)} async-done(((bf16[64,2176]{1,0:T(8,128)(2,1)}), bf16[64,2176]{1,0:T(8,128)(2,1)}) %all-reduce.5.cloned.1.call-update) | async-done | bytes 278544 | tf_op jit(solution)/shard_map/psum | solution.py:673
  696.4 1.5 slice.69
  697.9 1.7 slice.68
  (80 shorter events, 18.9 us)
Async XLA Ops:
  7.2 9.2 %copy-start.1 = (f32[2,64,2048]{2,1,0:T(8,128)S(1)}, f32[2,64,2048]{2,1,0:T(8,128)}, u32[]{:S(2)}) copy-start(f32[2,64,2048]{2,1,0:T(8,128)} %param.22) | copy-start | bytes 3145732
  7.2 38.0 %all-gather.11.cloned.1.call-start = ((), (), s32[]{:S(2)}) async-start(), calls=%async_computation.6 | async-start | bytes 2506752 | tf_op jit(solution)/shard_map/all_gather | solution.py:624
  14.0 3.3 copy-start.2
  14.0 102.7 %all-gather.15.cloned.1.call-start = ((), (), s32[]{:S(2)}) async-start(), calls=%async_computation.8 | async-start | bytes 4259840 | tf_op jit(solution)/shard_map/all_gather | solution.py:634
  16.3 2.0 copy-start.3
  16.3 2.9 copy-start.4
  16.3 138.1 %all-gather.17.cloned.1.call-start = ((), (), s32[]{:S(2)}) async-start(), calls=%async_computation.15 | async-start | bytes 4718592 | tf_op jit(solution)/shard_map/all_gather | solution.py:625
  17.3 176.1 %all-gather.19.cloned.1.call-start = ((), (), s32[]{:S(2)}) async-start(), calls=%async_computation.16 | async-start | bytes 4718592 | tf_op jit(solution)/shard_map/all_gather | solution.py:626
  18.2 244.3 %all-gather.13.cloned.1.call-start = ((), (), s32[]{:S(2)}) async-start(), calls=%async_computation.7 | async-start | bytes 4259840 | tf_op jit(solution)/shard_map/all_gather | solution.py:637
  63.6 370.4 %reduce-scatter.8.cloned.1.call-start = ((), (), s32[]{:S(2)}) async-start(), calls=%async_computation.10 | async-start | bytes 4259840 | tf_op jit(solution)/shard_map/reduce_scatter | solution.py:649
  356.0 132.6 %reduce-scatter.14.cloned.1.call-start = ((), (), s32[]{:S(2)}) async-start(), calls=%async_computation.14 | async-start | bytes 4718592 | tf_op jit(solution)/shard_map/reduce_scatter | solution.py:657
  356.7 186.4 %reduce-scatter.12.cloned.1.call-start = ((), (), s32[]{:S(2)}) async-start(), calls=%async_computation.13 | async-start | bytes 4718592 | tf_op jit(solution)/shard_map/reduce_scatter | solution.py:656
  357.5 230.8 %reduce-scatter.10.cloned.1.call-start = ((), (), s32[]{:S(2)}) async-start(), calls=%async_computation.11 | async-start | bytes 2506752 | tf_op jit(solution)/shard_map/reduce_scatter | solution.py:672
  466.1 188.8 %reduce-scatter.6.cloned.1.call-start = ((), (), s32[]{:S(2)}) async-start(), calls=%async_computation.9 | async-start | bytes 4259840 | tf_op jit(solution)/shard_map/reduce_scatter | solution.py:652
  466.7 188.3 %copy-start = (f32[832,512]{1,0:T(8,128)S(1)}, f32[832,512]{1,0:T(8,128)}, u32[]{:S(2)}) copy-start(f32[832,512]{1,0:T(8,128)} %get-tuple-element.24.hidden) | copy-start | bytes 5111812
  466.7 226.6 %all-reduce.5.cloned.1.call-start = ((), (), s32[]{:S(2)}) async-start(), calls=%async_computation.12 | async-start | bytes 557056 | tf_op jit(solution)/shard_map/psum | solution.py:673
Sparse Core Ops, SparseCore 0:
  14.1 31.0 all-gather.10
  46.8 69.8 all-gather.14
  119.2 35.1 all-gather.16
  156.7 36.5 all-gather.18
  194.8 67.7 all-gather.12
  356.1 77.8 reduce-scatter.7
  437.3 51.2 reduce-scatter.13
  492.0 51.1 reduce-scatter.11
  546.5 41.7 reduce-scatter.9
  590.4 64.4 reduce-scatter.5
  657.3 35.9 all-reduce.4

commit v2 on v1

--- a/solution.py
+++ b/solution.py
@@ -207,23 +207,24 @@
 ):
     width = rows.shape[1]
     step = pl.program_id(0)
-    member = jnp.minimum(step // parts, 1)
+    owned = out_low.shape[0]
+    member = jnp.minimum(step // parts, owned - 1)
     part = step - member * parts
     span = up_sum.shape[1]
-    stride = meta.shape[0] // 2
+    stride = meta.shape[0] // owned
 
     @pl.when(step == 0)
     def _():
         def clear(j, carry):
             at = pl.ds(pl.multiple_of(j * TILE, TILE), TILE)
-            for which in range(2):
+            for which in range(owned):
                 out_low[which, at, :] = jnp.zeros((TILE, width), BF)
                 back_low[which, at, :] = jnp.zeros((TILE, width), BF)
             return carry
 
         lax.fori_loop(0, room // TILE, clear, 0)
 
-    @pl.when((step < 2 * parts) & (part == 0))
+    @pl.when((step < owned * parts) & (part == 0))
     def _():
         def clear(j, carry):
             at = pl.ds(pl.multiple_of(j * TILE, TILE), TILE)
@@ -239,10 +240,11 @@
             base = begin // 16 * 16
             count = jnp.where(end > begin, (end - base + SUB - 1) // SUB, 0)
             at = pl.ds(pl.multiple_of(tile * TILE, TILE), TILE)
-            known = info[tile]
-            order = jnp.where(member == 0, known[0:1, :], known[1:2, :])
-            columns = known.T
-            gate = jnp.where(member == 0, columns[:, 2:3], columns[:, 3:4])
+            order = info[tile, pl.ds(member, 1), :]
+            columns = info[tile].T
+            which = lax.broadcasted_iota(jnp.int32, (1, columns.shape[1]), 1)
+            gate = jnp.where(which == owned + member, columns, 0.0)
+            gate = jnp.sum(gate, -1, keepdims=True)
             source = rows[at, :]
             gated = (upstream[at, :].astype(F32) * gate).astype(BF)
 
@@ -259,7 +261,7 @@
 
         lax.fori_loop(0, tiles, gather, 0)
 
-    @pl.when(step < 2 * parts)
+    @pl.when(step < owned * parts)
     def _():
         up_part = up[...].reshape(width, span)
         down_part = down[...].reshape(span, width)
@@ -300,9 +302,9 @@
         up_grad[...] = up_sum[...].astype(BF).reshape(up_grad.shape)
         down_grad[...] = down_sum[...].astype(BF).reshape(down_grad.shape)
 
-    @pl.when(step >= 2 * parts)
+    @pl.when(step >= owned * parts)
     def _():
-        tile = step - 2 * parts
+        tile = step - owned * parts
         at = pl.ds(pl.multiple_of(tile * TILE, TILE), TILE)
         columns = info[tile].T
         grads = upstream[at, :].astype(F32)
@@ -310,7 +312,7 @@
         lane = lax.broadcasted_iota(jnp.int32, (1, LANES), 1)
         zero = jnp.zeros((TILE, width), F32)
         mix, back, dots = zero, zero, jnp.zeros((TILE, LANES), F32)
-        for which in range(2):
+        for which in range(owned):
             begin = meta[which * stride + tile]
             end = meta[which * stride + tile + 1]
             base = begin // 16 * 16
@@ -328,7 +330,7 @@
                 return out, back
 
             out, back = lax.fori_loop(0, count, fetch, (zero, back))
-            mix += out * columns[:, 2 + which : 3 + which]
+            mix += out * columns[:, owned + which : owned + which + 1]
             dots += jnp.where(lane == which, jnp.sum(out * grads, -1, keepdims=True), 0.0)
         mixture[...] = mix.astype(BF)
         row_grad[...] = back.astype(BF)
@@ -336,15 +338,16 @@
 
 
 def expert_block(meta, info, up, down, rows, upstream, most):
-    shards, members, rows_up, hidden_units = up.shape
-    rows_down = down.shape[2]
+    groups, shards, members, rows_up, hidden_units = up.shape
+    rows_down = down.shape[3]
+    owned = groups * members
     count, width = rows.shape
     tiles = count // TILE
     parts = hidden_units // 512
     span = hidden_units // parts
     room = ceil_to(most, TILE) + TILE
     shape = jax.ShapeDtypeStruct
-    last = 2 * parts - 1
+    last = owned * parts - 1
 
     def member_of(i):
         return jnp.minimum(i, last) // parts
@@ -353,10 +356,12 @@
         return jnp.minimum(i, last) % parts
 
     up_spec = pl.BlockSpec(
-        (shards, 1, rows_up, span), lambda i, *_: (0, member_of(i), 0, part_of(i))
+        (1, shards, 1, rows_up, span),
+        lambda i, *_: (member_of(i) // members, 0, member_of(i) % members, 0, part_of(i)),
     )
     down_spec = pl.BlockSpec(
-        (span // rows_down, 1, rows_down, width), lambda i, *_: (part_of(i), member_of(i), 0, 0)
+        (1, span // rows_down, 1, rows_down, width),
+        lambda i, *_: (member_of(i) // members, part_of(i), member_of(i) % members, 0, 0),
     )
     tile_spec = pl.BlockSpec((TILE, width), lambda i, *_: (jnp.maximum(i - last - 1, 0), 0))
     whole = pl.BlockSpec(memory_space=pltpu.VMEM)
@@ -364,7 +369,7 @@
         partial(expert_kernel, tiles, parts, room),
         grid_spec=pltpu.PrefetchScalarGridSpec(
             num_scalar_prefetch=1,
-            grid=(2 * parts + tiles,),
+            grid=(owned * parts + tiles,),
             in_specs=[whole, up_spec, down_spec, whole, whole],
             out_specs=[
                 tile_spec,
@@ -378,8 +383,8 @@
                 pltpu.VMEM((room, width), BF),
                 pltpu.VMEM((room, width), F32),
                 pltpu.VMEM((room, width), F32),
-                pltpu.VMEM((2, room, width), BF),
-                pltpu.VMEM((2, room, width), BF),
+                pltpu.VMEM((owned, room, width), BF),
+                pltpu.VMEM((owned, room, width), BF),
                 pltpu.VMEM((width, span), F32),
                 pltpu.VMEM((span, width), F32),
             ],
@@ -408,18 +413,11 @@
     mixed,
     probs,
     gate_grad,
-    returned,
     packed,
-    token_grad,
-    grads,
-    first,
-    hidden_grad,
-    branch_grad,
-    joined_grad,
-    small,
-    sums,
-    totals,
+    *rest,
 ):
+    returned, rest = rest[:-9], rest[-9:]
+    token_grad, grads, first, hidden_grad, branch_grad, joined_grad, small, sums, totals = rest
     rows, width = tokens.shape
     real = token_grad.shape[0]
     images = rows // SEQ
@@ -445,8 +443,8 @@
     def norm_two(j, carry):
         part = pl.ds(pl.multiple_of(j * STRIP, STRIP), STRIP)
         change = hidden_grad[part, :]
-        for owner in range(returned.shape[0]):
-            change += returned[owner, part, :].astype(F32)
+        for arrived in returned:
+            change += arrived[part, :].astype(F32)
         unit, inverse = normalize(hidden[part, :])
         tail = change * unit
         totals[0] += jnp.sum(tail.reshape(STRIP // 8, 8, width), 0)
@@ -554,7 +552,7 @@
     return pl.pallas_call(
         partial(retreat_kernel, experts),
         out_shape=(shape((real, width), F32), shape(packed.shape, BF)),
-        in_specs=[pl.BlockSpec(memory_space=pltpu.VMEM)] * 10,
+        in_specs=[pl.BlockSpec(memory_space=pltpu.VMEM)] * (9 + len(returned)),
         out_specs=[pl.BlockSpec(memory_space=pltpu.VMEM)] * 2,
         scratch_shapes=[
             pltpu.VMEM((rows, width), BF),
@@ -567,19 +565,19 @@
         ],
         compiler_params=pltpu.CompilerParams(vmem_limit_bytes=VMEM_LIMIT),
         name="retreat",
-    )(tokens, cotangent, hidden, normed, qkv, mixed, probs, gate_grad, returned, packed)
-
-
-def plan_rows(routes, first_expert):
-    owners, _, padded = routes.shape
-    tiles = owners * padded // TILE
-    mine = first_expert + jnp.arange(2, dtype=jnp.int32)[:, None, None]
+    )(tokens, cotangent, hidden, normed, qkv, mixed, probs, gate_grad, packed, *returned)
+
+
+def plan_rows(routes, mine):
+    owned = mine.shape[0]
+    tiles = routes.shape[0] * routes.shape[2] // TILE
+    mine = mine[:, None, None]
     chosen = (routes[None, :, 0] == mine) | (routes[None, :, 1] == mine)
-    chosen = chosen.reshape(2, tiles, TILE)
+    chosen = chosen.reshape(owned, tiles, TILE)
     flags = chosen.astype(BF)
     upper = jnp.triu(jnp.ones((TILE, TILE), BF))
-    within = jnp.dot(flags.reshape(2 * tiles, TILE), upper, preferred_element_type=F32)
-    within = within.reshape(2, tiles, TILE)
+    within = jnp.dot(flags.reshape(owned * tiles, TILE), upper, preferred_element_type=F32)
+    within = within.reshape(owned, tiles, TILE)
     counts = within[:, :, -1]
     below = jnp.tril(jnp.ones((tiles + 1, tiles), F32), -1)
     begins = jnp.sum(below[None] * counts[:, None, :], 2)
@@ -587,7 +585,447 @@
     return order, begins.astype(jnp.int32).reshape(-1)
 
 
-def local(
+def table_of(order, gates):
+    owned, tiles, _ = order.shape
+    parts = [order, gates]
+    if 2 * owned < 8:
+        parts.append(jnp.zeros((8 - 2 * owned, tiles, TILE), F32))
+    return jnp.concatenate(parts, 0).transpose(1, 0, 2)
+
+
+MESH = pl.DeviceIdType.MESH
+ANY = pl.BlockSpec(memory_space=pl.ANY)
+VMEM = pl.BlockSpec(memory_space=pltpu.VMEM)
+PATHS = 10
+
+
+class Place:
+    def __init__(self):
+        z, me = lax.axis_index("expert"), lax.axis_index("fsdp")
+        self.me = me
+        self.x = me + 2 - 4 * ((me // 2) % 2)
+        turn = 4 - 8 * (me // 4)
+        self.y = me + turn
+        self.corner = self.x + turn
+        self.swap = 1 - 2 * (me % 2)
+        self.to_x, self.to_y = {"fsdp": self.x}, {"fsdp": self.y}
+        self.to_core = {"fsdp": me + self.swap}
+        self.to_twin = {"expert": z + 1 - 2 * (z % 2)}
+        self.to_far = {"expert": (z + 2) % 4}
+
+    def meet(self, partners):
+        barrier = pltpu.get_barrier_semaphore()
+        for partner in partners:
+            pl.semaphore_signal(barrier, inc=1, device_id=partner, device_id_type=MESH)
+        pl.semaphore_wait(barrier, len(partners))
+
+
+def send_to(source, target, sent, arrived, partner):
+    return pltpu.make_async_remote_copy(
+        src_ref=source,
+        dst_ref=target,
+        send_sem=sent,
+        recv_sem=arrived,
+        device_id=partner,
+        device_id_type=MESH,
+    )
+
+
+class Spread:
+    def __init__(self, place, source, target, sent, arrived):
+        def copy(path, piece, spot, partner):
+            return send_to(piece, spot, sent.at[path], arrived.at[path], partner)
+
+        def relay(path, spot, partner):
+            return copy(path, spot, spot, partner)
+
+        own = target.at[place.me]
+        self.own_x = copy(0, source, own, place.to_x)
+        self.own_y = copy(1, source, own, place.to_y)
+        self.own_core = copy(2, source, own, place.to_core)
+        self.x_on = relay(3, target.at[place.x, 0], place.to_y)
+        self.x_core = relay(4, target.at[place.x], place.to_core)
+        self.y_on = relay(5, target.at[place.y, 1], place.to_x)
+        self.y_core = relay(6, target.at[place.y], place.to_core)
+        self.low_core = relay(7, target.at[place.corner, 0], place.to_core)
+        self.high_core = relay(8, target.at[place.corner, 1], place.to_core)
+        self.last = (self.own_core, self.x_core, self.y_core, self.low_core, self.high_core)
+
+    def start(self):
+        for copy in (self.own_x, self.own_y, self.own_core):
+            copy.start()
+
+    def pass_on(self):
+        self.own_x.wait_recv()
+        self.x_on.start()
+        self.x_core.start()
+        self.own_y.wait_recv()
+        self.y_on.start()
+        self.y_core.start()
+
+    def share(self):
+        self.x_on.wait_recv()
+        self.low_core.start()
+        self.y_on.wait_recv()
+        self.high_core.start()
+
+    def finish(self):
+        for copy in self.last:
+            copy.wait_recv()
+        for copy in self.last + (self.own_x, self.own_y, self.x_on, self.y_on):
+            copy.wait_send()
+
+
+def add_up(target, *terms):
+    rows, columns = target.shape
+    strip = max(16, 16384 // columns // 16 * 16)
+    strip = min(strip, rows)
+
+    def body(j, carry):
+        part = pl.ds(pl.multiple_of(j * strip, strip), strip)
+        total = terms[0][part, :].astype(F32)
+        for term in terms[1:]:
+            total += term[part, :].astype(F32)
+        target[part, :] = total.astype(target.dtype)
+        return carry
+
+    lax.fori_loop(0, rows // strip, body, 0)
+
+
+class Fold:
+    def __init__(self, place, source, mine, got, bend, from_x, from_y, sent, arrived, loaded):
+        def copy(path, piece, spot, partner):
+            return send_to(piece, spot, sent.at[path], arrived.at[path], partner)
+
+        slots = (place.me, place.x, place.y, place.corner)
+        self.loads = [
+            pltpu.make_async_copy(source.at[slot], mine.at[i], loaded.at[i])
+            for i, slot in enumerate(slots)
+        ]
+        self.swaps = [
+            copy(i, source.at[slot + place.swap], got.at[i], place.to_core)
+            for i, slot in enumerate(slots)
+        ]
+        self.bend_y = copy(4, mine.at[3, 0], bend.at[0], place.to_y)
+        self.bend_x = copy(5, mine.at[3, 1], bend.at[1], place.to_x)
+        self.early_x = copy(6, mine.at[1, 1], from_x.at[1], place.to_x)
+        self.early_y = copy(7, mine.at[2, 0], from_y.at[0], place.to_y)
+        self.late_x = copy(8, mine.at[1, 0], from_x.at[0], place.to_x)
+        self.late_y = copy(9, mine.at[2, 1], from_y.at[1], place.to_y)
+        self.mine, self.got, self.bend = mine, got, bend
+        self.from_x, self.from_y = from_x, from_y
+
+    def start(self):
+        for i in (3, 1, 2, 0):
+            self.swaps[i].start()
+            self.loads[i].start()
+
+    def join(self, i):
+        self.loads[i].wait()
+        self.swaps[i].wait_recv()
+        for half in range(2):
+            mine = self.mine.at[i, half]
+            add_up(mine, mine, self.got.at[i, half])
+
+    def outward(self):
+        self.join(3)
+        self.bend_y.start()
+        self.bend_x.start()
+        self.join(1)
+        self.early_x.start()
+        self.join(2)
+        self.early_y.start()
+
+    def inward(self):
+        self.bend_y.wait_recv()
+        mine = self.mine.at[1, 0]
+        add_up(mine, mine, self.bend.at[0])
+        self.late_x.start()
+        self.bend_x.wait_recv()
+        mine = self.mine.at[2, 1]
+        add_up(mine, mine, self.bend.at[1])
+        self.late_y.start()
+
+    def total(self, target, *more):
+        self.loads[0].wait()
+        self.swaps[0].wait_recv()
+        for copy in (self.early_x, self.early_y, self.late_x, self.late_y):
+            copy.wait_recv()
+        for half in range(2):
+            terms = [self.mine.at[0, half], self.got.at[0, half]]
+            terms += [self.from_x.at[half], self.from_y.at[half]]
+            add_up(target.at[half], *terms, *[term.at[half] for term in more])
+
+    def finish(self):
+        for copy in self.swaps:
+            copy.wait_send()
+        for copy in (self.bend_y, self.bend_x, self.early_x, self.early_y):
+            copy.wait_send()
+        self.late_x.wait_send()
+        self.late_y.wait_send()
+
+
+def fold_scratch(half):
+    return [
+        pltpu.VMEM((4, 2, *half), BF),
+        pltpu.VMEM((4, 2, *half), BF),
+        pltpu.VMEM((2, *half), BF),
+        pltpu.VMEM((2, *half), BF),
+        pltpu.VMEM((2, *half), BF),
+        pltpu.SemaphoreType.DMA((PATHS,)),
+        pltpu.SemaphoreType.DMA((PATHS,)),
+        pltpu.SemaphoreType.DMA((4,)),
+    ]
+
+
+def comm_params(number):
+    return pltpu.CompilerParams(
+        collective_id=number, has_side_effects=True, vmem_limit_bytes=VMEM_LIMIT
+    )
+
+
+def gather_small_kernel(shard, full, sent, arrived, kept):
+    place = Place()
+    place.meet([place.to_x, place.to_y, place.to_core])
+    keep = pltpu.make_async_copy(shard, full.at[place.me], kept)
+    keep.start()
+    spread = Spread(place, shard, full, sent, arrived)
+    spread.start()
+    spread.pass_on()
+    spread.share()
+    spread.finish()
+    keep.wait()
+
+
+def gather_small(shard):
+    return pl.pallas_call(
+        gather_small_kernel,
+        out_shape=jax.ShapeDtypeStruct((8, *shard.shape), BF),
+        in_specs=[VMEM],
+        out_specs=VMEM,
+        scratch_shapes=[
+            pltpu.SemaphoreType.DMA((PATHS,)),
+            pltpu.SemaphoreType.DMA((PATHS,)),
+            pltpu.SemaphoreType.DMA(()),
+        ],
+        compiler_params=comm_params(1),
+        name="gather_small",
+    )(shard)
+
+
+def gather_large_kernel(
+    up, down, rows, upstream, gates, up_full, down_full, rows_full, upstream_full, gates_full, *sems
+):
+    sent, arrived, z_sent, z_arrived, kept = sems
+    place = Place()
+    place.meet([place.to_x, place.to_y, place.to_core, place.to_twin, place.to_far])
+    twins, near, far, keeps = [], [], [], []
+    for i, (source, full) in enumerate(((up, up_full), (down, down_full))):
+        spot = full.at[1, place.me]
+        twins.append(send_to(source, spot, z_sent.at[i], z_arrived.at[i], place.to_twin))
+        near.append(Spread(place, source, full.at[0], sent.at[i], arrived.at[i]))
+        far.append(Spread(place, spot, full.at[1], sent.at[2 + i], arrived.at[2 + i]))
+        keeps.append(pltpu.make_async_copy(source, full.at[0, place.me], kept.at[i]))
+    for copy in twins:
+        copy.start()
+    for spread in near:
+        spread.start()
+    pairs = ((rows, rows_full), (upstream, upstream_full), (gates, gates_full))
+    across = []
+    for i, (source, full) in enumerate(pairs):
+        at = 2 + i
+        across.append(
+            send_to(source, full.at[1], z_sent.at[at], z_arrived.at[at], place.to_far)
+        )
+        keeps.append(pltpu.make_async_copy(source, full.at[0], kept.at[at]))
+    for copy in across + keeps:
+        copy.start()
+    for i in range(2):
+        near[i].pass_on()
+        twins[i].wait_recv()
+        far[i].start()
+    for i in range(2):
+        near[i].share()
+        far[i].pass_on()
+    for i in range(2):
+        far[i].share()
+    for spread in near + far:
+        spread.finish()
+    for copy in twins:
+        copy.wait_send()
+    for copy in across + keeps:
+        copy.wait()
+
+
+def gather_large(up, down, rows, upstream, gates):
+    shape = jax.ShapeDtypeStruct
+    return pl.pallas_call(
+        gather_large_kernel,
+        out_shape=(
+            shape((2, 8, *up.shape), BF),
+            shape((2, 8, *down.shape), BF),
+            shape((2, *rows.shape), BF),
+            shape((2, *upstream.shape), BF),
+            shape((2, *gates.shape), F32),
+        ),
+        in_specs=[VMEM] * 5,
+        out_specs=[ANY] * 5,
+        scratch_shapes=[
+            pltpu.SemaphoreType.DMA((4, PATHS)),
+            pltpu.SemaphoreType.DMA((4, PATHS)),
+            pltpu.SemaphoreType.DMA((5,)),
+            pltpu.SemaphoreType.DMA((5,)),
+            pltpu.SemaphoreType.DMA((5,)),
+        ],
+        compiler_params=comm_params(2),
+        name="gather_large",
+    )(up, down, rows, upstream, gates)
+
+
+def reduce_large_kernel(
+    up, down, rows, mixture, gates, up_total, down_total, rows_far, mixture_far, gates_far, *rest
+):
+    z_sent, z_arrived, up_low, down_low, up_far, down_far = rest[:6]
+    buffers = rest[6:]
+    place = Place()
+    place.meet([place.to_x, place.to_y, place.to_core, place.to_twin, place.to_far])
+    count = rows_far.shape[0]
+    pairs = (
+        (rows.at[pl.ds(count, count)], rows_far),
+        (gates.at[:, pl.ds(count, count)], gates_far),
+        (mixture.at[pl.ds(count, count)], mixture_far),
+    )
+    across = [
+        send_to(source, target, z_sent.at[i], z_arrived.at[i], place.to_far)
+        for i, (source, target) in enumerate(pairs)
+    ]
+    for copy in across:
+        copy.start()
+    sources = (up.at[1], down.at[1], up.at[0], down.at[0])
+    folds = [
+        Fold(place, source, *buffers[8 * i : 8 * i + 8]) for i, source in enumerate(sources)
+    ]
+    twins = [
+        send_to(low, far, z_sent.at[3 + i], z_arrived.at[3 + i], place.to_twin)
+        for i, (low, far) in enumerate(((up_low, up_far), (down_low, down_far)))
+    ]
+    for fold in folds:
+        fold.start()
+    folds[0].outward()
+    folds[1].outward()
+    folds[0].inward()
+    folds[2].outward()
+    folds[1].inward()
+    folds[3].outward()
+    folds[0].total(up_low)
+    twins[0].start()
+    folds[2].inward()
+    folds[1].total(down_low)
+    twins[1].start()
+    folds[3].inward()
+    twins[0].wait_recv()
+    folds[2].total(up_total, up_far)
+    twins[1].wait_recv()
+    folds[3].total(down_total, down_far)
+    for fold in folds:
+        fold.finish()
+    for copy in twins:
+        copy.wait_send()
+    for copy in across:
+        copy.wait()
+
+
+def reduce_large(up, down, rows, mixture, gates):
+    shape = jax.ShapeDtypeStruct
+    count = rows.shape[0] // 2
+    half_up, half_down = up.shape[3:], down.shape[3:]
+    return pl.pallas_call(
+        reduce_large_kernel,
+        out_shape=(
+            shape(up.shape[2:], F32),
+            shape(down.shape[2:], F32),
+            shape((count, rows.shape[1]), BF),
+            shape((count, mixture.shape[1]), BF),
+            shape((gates.shape[0], count), F32),
+        ),
+        in_specs=[ANY] * 5,
+        out_specs=[VMEM, VMEM, ANY, ANY, ANY],
+        scratch_shapes=[
+            pltpu.SemaphoreType.DMA((5,)),
+            pltpu.SemaphoreType.DMA((5,)),
+            pltpu.VMEM((2, *half_up), BF),
+            pltpu.VMEM((2, *half_down), BF),
+            pltpu.VMEM((2, *half_up), BF),
+            pltpu.VMEM((2, *half_down), BF),
+            *(fold_scratch(half_up) + fold_scratch(half_down)) * 2,
+        ],
+        compiler_params=comm_params(3),
+        name="reduce_large",
+    )(up, down, rows, mixture, gates)
+
+
+def reduce_small_kernel(grads, total, z_sent, z_arrived, low, twin, middle, far, *buffers):
+    place = Place()
+    place.meet([place.to_x, place.to_y, place.to_core, place.to_twin, place.to_far])
+    fold = Fold(place, grads, *buffers)
+    fold.start()
+    fold.outward()
+    fold.inward()
+    fold.total(low)
+    first = send_to(low, twin, z_sent.at[0], z_arrived.at[0], place.to_twin)
+    first.start()
+    first.wait_recv()
+    for half in range(2):
+        add_up(middle.at[half], low.at[half], twin.at[half])
+    second = send_to(middle, far, z_sent.at[1], z_arrived.at[1], place.to_far)
+    second.start()
+    second.wait_recv()
+    for half in range(2):
+        add_up(total.at[half], middle.at[half], far.at[half])
+    fold.finish()
+    first.wait_send()
+    second.wait_send()
+
+
+def reduce_small(grads):
+    half = grads.shape[2:]
+    return pl.pallas_call(
+        reduce_small_kernel,
+        out_shape=jax.ShapeDtypeStruct(grads.shape[1:], F32),
+        in_specs=[ANY],
+        out_specs=VMEM,
+        scratch_shapes=[
+            pltpu.SemaphoreType.DMA((2,)),
+            pltpu.SemaphoreType.DMA((2,)),
+            *[pltpu.VMEM((2, *half), BF)] * 4,
+            *fold_scratch(half),
+        ],
+        compiler_params=comm_params(4),
+        name="reduce_small",
+    )(grads)
+
+
+def pack(triple, merge, router, gain_one, bias_one, gain_two, bias_two):
+    spare = LANES - router.shape[1] - 4
+    columns = [vector[:, None] for vector in (gain_one, bias_one, gain_two, bias_two)]
+    blank = jnp.zeros((router.shape[0], spare), F32)
+    return jnp.concatenate([triple, merge, router, *columns, blank], 1).astype(BF)
+
+
+def unpack(grads, width, experts):
+    rest = grads[:, 4 * width :]
+    return (
+        rest[:, experts],
+        rest[:, experts + 1],
+        grads[:, : 3 * width],
+        grads[:, 3 * width : 4 * width],
+        rest[:, experts + 2],
+        rest[:, experts + 3],
+        rest[:, :experts],
+    )
+
+
+def local_any(
     tokens,
     routes,
     cotangent,
@@ -606,21 +1044,17 @@
     owners = lax.axis_size("expert")
     capacity = 2 * TOP * real // experts
     padded = ceil_to(real, STRIP)
-    spare = LANES - experts - 4
     here = lax.axis_index("expert")
 
-    small = jnp.concatenate(
-        [
-            router_weight,
-            attend_gain[:, None],
-            attend_bias[:, None],
-            mixture_gain[:, None],
-            mixture_bias[:, None],
-            jnp.zeros((router_weight.shape[0], spare), F32),
-        ],
-        1,
-    )
-    packed = jnp.concatenate([triple_weight, merge_weight, small], 1).astype(BF)
+    packed = pack(
+        triple_weight,
+        merge_weight,
+        router_weight,
+        attend_gain,
+        attend_bias,
+        mixture_gain,
+        mixture_bias,
+    )
     packed = lax.all_gather(packed, "fsdp", axis=0, tiled=True)
     up_full = lax.all_gather(expert_up.astype(BF), "fsdp", axis=0)
     down_full = lax.all_gather(expert_down.astype(BF), "fsdp", axis=0)
@@ -629,7 +1063,7 @@
     upstream = jnp.pad(cotangent, ((0, padded - real), (0, 0)))
     route_rows = jnp.pad(routes.T, ((0, 0), (0, padded - real)), constant_values=-1)
     all_routes = lax.all_gather(route_rows, "expert", axis=0)
-    order, meta = plan_rows(all_routes, here * 2)
+    order, meta = plan_rows(all_routes, here * 2 + jnp.arange(2, dtype=jnp.int32))
     tiles = owners * padded // TILE
     all_upstream = lax.all_gather(upstream, "expert", axis=0, tiled=True)
 
@@ -638,11 +1072,10 @@
     all_gates = lax.all_gather(gates, "expert", axis=0)
     own_gates = lax.dynamic_slice_in_dim(all_gates, here * 2, 2, 1)
     own_gates = own_gates.transpose(1, 0, 2).reshape(2, tiles, TILE)
-    info = jnp.concatenate([order, own_gates, jnp.zeros((4, tiles, TILE), F32)], 0)
-    info = info.transpose(1, 0, 2)
+    info = table_of(order, own_gates)
 
     mixture, row_grad, gate_grad, up_grad, down_grad = expert_block(
-        meta, info, up_full, down_full, all_rows, all_upstream, owners * capacity
+        meta, info, up_full[None], down_full[None], all_rows, all_upstream, owners * capacity
     )
     gate_grad = gate_grad[:2].reshape(2, owners, padded).transpose(1, 0, 2)
     gate_grad = lax.all_to_all(gate_grad, "expert", 0, 0).reshape(experts, padded)
@@ -653,8 +1086,8 @@
         mixture.reshape(owners, padded, width), "expert", scatter_dimension=0, tiled=True
     )
     block_out = (hidden[:real] + mixture[0, :real].astype(F32)).astype(BF)
-    up_grad = lax.psum_scatter(up_grad, "fsdp", scatter_dimension=0, tiled=True)
-    down_grad = lax.psum_scatter(down_grad, "fsdp", scatter_dimension=0, tiled=True)
+    up_grad = lax.psum_scatter(up_grad[0], "fsdp", scatter_dimension=0, tiled=True)
+    down_grad = lax.psum_scatter(down_grad[0], "fsdp", scatter_dimension=0, tiled=True)
 
     token_grad, grads = retreat(
         token_rows,
@@ -665,31 +1098,111 @@
         mixed,
         probs,
         gate_grad,
-        row_grad,
+        tuple(row_grad),
         packed,
         real,
     )
     grads = lax.psum_scatter(grads, "fsdp", scatter_dimension=0, tiled=True)
     grads = lax.psum(grads, "expert").astype(F32)
-    rest = grads[:, 4 * width :]
-    return (
-        block_out,
-        token_grad,
-        rest[:, experts],
-        rest[:, experts + 1],
-        grads[:, : 3 * width],
-        grads[:, 3 * width : 4 * width],
-        rest[:, experts + 2],
-        rest[:, experts + 3],
-        rest[:, :experts],
+    return (block_out, token_grad) + unpack(grads, width, experts) + (
         up_grad[0].astype(F32),
         down_grad[0].astype(F32),
     )
 
 
+def swapped(pair, flag, axis):
+    return jnp.where(flag, jnp.flip(pair, axis), pair)
+
+
+def local_square(
+    tokens,
+    routes,
+    cotangent,
+    attend_gain,
+    attend_bias,
+    triple_weight,
+    merge_weight,
+    mixture_gain,
+    mixture_bias,
+    router_weight,
+    expert_up,
+    expert_down,
+):
+    real, width = tokens.shape
+    experts = router_weight.shape[1]
+    capacity = 2 * TOP * real // experts
+    padded = ceil_to(real, LANES)
+    tiles = 2 * padded // TILE
+    z = lax.axis_index("expert")
+    odd, upper = z % 2 == 1, z >= 2
+
+    shard = pack(
+        triple_weight,
+        merge_weight,
+        router_weight,
+        attend_gain,
+        attend_bias,
+        mixture_gain,
+        mixture_bias,
+    )
+    packed = gather_small(shard.reshape(2, shard.shape[0] // 2, shard.shape[1]))
+    packed = packed.reshape(8 * shard.shape[0], shard.shape[1])
+
+    token_rows = jnp.pad(tokens, ((0, padded - real), (0, 0)))
+    upstream = jnp.pad(cotangent, ((0, padded - real), (0, 0)))
+    route_rows = jnp.pad(routes.T, ((0, 0), (0, padded - real)), constant_values=-1)
+    far_routes = lax.ppermute(route_rows, "expert", [(i, (i + 2) % 4) for i in range(4)])
+    mine = jnp.arange(2, dtype=jnp.int32)
+    mine = jnp.concatenate([2 * z + mine, 2 * (z + 1 - 2 * (z % 2)) + mine])
+    order, meta = plan_rows(jnp.stack([route_rows, far_routes]), mine)
+
+    qkv, mixed, hidden, normed, probs, gates = attend(token_rows, route_rows, packed, experts)
+    up_full, down_full, all_rows, all_upstream, all_gates = gather_large(
+        expert_up.astype(BF), expert_down.astype(BF), normed, upstream, gates
+    )
+    own_gates = all_gates.reshape(2, 2, 2, 2, padded)
+    own_gates = jnp.where(upper, own_gates[:, 1], own_gates[:, 0])
+    own_gates = swapped(own_gates, odd, 1).transpose(1, 2, 0, 3)
+    info = table_of(order, own_gates.reshape(4, tiles, TILE))
+
+    mixture, row_grad, gate_grad, up_grad, down_grad = expert_block(
+        meta,
+        info,
+        up_full,
+        down_full,
+        all_rows.reshape(2 * padded, width),
+        all_upstream.reshape(2 * padded, width),
+        2 * capacity,
+    )
+    up_grad, down_grad, row_far, mixture_far, gate_far = reduce_large(
+        up_grad, down_grad, row_grad, mixture, gate_grad
+    )
+    gate_grad = jnp.stack([gate_grad[:4, :padded], gate_far[:4]]).reshape(2, 2, 2, padded)
+    gate_grad = swapped(swapped(gate_grad, odd, 1), upper, 0).reshape(experts, padded)
+    total = hidden[:real] + mixture[:real].astype(F32) + mixture_far[:real].astype(F32)
+    block_out = total.astype(BF)
+    token_grad, grads = retreat(
+        token_rows,
+        upstream,
+        hidden,
+        normed,
+        qkv,
+        mixed,
+        probs,
+        gate_grad,
+        (row_grad, row_far),
+        packed,
+        real,
+    )
+    grads = reduce_small(grads.reshape(8, 2, shard.shape[0] // 2, shard.shape[1]))
+    grads = grads.reshape(shard.shape)
+    return (block_out, token_grad) + unpack(grads, width, experts) + (up_grad, down_grad)
+
+
 def solution(mesh):
+    square = dict(mesh.shape) == {"expert": 4, "fsdp": 8}
     return jax.shard_map(
-        local,
+        local_square if square else local_any,
         mesh=mesh,
         in_specs=(
             P(("expert", "fsdp"), None),

time: 715 us -> 451 us (0.63); the launches traced: 706 us -> 451 us
  waiting for transfers between devices: 466 us -> 0.01 us
  Pallas kernels: 144 us -> 416 us
  blocking collectives: 52 us -> 0 us
  between operations: 14 us -> 0.86 us
    pallas_call x0 -> x4, Pallas kernels: none -> 246 us  [the longest x1 102 us: reduce_large(): pl.pallas_call(reduce_large_kernel, out_shape=(shape(up.shape[2:], F32),...]
    reduce_scatter x5 -> x0, waiting for transfers between devices: 235 us -> none  [the longest x1 66.6 us: local(): lax.psum_scatter(mixture.reshape(owners, padded, width), 'expert', scatte...]
    all_gather x5 -> x0, waiting for transfers between devices: 193 us -> none  [the longest x1 69.2 us: local(): all_rows = lax.all_gather(normed, 'expert', axis=0, tiled=True)]
    psum x1 -> x0, waiting for transfers between devices: 36 us -> none  [local(): grads = lax.psum(grads, 'expert').astype(F32)]
    all_gather x2 -> x0, blocking collectives: 28.6 us -> none  [the longest x1 14.8 us: local(): all_gates = lax.all_gather(gates, 'expert', axis=0)]
    pallas_call x1, Pallas kernels: 93.4 us -> 118 us  [expert_block(): pl.pallas_call(partial(expert_kernel, tiles, parts, room), grid_spec=pltp...]
    all_to_all x1 -> x0, blocking collectives: 23.4 us -> none  [local(): lax.all_to_all(gate_grad, 'expert', 0, 0).reshape(experts, padded)]
  transfers between devices with their start and end apart: 11 -> 1, of which waited for: 11 -> 0; matrix products, arithmetic and copies ran while one was open for 2% -> 3% of each run, Pallas kernels for 7% -> 27%
where the time goes in v2:
time: 451 us
  Pallas kernels  416 us (92%)
  local copies, waits for them, and re-layouts  17.2 us (4%)
  other arithmetic  11.9 us (3%)
    pallas_call x1, Pallas kernels, expert_block(): pl.pallas_call(partial(expert_kernel, tiles, parts, room), grid_spec=pltp...  118 us
    pallas_call x1, Pallas kernels, reduce_large(): pl.pallas_call(reduce_large_kernel, out_shape=(shape(up.shape[2:], F32),...  102 us
    pallas_call x1, Pallas kernels, gather_large(): pl.pallas_call(gather_large_kernel, out_shape=(shape((2, 8, *up.shape), B...  86.5 us
    pallas_call x1, Pallas kernels, reduce_small(): pl.pallas_call(reduce_small_kernel, out_shape=jax.ShapeDtypeStruct(grads....  39.5 us
    pallas_call x1, Pallas kernels, retreat(): pl.pallas_call(partial(retreat_kernel, experts), out_shape=(shape((real,...  33.2 us
    pallas_call x1, Pallas kernels, attend(): pl.pallas_call(partial(attend_kernel, experts), out_shape=(shape((rows, 3...  19.1 us
    pallas_call x1, Pallas kernels, gather_small(): pl.pallas_call(gather_small_kernel, out_shape=jax.ShapeDtypeStruct((8, *s...  17.3 us
  transfers between devices with their start and end apart: 1, of which 0 were waited for; matrix products, arithmetic and copies ran while one was open for 3% of the time, Pallas kernels for 27%

profile of v2, /device:TPU:0, one launch (start us, length us, event | category | flops | bytes accessed | tf_op | source)
XLA Modules:
  0.0 450.6 jit_solution(1180814187632748445)
XLA Ops:
  0.7 0.8 pad_bitcast_fusion
  1.4 4.1 collective-permute-start
  9.6 0.9 convert.31
  10.6 1.1 convert.30
  11.7 2.1 convert_element_type.30.up
  13.8 0.9 convert_element_type.31.down
  14.6 1.0 pad.11.tokens
  15.6 1.0 pad.13.upstream.cotangent
  16.6 0.8 concatenate.33.shard
  17.4 17.3 %gather_small.1 = bf16[8,2,32,2176]{3,2,1,0:T(8,128)(2,1)} custom-call(bf16[2,32,2176]{2,1,0:T(8,128)(2,1)} %concatenate.33.shard), custom_call_target="tpu_custom_call" | custom-call | tf_op jit(solution)/shard_map/gather_small/pallas_call | solution.py:801
  34.8 19.1 %attend.1 = (bf16[896,1536]{1,0:T(8,128)(2,1)}, bf16[896,512]{1,0:T(8,128)(2,1)}, f32[896,512]{1,0:T(8,128)}, bf16[896,512]{1,0:T(8,128)(2,1)}, f32[8,896]{1,0:T(8,128)}, /*index=5*/f32[8,896]{1,0:T(8,128)}) custom-call(bf16[896,512]{1,0:T(8,128)(2,1)} %pad.11.tokens, s32[2,896]{1,0:T(2,128)} %copy-done.7, bf16[512,2176]{1,0:T(8,128)(2,1)} %bitcast.24), custom_call_target="tpu_custom_call" | custom-call | tf_op jit(solution)/shard_map/attend/pallas_call | solution.py:166
  53.9 86.5 %gather_large.1 = (bf16[2,8,2,64,2048]{4,3,2,1,0:T(8,128)(2,1)}, bf16[2,8,2,256,512]{4,3,2,1,0:T(8,128)(2,1)}, bf16[2,896,512]{2,1,0:T(8,128)(2,1)}, bf16[2,896,512]{2,1,0:T(8,128)(2,1)}, f32[2,8,896]{2,1,0:T(8,128)}) custom-call(bf16[2,64,2048]{2,1,0:T(8,128)(2,1)} %convert_element_type.30.up, bf16[2,256,512]{2,1,0:T(8,128)(2,1)} %convert_element_type.31.down, ...), custom_call_target="tpu_custom_call" | custom-call | tf_op jit(solution)/shard_map/gather_large/pallas_call | solution.py:862
  140.4 0.8 copy.66
  143.6 118.3 %experts.1 = (bf16[1792,512]{1,0:T(8,128)(2,1)}, bf16[1792,512]{1,0:T(8,128)(2,1)}, f32[8,1792]{1,0:T(8,128)}, bf16[2,8,2,64,2048]{4,3,2,1,0:T(8,128)(2,1)}, bf16[2,8,2,256,512]{4,3,2,1,0:T(8,128)(2,1)}) custom-call(s32[32]{0:T(128)} %convert_element_type.29.meta, f32[7,8,256]{2,1,0:T(8,128)} %maximum_bitcast_fusion.info, ...), custom_call_target="tpu_custom_call" | custom-call | tf_op jit(solution)/shard_map/experts/pallas_call | solution.py:368
  262.7 102.2 %reduce_large.1 = (f32[2,64,2048]{2,1,0:T(8,128)}, f32[2,256,512]{2,1,0:T(8,128)}, bf16[896,512]{1,0:T(8,128)(2,1)}, bf16[896,512]{1,0:T(8,128)(2,1)}, f32[8,896]{1,0:T(8,128)}) custom-call(bf16[2,8,2,64,2048]{4,3,2,1,0:T(8,128)(2,1)} %get-tuple-element.43.up, bf16[2,8,2,256,512]{4,3,2,1,0:T(8,128)(2,1)} %get-tuple-element.44.down, ...), custom_call_target="tpu_custom_call" | custom-call | tf_op jit(solution)/shard_map/reduce_large/pallas_call | solution.py:942
  366.7 33.2 %retreat.1 = (f32[788,512]{1,0:T(8,128)}, bf16[512,2176]{1,0:T(8,128)(2,1)}) custom-call(bf16[896,512]{1,0:T(8,128)(2,1)} %pad.11.tokens, bf16[896,512]{1,0:T(8,128)(2,1)} %pad.13.upstream.cotangent, f32[896,512]{1,0:T(8,128)} %get-tuple-element.34.hidden, bf16[896,512]{1,0:T(8,128)(2,1)} %get-tuple-element.35.rows.normed, ...), custom_call_target="tpu_custom_call" | custom-call | tf_op jit(solution)/shard_map/retreat/pallas_call | solution.py:552
  400.0 39.5 %reduce_small.1 = f32[2,32,2176]{2,1,0:T(8,128)} custom-call(bf16[8,2,32,2176]{3,2,1,0:T(8,128)(2,1)} %bitcast.30), custom_call_target="tpu_custom_call" | custom-call | tf_op jit(solution)/shard_map/reduce_small/pallas_call | solution.py:992
  439.5 1.9 slice_reduce_fusion
  441.4 0.8 slice.89
  442.2 1.6 slice.86
  443.8 1.8 slice.85
  445.5 2.5 add_convert_fusion
  448.6 1.0 copy.77
  449.6 1.0 copy.78
  (61 shorter events, 9.5 us)
Async XLA Ops:
  0.6 13.1 %copy-start.1 = (f32[2,256,512]{2,1,0:T(8,128)S(1)}, f32[2,256,512]{2,1,0:T(8,128)}, u32[]{:S(2)}) copy-start(f32[2,256,512]{2,1,0:T(8,128)} %param.23) | copy-start | bytes 3145732
  1.4 13.2 %copy-start.7 = (s32[2,896]{1,0:T(2,128)}, s32[2,896]{1,0:T(2,128)S(1)}, u32[]{:S(2)}) copy-start(s32[2,896]{1,0:T(2,128)S(1)} %get-tuple-element.64.routes) | copy-start | bytes 21508
  1.4 140.0 %collective-permute-start = (s32[2,896]{1,0:T(2,128)S(1)}, s32[2,896]{1,0:T(2,128)S(1)}, u32[]{:S(2)}, u32[]{:S(2)}) collective-permute-start(s32[2,896]{1,0:T(2,128)S(1)} %get-tuple-element.64.routes), channel_id=1, source_target_pairs={{0,16},{8,24},{16,0},{24,8},{1,17},{9,25},{17,1},{25,9},{2,18},{10... | collective-permute-start | bytes 21512 | tf_op jit(solution)/shard_map/ppermute | solution.py:1154
  10.6 4.1 copy-start.4
  13.8 1.9 copy-start.5
  399.9 45.6 %copy-start = (f32[896,512]{1,0:T(8,128)S(1)}, f32[896,512]{1,0:T(8,128)}, u32[]{:S(2)}) copy-start(f32[896,512]{1,0:T(8,128)} %get-tuple-element.34.hidden) | copy-start | bytes 5505028
  399.9 45.6 %copy-start.6 = (bf16[896,512]{1,0:T(8,128)(2,1)S(1)}, bf16[896,512]{1,0:T(8,128)(2,1)}, u32[]{:S(2)}) copy-start(bf16[896,512]{1,0:T(8,128)(2,1)} %get-tuple-element.47) | copy-start | bytes 2752516
  445.5 3.1 copy-start.3
  448.0 1.6 copy-start.2

commit v3 on v2

--- a/solution.py
+++ b/solution.py
@@ -67,6 +67,11 @@
     return center * inverse, inverse
 
 
+def weight(packed, columns):
+    part = packed[:, :, :, columns]
+    return part.reshape(-1, part.shape[-1])
+
+
 def window(image):
     start = image * SEQ // 16 * 16
     offset = image * SEQ - start
@@ -82,7 +87,7 @@
     rows, width = tokens.shape
     images = rows // SEQ
     half = rows // 2
-    small[...] = packed[:, 4 * width :].astype(F32).T
+    small[...] = weight(packed, slice(4 * width, None)).astype(F32).T
     gain_one, bias_one = small[experts : experts + 1, :], small[experts + 1 : experts + 2, :]
     gain_two, bias_two = small[experts + 2 : experts + 3, :], small[experts + 3 : experts + 4, :]
 
@@ -99,7 +104,7 @@
 
         def project(j, carry):
             part = pl.ds(pl.multiple_of(j * half, 16), half)
-            qkv[part, columns] = dot_nn(first[part, :], packed[:, columns]).astype(BF)
+            qkv[part, columns] = dot_nn(first[part, :], weight(packed, columns)).astype(BF)
             return carry
 
         lax.fori_loop(0, 2, project, 0)
@@ -136,7 +141,7 @@
 
     def merge(j, carry):
         part = pl.ds(pl.multiple_of(j * half, 16), half)
-        hidden[part, :] = dot_nn(mixed[part, :], packed[:, 3 * width : 4 * width])
+        hidden[part, :] = dot_nn(mixed[part, :], weight(packed, slice(3 * width, 4 * width)))
         return carry
 
     lax.fori_loop(0, 2, merge, 0)
@@ -422,7 +427,7 @@
     real = token_grad.shape[0]
     images = rows // SEQ
     half = rows // 2
-    small[...] = packed[:, 4 * width :].astype(F32).T
+    small[...] = weight(packed, slice(4 * width, None)).astype(F32).T
     gain_one, bias_one = small[experts : experts + 1, :], small[experts + 1 : experts + 2, :]
     gain_two = small[experts + 2 : experts + 3, :]
     sums[...] = jnp.zeros(sums.shape, F32)
@@ -466,7 +471,7 @@
 
     def project(j, carry):
         part = pl.ds(pl.multiple_of(j * half, 16), half)
-        branch_grad[part, :] = dot_nt(branch_grad[part, :], packed[:, merge]).astype(BF)
+        branch_grad[part, :] = dot_nt(branch_grad[part, :], weight(packed, merge)).astype(BF)
         return carry
 
     lax.fori_loop(0, 2, project, 0)
@@ -517,7 +522,7 @@
 
     def finish(start, size):
         part = pl.ds(start, size)
-        change = dot_nt(joined_grad[part, :], packed[:, : 3 * width])
+        change = dot_nt(joined_grad[part, :], weight(packed, slice(0, 3 * width)))
         unit, inverse = normalize(tokens[part, :].astype(F32))
         tail = change * unit
         totals[2] += jnp.sum(tail.reshape(size // 8, 8, width), 0)
@@ -551,7 +556,7 @@
     shape = jax.ShapeDtypeStruct
     return pl.pallas_call(
         partial(retreat_kernel, experts),
-        out_shape=(shape((real, width), F32), shape(packed.shape, BF)),
+        out_shape=(shape((real, width), F32), shape((width, packed.shape[-1]), BF)),
         in_specs=[pl.BlockSpec(memory_space=pltpu.VMEM)] * (9 + len(returned)),
         out_specs=[pl.BlockSpec(memory_space=pltpu.VMEM)] * 2,
         scratch_shapes=[
@@ -784,62 +789,103 @@
     )
 
 
-def gather_small_kernel(shard, full, sent, arrived, kept):
-    place = Place()
-    place.meet([place.to_x, place.to_y, place.to_core])
-    keep = pltpu.make_async_copy(shard, full.at[place.me], kept)
-    keep.start()
-    spread = Spread(place, shard, full, sent, arrived)
-    spread.start()
-    spread.pass_on()
-    spread.share()
-    spread.finish()
-    keep.wait()
-
-
-def gather_small(shard):
-    return pl.pallas_call(
-        gather_small_kernel,
-        out_shape=jax.ShapeDtypeStruct((8, *shard.shape), BF),
-        in_specs=[VMEM],
-        out_specs=VMEM,
-        scratch_shapes=[
-            pltpu.SemaphoreType.DMA((PATHS,)),
-            pltpu.SemaphoreType.DMA((PATHS,)),
-            pltpu.SemaphoreType.DMA(()),
-        ],
-        compiler_params=comm_params(1),
-        name="gather_small",
-    )(shard)
-
-
-def gather_large_kernel(
-    up, down, rows, upstream, gates, up_full, down_full, rows_full, upstream_full, gates_full, *sems
+def front_kernel(
+    experts,
+    tokens,
+    cotangent,
+    routes,
+    triple,
+    merge,
+    rest,
+    up_shard,
+    down_shard,
+    token_rows,
+    upstream,
+    packed,
+    qkv,
+    mixed,
+    hidden,
+    normed,
+    probs,
+    up_full,
+    down_full,
+    rows_full,
+    upstream_full,
+    gates_full,
+    shard,
+    up,
+    down,
+    gates,
+    first,
+    small,
+    sent,
+    arrived,
+    z_sent,
+    z_arrived,
+    kept,
 ):
-    sent, arrived, z_sent, z_arrived, kept = sems
+    real, width = tokens.shape
+    count = token_rows.shape[0]
+    crossing = ceil_to(real, 16)
     place = Place()
     place.meet([place.to_x, place.to_y, place.to_core, place.to_twin, place.to_far])
-    twins, near, far, keeps = [], [], [], []
+    for half in range(2):
+        part = slice(half * triple.shape[0] // 2, (half + 1) * triple.shape[0] // 2)
+        shard[half, :, : 3 * width] = triple[part, :].astype(BF)
+        shard[half, :, 3 * width : 4 * width] = merge[part, :].astype(BF)
+        shard[half, :, 4 * width :] = rest[part, :].astype(BF)
+    spread = Spread(place, shard, packed, sent.at[0], arrived.at[0])
+    spread.start()
+    keeps = [pltpu.make_async_copy(shard, packed.at[place.me], kept.at[0])]
+    keeps[0].start()
+
+    for half in range(2):
+        add_up(up.at[half], up_shard.at[half])
+        add_up(down.at[half], down_shard.at[half])
+    twins, near, far = [], [], []
     for i, (source, full) in enumerate(((up, up_full), (down, down_full))):
         spot = full.at[1, place.me]
         twins.append(send_to(source, spot, z_sent.at[i], z_arrived.at[i], place.to_twin))
-        near.append(Spread(place, source, full.at[0], sent.at[i], arrived.at[i]))
-        far.append(Spread(place, spot, full.at[1], sent.at[2 + i], arrived.at[2 + i]))
-        keeps.append(pltpu.make_async_copy(source, full.at[0, place.me], kept.at[i]))
+        near.append(Spread(place, source, full.at[0], sent.at[1 + i], arrived.at[1 + i]))
+        far.append(Spread(place, spot, full.at[1], sent.at[3 + i], arrived.at[3 + i]))
+        keeps.append(pltpu.make_async_copy(source, full.at[0, place.me], kept.at[1 + i]))
     for copy in twins:
         copy.start()
-    for spread in near:
-        spread.start()
-    pairs = ((rows, rows_full), (upstream, upstream_full), (gates, gates_full))
+    pad_rows(cotangent, upstream)
     across = []
-    for i, (source, full) in enumerate(pairs):
-        at = 2 + i
-        across.append(
-            send_to(source, full.at[1], z_sent.at[at], z_arrived.at[at], place.to_far)
-        )
-        keeps.append(pltpu.make_async_copy(source, full.at[0], kept.at[at]))
-    for copy in across + keeps:
+
+    def cross(source, full, whole):
+        at = 2 + len(across)
+        count = source.shape[0] if whole else crossing
+        part = source.at[pl.ds(0, count)]
+        target = full.at[1, pl.ds(0, count)]
+        across.append(send_to(part, target, z_sent.at[at], z_arrived.at[at], place.to_far))
+        across[-1].start()
+        keeps.append(pltpu.make_async_copy(source, full.at[0], kept.at[len(keeps)]))
+        keeps[-1].start()
+        if not whole:
+            left = pl.ds(crossing, source.shape[0] - crossing)
+            copy = pltpu.make_async_copy(source.at[left], full.at[1, left], kept.at[len(keeps)])
+            copy.start()
+            keeps.append(copy)
+
+    cross_first = len(keeps)
+    for copy in keeps[1:cross_first]:
         copy.start()
+    cross(upstream, upstream_full, False)
+    pad_rows(tokens, token_rows)
+    spread.pass_on()
+    for other in near:
+        other.start()
+    spread.share()
+    keeps[0].wait()
+    spread.finish()
+
+    attend_kernel(
+        experts, token_rows, routes, packed, qkv, mixed, hidden, normed, probs, gates, first, small
+    )
+    cross(normed, rows_full, False)
+    cross(gates, gates_full, True)
     for i in range(2):
         near[i].pass_on()
         twins[i].wait_recv()
@@ -849,37 +895,71 @@
         far[i].pass_on()
     for i in range(2):
         far[i].share()
-    for spread in near + far:
-        spread.finish()
+    for other in near + far:
+        other.finish()
     for copy in twins:
         copy.wait_send()
-    for copy in across + keeps:
+    for copy in across + keeps[1:]:
         copy.wait()
 
 
-def gather_large(up, down, rows, upstream, gates):
+def pad_rows(source, target):
+    real, width = source.shape
+    whole = real // STRIP * STRIP
+
+    def body(j, carry):
+        part = pl.ds(pl.multiple_of(j * STRIP, STRIP), STRIP)
+        target[part, :] = source[part, :]
+        return carry
+
+    lax.fori_loop(0, whole // STRIP, body, 0)
+    if whole < target.shape[0]:
+        target[whole:, :] = jnp.zeros((target.shape[0] - whole, width), target.dtype)
+    if whole < real:
+        target[whole:real, :] = source[whole:real, :]
+
+
+def front(tokens, cotangent, routes, triple, merge, rest, up, down, experts):
+    real, width = tokens.shape
+    rows = routes.shape[1]
     shape = jax.ShapeDtypeStruct
+    columns = 4 * width + LANES
+    half = triple.shape[0] // 2
     return pl.pallas_call(
-        gather_large_kernel,
+        partial(front_kernel, experts),
         out_shape=(
+            shape((rows, width), BF),
+            shape((rows, width), BF),
+            shape((8, 2, half, columns), BF),
+            shape((rows, 3 * width), BF),
+            shape((rows, width), BF),
+            shape((rows, width), F32),
+            shape((rows, width), BF),
+            shape((experts, rows), F32),
             shape((2, 8, *up.shape), BF),
             shape((2, 8, *down.shape), BF),
-            shape((2, *rows.shape), BF),
-            shape((2, *upstream.shape), BF),
-            shape((2, *gates.shape), F32),
+            shape((2, rows, width), BF),
+            shape((2, rows, width), BF),
+            shape((2, experts, rows), F32),
         ),
-        in_specs=[VMEM] * 5,
-        out_specs=[ANY] * 5,
+        in_specs=[VMEM] * 8,
+        out_specs=[VMEM] * 8 + [ANY] * 5,
         scratch_shapes=[
-            pltpu.SemaphoreType.DMA((4, PATHS)),
-            pltpu.SemaphoreType.DMA((4, PATHS)),
+            pltpu.VMEM((2, half, columns), BF),
+            pltpu.VMEM(up.shape, BF),
+            pltpu.VMEM(down.shape, BF),
+            pltpu.VMEM((experts, rows), F32),
+            pltpu.VMEM((rows, width), BF),
+            pltpu.VMEM((LANES, width), F32),
+            pltpu.SemaphoreType.DMA((5, PATHS)),
+            pltpu.SemaphoreType.DMA((5, PATHS)),
             pltpu.SemaphoreType.DMA((5,)),
             pltpu.SemaphoreType.DMA((5,)),
-            pltpu.SemaphoreType.DMA((5,)),
+            pltpu.SemaphoreType.DMA((8,)),
         ],
-        compiler_params=comm_params(2),
-        name="gather_large",
-    )(up, down, rows, upstream, gates)
+        compiler_params=comm_params(1),
+        name="front",
+    )(tokens, cotangent, routes, triple, merge, rest, up, down)
 
 
 def reduce_large_kernel(
@@ -1006,10 +1086,16 @@
 
 
 def pack(triple, merge, router, gain_one, bias_one, gain_two, bias_two):
-    spare = LANES - router.shape[1] - 4
-    columns = [vector[:, None] for vector in (gain_one, bias_one, gain_two, bias_two)]
-    blank = jnp.zeros((router.shape[0], spare), F32)
-    return jnp.concatenate([triple, merge, router, *columns, blank], 1).astype(BF)
+    rest = pack_small(router, gain_one, bias_one, gain_two, bias_two)
+    return jnp.concatenate([triple, merge, rest], 1).astype(BF)
+
+
+def pack_small(router, *vectors):
+    total = jnp.pad(router, ((0, 0), (0, LANES - router.shape[1])))
+    for i, vector in enumerate(vectors):
+        at = router.shape[1] + i
+        total += jnp.pad(vector[:, None], ((0, 0), (at, LANES - at - 1)))
+    return total
 
 
 def unpack(grads, width, experts):
@@ -1056,6 +1142,7 @@
         mixture_bias,
     )
     packed = lax.all_gather(packed, "fsdp", axis=0, tiled=True)
+    packed = packed.reshape(-1, 2, STRIP // 2, packed.shape[1])
     up_full = lax.all_gather(expert_up.astype(BF), "fsdp", axis=0)
     down_full = lax.all_gather(expert_down.astype(BF), "fsdp", axis=0)
 
@@ -1136,29 +1223,36 @@
     z = lax.axis_index("expert")
     odd, upper = z % 2 == 1, z >= 2
 
-    shard = pack(
-        triple_weight,
-        merge_weight,
-        router_weight,
-        attend_gain,
-        attend_bias,
-        mixture_gain,
-        mixture_bias,
-    )
-    packed = gather_small(shard.reshape(2, shard.shape[0] // 2, shard.shape[1]))
-    packed = packed.reshape(8 * shard.shape[0], shard.shape[1])
-
-    token_rows = jnp.pad(tokens, ((0, padded - real), (0, 0)))
-    upstream = jnp.pad(cotangent, ((0, padded - real), (0, 0)))
     route_rows = jnp.pad(routes.T, ((0, 0), (0, padded - real)), constant_values=-1)
     far_routes = lax.ppermute(route_rows, "expert", [(i, (i + 2) % 4) for i in range(4)])
     mine = jnp.arange(2, dtype=jnp.int32)
     mine = jnp.concatenate([2 * z + mine, 2 * (z + 1 - 2 * (z % 2)) + mine])
     order, meta = plan_rows(jnp.stack([route_rows, far_routes]), mine)
-
-    qkv, mixed, hidden, normed, probs, gates = attend(token_rows, route_rows, packed, experts)
-    up_full, down_full, all_rows, all_upstream, all_gates = gather_large(
-        expert_up.astype(BF), expert_down.astype(BF), normed, upstream, gates
+    rest = pack_small(router_weight, attend_gain, attend_bias, mixture_gain, mixture_bias)
+    (
+        token_rows,
+        upstream,
+        packed,
+        qkv,
+        mixed,
+        hidden,
+        normed,
+        probs,
+        up_full,
+        down_full,
+        all_rows,
+        all_upstream,
+        all_gates,
+    ) = front(
+        tokens,
+        cotangent,
+        route_rows,
+        triple_weight,
+        merge_weight,
+        rest,
+        expert_up,
+        expert_down,
+        experts,
     )
     own_gates = all_gates.reshape(2, 2, 2, 2, padded)
     own_gates = jnp.where(upper, own_gates[:, 1], own_gates[:, 0])
@@ -1194,8 +1288,7 @@
         packed,
         real,
     )
-    grads = reduce_small(grads.reshape(8, 2, shard.shape[0] // 2, shard.shape[1]))
-    grads = grads.reshape(shard.shape)
+    grads = reduce_small(grads.reshape(packed.shape)).reshape(-1, packed.shape[-1])
     return (block_out, token_grad) + unpack(grads, width, experts) + (up_grad, down_grad)
 
 

time: 451 us -> 412 us (0.914)
  Pallas kernels: 416 us -> 386 us
  other arithmetic: 11.9 us -> 4.31 us
    pallas_call x3 -> x1, Pallas kernels: 123 us -> 89.9 us  [front(): pl.pallas_call(partial(front_kernel, experts), out_shape=(shape((rows, wi...]
    pallas_call x1, Pallas kernels: 118 us -> 111 us  [expert_block(): pl.pallas_call(partial(expert_kernel, tiles, parts, room), grid_spec=pltp...]
    pallas_call x1, Pallas kernels: 102 us -> 108 us  [reduce_large(): pl.pallas_call(reduce_large_kernel, out_shape=(shape(up.shape[2:], F32),...]
    another operation x7 -> x0, other arithmetic: 5.33 us -> none
  transfers between devices with their start and end apart: 1 -> 1, of which waited for: 0 -> 0; matrix products, arithmetic and copies ran while one was open for 3% -> 1% of each run, Pallas kernels for 27% -> 22%
where the time goes in v3:
time: 412 us; the launch traced here: 413 us
  Pallas kernels  386 us (94%)
  local copies, waits for them, and re-layouts  17.4 us (4%)
  other arithmetic  4.31 us (1%)
  starting transfers between devices  4.12 us (1%)
    pallas_call x1, Pallas kernels, expert_block(): pl.pallas_call(partial(expert_kernel, tiles, parts, room), grid_spec=pltp...  111 us
    pallas_call x1, Pallas kernels, reduce_large(): pl.pallas_call(reduce_large_kernel, out_shape=(shape(up.shape[2:], F32),...  108 us
    pallas_call x1, Pallas kernels, front(): pl.pallas_call(partial(front_kernel, experts), out_shape=(shape((rows, wi...  89.9 us
    pallas_call x1, Pallas kernels, reduce_small(): pl.pallas_call(reduce_small_kernel, out_shape=jax.ShapeDtypeStruct(grads....  43.1 us
    pallas_call x1, Pallas kernels, retreat(): pl.pallas_call(partial(retreat_kernel, experts), out_shape=(shape((real,...  33.2 us
  transfers between devices with their start and end apart: 1, of which 0 were waited for; matrix products, arithmetic and copies ran while one was open for 1% of the time, Pallas kernels for 22%

profile of v3, /device:TPU:0, one launch (start us, length us, event | category | flops | bytes accessed | tf_op | source)
XLA Modules:
  0.0 412.6 jit_solution(2438575936577710490)
XLA Ops:
  0.6 0.7 pad_bitcast_fusion
  1.3 4.1 collective-permute-start
  5.5 0.7 copy.50
  6.2 0.7 copy.51
  7.0 0.7 copy.52
  7.7 0.7 copy.53
  8.5 0.8 copy.49
  9.2 0.7 pad_add_fusion.rest
  10.0 89.9 %front.1 = (bf16[896,512]{1,0:T(8,128)(2,1)}, bf16[896,512]{1,0:T(8,128)(2,1)}, bf16[8,2,32,2176]{3,2,1,0:T(8,128)(2,1)}, bf16[896,1536]{1,0:T(8,128)(2,1)}, bf1...) custom-call(bf16[788,512]{1,0:T(8,128)(2,1)} %tokens.1, ...), custom_call_target="tpu_custom_call" | custom-call | tf_op jit(solution)/shard_map/front/pallas_call | solution.py:928
  99.9 0.8 copy.66
  103.0 111.3 %experts.1 = (bf16[1792,512]{1,0:T(8,128)(2,1)}, bf16[1792,512]{1,0:T(8,128)(2,1)}, f32[8,1792]{1,0:T(8,128)}, bf16[2,8,2,64,2048]{4,3,2,1,0:T(8,128)(2,1)}, bf16[2,8,2,256,512]{4,3,2,1,0:T(8,128)(2,1)}) custom-call(s32[32]{0:T(128)} %convert_element_type.28.meta, f32[7,8,256]{2,1,0:T(8,128)} %maximum_bitcast_fusion.info, ...), custom_call_target="tpu_custom_call" | custom-call | tf_op jit(solution)/shard_map/experts/pallas_call | solution.py:373
  214.3 0.8 slice.69
  215.1 108.3 %reduce_large.1 = (f32[2,64,2048]{2,1,0:T(8,128)}, f32[2,256,512]{2,1,0:T(8,128)}, bf16[896,512]{1,0:T(8,128)(2,1)}, bf16[896,512]{1,0:T(8,128)(2,1)}, f32[8,896]{1,0:T(8,128)}) custom-call(bf16[2,8,2,64,2048]{4,3,2,1,0:T(8,128)(2,1)} %get-tuple-element.43.up, bf16[2,8,2,256,512]{4,3,2,1,0:T(8,128)(2,1)} %get-tuple-element.44.down, ...), custom_call_target="tpu_custom_call" | custom-call | tf_op jit(solution)/shard_map/reduce_large/pallas_call | solution.py:1022
  323.4 0.8 slice.70
  325.2 33.2 %retreat.1 = (f32[788,512]{1,0:T(8,128)}, bf16[512,2176]{1,0:T(8,128)(2,1)}) custom-call(bf16[896,512]{1,0:T(8,128)(2,1)} %get-tuple-element.48.tokens, bf16[896,512]{1,0:T(8,128)(2,1)} %get-tuple-element.49.cotangent, f32[896,512]{1,0:T(8,128)} %get-tuple-element.36.hidden, bf16[896,512]{1,0:T(8,128)(2,1)} %get-tuple-element.50.normed, ...), custom_call_target="tpu_custom_call" | custom-call | tf_op jit(solution)/shard_map/retreat/pallas_call | solution.py:557
  358.4 43.1 %reduce_small.1 = f32[2,32,2176]{2,1,0:T(8,128)} custom-call(bf16[8,2,32,2176]{3,2,1,0:T(8,128)(2,1)} %bitcast.28), custom_call_target="tpu_custom_call" | custom-call | tf_op jit(solution)/shard_map/reduce_small/pallas_call | solution.py:1072
  401.5 1.9 slice_reduce_fusion
  403.4 0.8 slice.89
  404.2 1.6 slice.86
  405.7 1.8 slice.85
  407.5 2.5 add_convert_fusion
  410.0 0.7 copy.67
  410.6 1.0 copy.77
  411.6 1.0 copy.78
  (41 shorter events, 3.3 us)
Async XLA Ops:
  1.3 8.6 %copy-start.4 = (s32[2,896]{1,0:T(2,128)}, s32[2,896]{1,0:T(2,128)S(1)}, u32[]{:S(2)}) copy-start(s32[2,896]{1,0:T(2,128)S(1)} %get-tuple-element.68.routes) | copy-start | bytes 21508
  1.3 99.6 %collective-permute-start = (s32[2,896]{1,0:T(2,128)S(1)}, s32[2,896]{1,0:T(2,128)S(1)}, u32[]{:S(2)}, u32[]{:S(2)}) collective-permute-start(s32[2,896]{1,0:T(2,128)S(1)} %get-tuple-element.68.routes), channel_id=1, source_target_pairs={{0,16},{8,24},{16,0},{24,8},{1,17},{9,25},{17,1},{25,9},{2,18},{10... | collective-permute-start | bytes 21512 | tf_op jit(solution)/shard_map/ppermute | solution.py:1227
  358.4 49.1 %copy-start = (f32[896,512]{1,0:T(8,128)S(1)}, f32[896,512]{1,0:T(8,128)}, u32[]{:S(2)}) copy-start(f32[896,512]{1,0:T(8,128)} %get-tuple-element.36.hidden) | copy-start | bytes 5505028
  358.4 49.1 %copy-start.3 = (bf16[896,512]{1,0:T(8,128)(2,1)S(1)}, bf16[896,512]{1,0:T(8,128)(2,1)}, u32[]{:S(2)}) copy-start(bf16[896,512]{1,0:T(8,128)(2,1)} %get-tuple-element.47) | copy-start | bytes 2752516
  407.5 3.1 copy-start.2
  410.0 1.6 copy-start.1

commit v4 on v3

--- a/solution.py
+++ b/solution.py
@@ -18,7 +18,7 @@
 FAR = -1e30
 BF = jnp.bfloat16
 F32 = jnp.float32
-VMEM_LIMIT = 60 * 1024 * 1024
+VMEM_LIMIT = 63 * 1024 * 1024
 
 ERFC = (
     0.2820843458175659,
@@ -70,6 +70,11 @@
 def weight(packed, columns):
     part = packed[:, :, :, columns]
     return part.reshape(-1, part.shape[-1])
+
+
+def set_weight(grads, columns, value):
+    spot = grads.shape[:3]
+    grads[:, :, :, columns] = value.astype(BF).reshape(*spot, value.shape[1])
 
 
 def window(image):
@@ -410,6 +415,7 @@
 
 def retreat_kernel(
     experts,
+    steps,
     tokens,
     cotangent,
     hidden,
@@ -467,7 +473,7 @@
 
     lax.fori_loop(0, rows // STRIP, norm_two, 0)
     merge = slice(3 * width, 4 * width)
-    grads[:, merge] = dot_tn(mixed[...], branch_grad[...]).astype(BF)
+    set_weight(grads, merge, dot_tn(mixed[...], branch_grad[...]))
 
     def project(j, carry):
         part = pl.ds(pl.multiple_of(j * half, 16), half)
@@ -475,6 +481,7 @@
         return carry
 
     lax.fori_loop(0, 2, project, 0)
+    steps[0]()
 
     lane = lax.broadcasted_iota(jnp.int32, (1, LANES), 1)
     low = lane < HEAD_DIM
@@ -516,9 +523,11 @@
         return carry
 
     lax.fori_loop(0, images, attend, 0)
+    steps[1]()
     for third in range(3):
         columns = slice(third * width, (third + 1) * width)
-        grads[:, columns] = dot_tn(first[...], joined_grad[:, columns]).astype(BF)
+        set_weight(grads, columns, dot_tn(first[...], joined_grad[:, columns]))
+    steps[2]()
 
     def finish(start, size):
         part = pl.ds(start, size)
@@ -545,7 +554,7 @@
         token_grad[done:real, :] = finish(done, ceil_to(real - done, 16))[: real - done]
     for which, row in ((2, experts), (3, experts + 1), (0, experts + 2), (1, experts + 3)):
         sums[row : row + 1, :] = jnp.sum(totals[which], 0, keepdims=True)
-    grads[:, 4 * width :] = sums[...].T.astype(BF)
+    set_weight(grads, slice(4 * width, None), sums[...].T)
 
 
 def retreat(
@@ -555,8 +564,8 @@
     experts = probs.shape[0]
     shape = jax.ShapeDtypeStruct
     return pl.pallas_call(
-        partial(retreat_kernel, experts),
-        out_shape=(shape((real, width), F32), shape((width, packed.shape[-1]), BF)),
+        partial(retreat_kernel, experts, (lambda: None,) * 3),
+        out_shape=(shape((real, width), F32), shape(packed.shape, BF)),
         in_specs=[pl.BlockSpec(memory_space=pltpu.VMEM)] * (9 + len(returned)),
         out_specs=[pl.BlockSpec(memory_space=pltpu.VMEM)] * 2,
         scratch_shapes=[
@@ -962,18 +971,65 @@
     )(tokens, cotangent, routes, triple, merge, rest, up, down)
 
 
-def reduce_large_kernel(
-    up, down, rows, mixture, gates, up_total, down_total, rows_far, mixture_far, gates_far, *rest
+def back_kernel(
+    experts,
+    tokens,
+    cotangent,
+    hidden,
+    normed,
+    qkv,
+    mixed,
+    probs,
+    packed,
+    gates,
+    rows,
+    mixture,
+    up,
+    down,
+    block_out,
+    token_grad,
+    triple_total,
+    merge_total,
+    small_total,
+    up_total,
+    down_total,
+    gates_far,
+    rows_near,
+    rows_far,
+    mixture_near,
+    mixture_far,
+    change,
+    first,
+    hidden_grad,
+    branch_grad,
+    joined_grad,
+    small,
+    sums,
+    totals,
+    grads,
+    grads_low,
+    grads_twin,
+    grads_middle,
+    grads_far,
+    up_low,
+    down_low,
+    up_far,
+    down_far,
+    z_sent,
+    z_arrived,
+    loaded,
+    *buffers,
 ):
-    z_sent, z_arrived, up_low, down_low, up_far, down_far = rest[:6]
-    buffers = rest[6:]
+    real, width = token_grad.shape
+    count = tokens.shape[0]
+    crossing = ceil_to(real, 16)
     place = Place()
     place.meet([place.to_x, place.to_y, place.to_core, place.to_twin, place.to_far])
-    count = rows_far.shape[0]
+    near, far = pl.ds(0, crossing), pl.ds(count, crossing)
     pairs = (
-        (rows.at[pl.ds(count, count)], rows_far),
+        (rows.at[far], rows_far.at[near]),
         (gates.at[:, pl.ds(count, count)], gates_far),
-        (mixture.at[pl.ds(count, count)], mixture_far),
+        (mixture.at[far], mixture_far),
     )
     across = [
         send_to(source, target, z_sent.at[i], z_arrived.at[i], place.to_far)
@@ -981,108 +1037,172 @@
     ]
     for copy in across:
         copy.start()
-    sources = (up.at[1], down.at[1], up.at[0], down.at[0])
+    sources = (up.at[1], down.at[1], up.at[0], down.at[0], grads)
     folds = [
         Fold(place, source, *buffers[8 * i : 8 * i + 8]) for i, source in enumerate(sources)
     ]
     twins = [
-        send_to(low, far, z_sent.at[3 + i], z_arrived.at[3 + i], place.to_twin)
-        for i, (low, far) in enumerate(((up_low, up_far), (down_low, down_far)))
+        send_to(low, other, z_sent.at[3 + i], z_arrived.at[3 + i], place.to_twin)
+        for i, (low, other) in enumerate(
+            ((up_low, up_far), (down_low, down_far), (grads_low, grads_twin))
+        )
     ]
-    for fold in folds:
+    last = send_to(grads_middle, grads_far, z_sent.at[6], z_arrived.at[6], place.to_far)
+    for fold in folds[:4]:
         fold.start()
+    loads = (
+        pltpu.make_async_copy(rows.at[pl.ds(0, count)], rows_near, loaded.at[0]),
+        pltpu.make_async_copy(mixture.at[near], mixture_near, loaded.at[1]),
+    )
+    for copy in loads:
+        copy.start()
+    rows_far[crossing:, :] = jnp.zeros((count - crossing, width), BF)
     folds[0].outward()
     folds[1].outward()
     folds[0].inward()
     folds[2].outward()
-    folds[1].inward()
     folds[3].outward()
-    folds[0].total(up_low)
-    twins[0].start()
-    folds[2].inward()
-    folds[1].total(down_low)
-    twins[1].start()
-    folds[3].inward()
+
+    across[1].wait_recv()
+    z = lax.axis_index("expert")
+    own = [gates[at : at + 2, :count] for at in (0, 2)]
+    other = [gates_far[at : at + 2, :] for at in (0, 2)]
+    odd = jnp.full((2, count), z % 2, jnp.int32) == 1
+    upper = jnp.full((2, count), z // 2, jnp.int32) == 1
+    for pair in (own, other):
+        pair[:] = [jnp.where(odd, pair[1], pair[0]), jnp.where(odd, pair[0], pair[1])]
+    for i in range(2):
+        change[2 * i : 2 * i + 2, :] = jnp.where(upper, other[i], own[i])
+        change[4 + 2 * i : 6 + 2 * i, :] = jnp.where(upper, own[i], other[i])
+    loads[0].wait()
+    across[0].wait_recv()
+
+    def middle_step():
+        folds[2].inward()
+        folds[0].total(up_low)
+        twins[0].start()
+
+    def late_step():
+        folds[3].inward()
+        folds[1].total(down_low)
+        twins[1].start()
+
+    retreat_kernel(
+        experts,
+        (folds[1].inward, middle_step, late_step),
+        tokens,
+        cotangent,
+        hidden,
+        normed,
+        qkv,
+        mixed,
+        probs,
+        change,
+        packed,
+        rows_near,
+        rows_far,
+        token_grad,
+        grads,
+        first,
+        hidden_grad,
+        branch_grad,
+        joined_grad,
+        small,
+        sums,
+        totals,
+    )
+    tail = folds[4]
+    tail.start()
+    tail.outward()
+    tail.inward()
+    tail.total(grads_low)
+    twins[2].start()
+
+    loads[1].wait()
+    across[2].wait_recv()
+
+    def output(start, size):
+        part = pl.ds(start, size)
+        total = hidden[part, :] + mixture_near[part, :].astype(F32)
+        return (total + mixture_far[part, :].astype(F32)).astype(BF)
+
+    def output_loop(j, carry):
+        start = pl.multiple_of(j * STRIP, STRIP)
+        block_out[pl.ds(start, STRIP), :] = output(start, STRIP)
+        return carry
+
+    lax.fori_loop(0, real // STRIP, output_loop, 0)
+    done = real // STRIP * STRIP
+    if done < real:
+        block_out[done:real, :] = output(done, crossing - done)[: real - done]
+
+    twins[2].wait_recv()
+    for half in range(2):
+        add_up(grads_middle.at[half], grads_low.at[half], grads_twin.at[half])
+    last.start()
     twins[0].wait_recv()
     folds[2].total(up_total, up_far)
     twins[1].wait_recv()
     folds[3].total(down_total, down_far)
+    last.wait_recv()
+    size = triple_total.shape[0] // 2
+    for half in range(2):
+        part = slice(half * size, half * size + size)
+        total = grads_middle[half].astype(F32) + grads_far[half].astype(F32)
+        triple_total[part, :] = total[:, : 3 * width]
+        merge_total[part, :] = total[:, 3 * width : 4 * width]
+        small_total[part, :] = total[:, 4 * width :]
     for fold in folds:
         fold.finish()
-    for copy in twins:
+    for copy in across + twins + [last]:
         copy.wait_send()
-    for copy in across:
-        copy.wait()
-
-
-def reduce_large(up, down, rows, mixture, gates):
+
+
+def back(
+    tokens, cotangent, hidden, normed, qkv, mixed, probs, packed, gates, rows, mixture, up, down, real
+):
+    count, width = tokens.shape
+    experts = probs.shape[0]
     shape = jax.ShapeDtypeStruct
-    count = rows.shape[0] // 2
-    half_up, half_down = up.shape[3:], down.shape[3:]
+    halves = [up.shape[3:], down.shape[3:]] * 2 + [packed.shape[2:]]
+    size = 2 * packed.shape[2]
+    crossing = ceil_to(real, 16)
+    scratch = [pltpu.VMEM((8, count), F32)]
+    scratch += [pltpu.VMEM((count, width), BF)] * 2
+    scratch += [pltpu.VMEM((crossing, width), BF)] * 2
+    scratch += [
+        pltpu.VMEM((experts, count), F32),
+        pltpu.VMEM((count, width), BF),
+        pltpu.VMEM((count, width), F32),
+        pltpu.VMEM((count, width), BF),
+        pltpu.VMEM((count, 3 * width), BF),
+        pltpu.VMEM((LANES, width), F32),
+        pltpu.VMEM((LANES, width), F32),
+        pltpu.VMEM((4, 8, width), F32),
+        pltpu.VMEM(packed.shape, BF),
+    ]
+    scratch += [pltpu.VMEM(packed.shape[1:], BF)] * 4
+    scratch += [pltpu.VMEM((2, *half), BF) for half in halves[:4]]
+    scratch += [pltpu.SemaphoreType.DMA((7,))] * 2 + [pltpu.SemaphoreType.DMA((2,))]
+    for half in halves:
+        scratch += fold_scratch(half)
     return pl.pallas_call(
-        reduce_large_kernel,
+        partial(back_kernel, experts),
         out_shape=(
+            shape((real, width), BF),
+            shape((real, width), F32),
+            shape((size, 3 * width), F32),
+            shape((size, width), F32),
+            shape((size, LANES), F32),
             shape(up.shape[2:], F32),
             shape(down.shape[2:], F32),
-            shape((count, rows.shape[1]), BF),
-            shape((count, mixture.shape[1]), BF),
-            shape((gates.shape[0], count), F32),
         ),
-        in_specs=[ANY] * 5,
-        out_specs=[VMEM, VMEM, ANY, ANY, ANY],
-        scratch_shapes=[
-            pltpu.SemaphoreType.DMA((5,)),
-            pltpu.SemaphoreType.DMA((5,)),
-            pltpu.VMEM((2, *half_up), BF),
-            pltpu.VMEM((2, *half_down), BF),
-            pltpu.VMEM((2, *half_up), BF),
-            pltpu.VMEM((2, *half_down), BF),
-            *(fold_scratch(half_up) + fold_scratch(half_down)) * 2,
-        ],
+        in_specs=[VMEM] * 9 + [ANY] * 4,
+        out_specs=[VMEM] * 7,
+        scratch_shapes=scratch,
         compiler_params=comm_params(3),
-        name="reduce_large",
-    )(up, down, rows, mixture, gates)
-
-
-def reduce_small_kernel(grads, total, z_sent, z_arrived, low, twin, middle, far, *buffers):
-    place = Place()
-    place.meet([place.to_x, place.to_y, place.to_core, place.to_twin, place.to_far])
-    fold = Fold(place, grads, *buffers)
-    fold.start()
-    fold.outward()
-    fold.inward()
-    fold.total(low)
-    first = send_to(low, twin, z_sent.at[0], z_arrived.at[0], place.to_twin)
-    first.start()
-    first.wait_recv()
-    for half in range(2):
-        add_up(middle.at[half], low.at[half], twin.at[half])
-    second = send_to(middle, far, z_sent.at[1], z_arrived.at[1], place.to_far)
-    second.start()
-    second.wait_recv()
-    for half in range(2):
-        add_up(total.at[half], middle.at[half], far.at[half])
-    fold.finish()
-    first.wait_send()
-    second.wait_send()
-
-
-def reduce_small(grads):
-    half = grads.shape[2:]
-    return pl.pallas_call(
-        reduce_small_kernel,
-        out_shape=jax.ShapeDtypeStruct(grads.shape[1:], F32),
-        in_specs=[ANY],
-        out_specs=VMEM,
-        scratch_shapes=[
-            pltpu.SemaphoreType.DMA((2,)),
-            pltpu.SemaphoreType.DMA((2,)),
-            *[pltpu.VMEM((2, *half), BF)] * 4,
-            *fold_scratch(half),
-        ],
-        compiler_params=comm_params(4),
-        name="reduce_small",
-    )(grads)
+        name="back",
+    )(tokens, cotangent, hidden, normed, qkv, mixed, probs, packed, gates, rows, mixture, up, down)
 
 
 def pack(triple, merge, router, gain_one, bias_one, gain_two, bias_two):
@@ -1189,6 +1309,7 @@
         packed,
         real,
     )
+    grads = grads.reshape(width, packed.shape[-1])
     grads = lax.psum_scatter(grads, "fsdp", scatter_dimension=0, tiled=True)
     grads = lax.psum(grads, "expert").astype(F32)
     return (block_out, token_grad) + unpack(grads, width, experts) + (
@@ -1268,14 +1389,7 @@
         all_upstream.reshape(2 * padded, width),
         2 * capacity,
     )
-    up_grad, down_grad, row_far, mixture_far, gate_far = reduce_large(
-        up_grad, down_grad, row_grad, mixture, gate_grad
-    )
-    gate_grad = jnp.stack([gate_grad[:4, :padded], gate_far[:4]]).reshape(2, 2, 2, padded)
-    gate_grad = swapped(swapped(gate_grad, odd, 1), upper, 0).reshape(experts, padded)
-    total = hidden[:real] + mixture[:real].astype(F32) + mixture_far[:real].astype(F32)
-    block_out = total.astype(BF)
-    token_grad, grads = retreat(
+    block_out, token_grad, triple_grad, merge_grad, rest, up_grad, down_grad = back(
         token_rows,
         upstream,
         hidden,
@@ -1283,13 +1397,27 @@
         qkv,
         mixed,
         probs,
+        packed,
         gate_grad,
-        (row_grad, row_far),
-        packed,
+        row_grad,
+        mixture,
+        up_grad,
+        down_grad,
         real,
     )
-    grads = reduce_small(grads.reshape(packed.shape)).reshape(-1, packed.shape[-1])
-    return (block_out, token_grad) + unpack(grads, width, experts) + (up_grad, down_grad)
+    return (
+        block_out,
+        token_grad,
+        rest[:, experts],
+        rest[:, experts + 1],
+        triple_grad,
+        merge_grad,
+        rest[:, experts + 2],
+        rest[:, experts + 3],
+        rest[:, :experts],
+        up_grad,
+        down_grad,
+    )
 
 
 def solution(mesh):

time: 412 us -> 364 us (0.88); the launches traced: 413 us -> 360 us
  Pallas kernels: 386 us -> 337 us
    pallas_call x3 -> x1, Pallas kernels: 185 us -> 129 us  [back(): pl.pallas_call(partial(back_kernel, experts), out_shape=(shape((real, wid...]
    pallas_call x1, Pallas kernels: 111 us -> 118 us  [expert_block(): pl.pallas_call(partial(expert_kernel, tiles, parts, room), grid_spec=pltp...]
    slice x6 -> x1, local copies, waits for them, and re-layouts: 7.52 us -> 1.69 us  [local_square(): rest[:, experts + 3]]
    unnamed x14 -> x20, local copies, waits for them, and re-layouts: 3.39 us -> 8.83 us
  transfers between devices with their start and end apart: 1 -> 1, of which waited for: 0 -> 0; matrix products, arithmetic and copies ran while one was open for 1% -> 2% of each run, Pallas kernels for 22% -> 25%
where the time goes in v4:
time: 364 us; the launch traced here: 360 us
  Pallas kernels  337 us (93%)
  local copies, waits for them, and re-layouts  16 us (4%)
  starting transfers between devices  4.12 us (1%)
    pallas_call x1, Pallas kernels, back(): pl.pallas_call(partial(back_kernel, experts), out_shape=(shape((real, wid...  129 us
    pallas_call x1, Pallas kernels, expert_block(): pl.pallas_call(partial(expert_kernel, tiles, parts, room), grid_spec=pltp...  118 us
    pallas_call x1, Pallas kernels, front(): pl.pallas_call(partial(front_kernel, experts), out_shape=(shape((rows, wi...  89.9 us
    unnamed x20, local copies, waits for them, and re-layouts  8.83 us
  transfers between devices with their start and end apart: 1, of which 0 were waited for; matrix products, arithmetic and copies ran while one was open for 2% of the time, Pallas kernels for 25%

profile of v4, /device:TPU:0, one launch (start us, length us, event | category | flops | bytes accessed | tf_op | source)
XLA Modules:
  0.0 360.0 jit_solution(10223051314252856609)
XLA Ops:
  0.6 0.7 pad_bitcast_fusion
  1.3 4.1 %collective-permute-start = (s32[2,896]{1,0:T(2,128)S(1)}, s32[2,896]{1,0:T(2,128)S(1)}, u32[]{:S(2)}, u32[]{:S(2)}) collective-permute-start(s32[2,896]{1,0:T(2,128)S(1)} %get-tuple-element.101.routes), channel_id=1, source_target_pairs={{0,16},{8,24},{16,0},{24,8},{1,17},{9,25},{17,1},{25,9},{2,18},{10... | collective-permute-start | bytes 21512 | tf_op jit(solution)/shard_map/ppermute | solution.py:1348
  5.5 0.7 copy.45
  6.2 0.7 copy.46
  7.0 0.7 copy.47
  7.7 0.7 copy.48
  8.5 0.8 copy.44
  9.2 0.7 pad_add_fusion.rest
  10.0 89.9 %front.1 = (bf16[896,512]{1,0:T(8,128)(2,1)}, bf16[896,512]{1,0:T(8,128)(2,1)}, bf16[8,2,32,2176]{3,2,1,0:T(8,128)(2,1)}, bf16[896,1536]{1,0:T(8,128)(2,1)}, bf1...) custom-call(bf16[788,512]{1,0:T(8,128)(2,1)} %tokens.1, ...), custom_call_target="tpu_custom_call" | custom-call | tf_op jit(solution)/shard_map/front/pallas_call | solution.py:937
  99.9 0.8 copy.58
  101.1 0.2 fusion.2
  101.4 0.1 copy.57
  101.6 0.6 convert_element_type.19.meta
  102.4 0.6 maximum_bitcast_fusion.info
  103.0 118.3 %experts.1 = (bf16[1792,512]{1,0:T(8,128)(2,1)}, bf16[1792,512]{1,0:T(8,128)(2,1)}, f32[8,1792]{1,0:T(8,128)}, bf16[2,8,2,64,2048]{4,3,2,1,0:T(8,128)(2,1)}, bf16[2,8,2,256,512]{4,3,2,1,0:T(8,128)(2,1)}) custom-call(s32[32]{0:T(128)} %convert_element_type.19.meta, f32[7,8,256]{2,1,0:T(8,128)} %maximum_bitcast_fusion.info, ...), custom_call_target="tpu_custom_call" | custom-call | tf_op jit(solution)/shard_map/experts/pallas_call | solution.py:378
  221.3 128.9 %back.1 = (bf16[788,512]{1,0:T(8,128)(2,1)}, f32[788,512]{1,0:T(8,128)}, f32[64,1536]{1,0:T(8,128)}, f32[64,512]{1,0:T(8,128)}, f32[64,128]{1,0:T(8,128)}, /*ind...) custom-call(bf16[896,512]{1,0:T(8,128)(2,1)} %get-tuple-element.36.tokens, bf16[896,512]{1,0:T(8,128)(2,1)} %get-tuple-element.37.cotangent, ...), custom_call_target="tpu_custom_call" | custom-call | tf_op jit(solution)/shard_map/back/pallas_call | solution.py:1189
  350.2 1.7 slice_reduce_fusion
  351.9 1.4 copy.56
  353.3 2.1 copy.72
  355.4 1.2 copy.73
  356.6 0.7 copy.74
  357.4 0.7 copy.75
  358.0 1.0 copy.76
  359.0 1.0 copy.77
  (31 shorter events, 0.7 us)
Async XLA Ops:
  1.3 8.6 %copy-start.5 = (s32[2,896]{1,0:T(2,128)}, s32[2,896]{1,0:T(2,128)S(1)}, u32[]{:S(2)}) copy-start(s32[2,896]{1,0:T(2,128)S(1)} %get-tuple-element.101.routes) | copy-start | bytes 21508
  1.3 99.6 %collective-permute-start = (s32[2,896]{1,0:T(2,128)S(1)}, s32[2,896]{1,0:T(2,128)S(1)}, u32[]{:S(2)}, u32[]{:S(2)}) collective-permute-start(s32[2,896]{1,0:T(2,128)S(1)} %get-tuple-element.101.routes), channel_id=1, source_target_pairs={{0,16},{8,24},{16,0},{24,8},{1,17},{9,25},{17,1},{25,9},{2,18},{10... | collective-permute-start | bytes 21512 | tf_op jit(solution)/shard_map/ppermute | solution.py:1348
  350.2 5.2 %copy-start = (f32[788,512]{1,0:T(8,128)S(1)}, f32[788,512]{1,0:T(8,128)}, u32[]{:S(2)}) copy-start(f32[788,512]{1,0:T(8,128)} %get-tuple-element.116) | copy-start | bytes 4841476
  355.4 1.2 copy-start.3
  355.4 2.0 copy-start.4
  355.4 2.6 copy-start.2
  356.6 2.4 copy-start.1

commit v5 on v4

--- a/solution.py
+++ b/solution.py
@@ -206,65 +206,64 @@
     gate_grad,
     up_grad,
     down_grad,
-    packed_rows,
-    packed_grads,
+    slot_gate,
     out_sum,
     back_sum,
-    out_low,
-    back_low,
+    packed,
     up_sum,
     down_sum,
 ):
     width = rows.shape[1]
     step = pl.program_id(0)
-    owned = out_low.shape[0]
+    owned = packed.shape[0]
     member = jnp.minimum(step // parts, owned - 1)
     part = step - member * parts
     span = up_sum.shape[1]
     stride = meta.shape[0] // owned
+
+    def windows(tile):
+        bases, count = [], 0
+        for which in range(owned):
+            begin = meta[which * stride + tile]
+            end = meta[which * stride + tile + 1]
+            bases.append(begin // 16 * 16)
+            used = jnp.where(end > begin, (end - bases[-1] + SUB - 1) // SUB, 0)
+            count = jnp.maximum(count, used)
+        return bases, count
 
     @pl.when(step == 0)
     def _():
         def clear(j, carry):
             at = pl.ds(pl.multiple_of(j * TILE, TILE), TILE)
             for which in range(owned):
-                out_low[which, at, :] = jnp.zeros((TILE, width), BF)
-                back_low[which, at, :] = jnp.zeros((TILE, width), BF)
+                packed[which, at, :] = jnp.zeros((TILE, packed.shape[2]), BF)
+                slot_gate[which, at, :] = jnp.zeros((TILE, LANES), F32)
             return carry
 
         lax.fori_loop(0, room // TILE, clear, 0)
 
-    @pl.when((step < owned * parts) & (part == 0))
-    def _():
-        def clear(j, carry):
-            at = pl.ds(pl.multiple_of(j * TILE, TILE), TILE)
-            packed_rows[at, :] = jnp.zeros((TILE, width), BF)
-            packed_grads[at, :] = jnp.zeros((TILE, width), BF)
-            return carry
-
-        lax.fori_loop(0, room // TILE, clear, 0)
-
         def gather(tile, carry):
-            begin = meta[member * stride + tile]
-            end = meta[member * stride + tile + 1]
-            base = begin // 16 * 16
-            count = jnp.where(end > begin, (end - base + SUB - 1) // SUB, 0)
+            bases, count = windows(tile)
             at = pl.ds(pl.multiple_of(tile * TILE, TILE), TILE)
-            order = info[tile, pl.ds(member, 1), :]
-            columns = info[tile].T
-            which = lax.broadcasted_iota(jnp.int32, (1, columns.shape[1]), 1)
-            gate = jnp.where(which == owned + member, columns, 0.0)
-            gate = jnp.sum(gate, -1, keepdims=True)
-            source = rows[at, :]
-            gated = (upstream[at, :].astype(F32) * gate).astype(BF)
+            known = info[tile]
 
             def place(j, inner):
-                origin = pl.multiple_of(base + j * SUB, 16)
-                wanted = lax.broadcasted_iota(jnp.int32, (SUB, 1), 0) + origin
-                chosen = jnp.where(order == wanted.astype(F32), 1.0, 0.0).astype(BF)
-                to = pl.ds(origin, SUB)
-                packed_rows[to, :] += dot_nn(chosen, source).astype(BF)
-                packed_grads[to, :] += dot_nn(chosen, gated).astype(BF)
+                spots, chosen = [], []
+                for which in range(owned):
+                    origin = pl.multiple_of(bases[which] + j * SUB, 16)
+                    wanted = lax.broadcasted_iota(jnp.int32, (SUB, 1), 0) + origin
+                    hit = known[which : which + 1, :] == wanted.astype(F32)
+                    gate = jnp.where(hit, known[owned + which : owned + which + 1, :], 0.0)
+                    to = pl.ds(origin, SUB)
+                    slot_gate[which, to, :] += jnp.sum(gate, -1, keepdims=True)
+                    spots.append(to)
+                    chosen.append(jnp.where(hit, 1.0, 0.0).astype(BF))
+                chosen = jnp.concatenate(chosen, 0)
+                for at_column, source in ((0, rows), (width, upstream)):
+                    picked = dot_nn(chosen, source[at, :]).astype(BF)
+                    columns = slice(at_column, at_column + width)
+                    for which, to in enumerate(spots):
+                        packed[which, to, columns] += picked[which * SUB : (which + 1) * SUB]
                 return inner
 
             return lax.fori_loop(0, count, place, carry)
@@ -281,8 +280,10 @@
 
         def chunk(j, carry):
             at = pl.ds(pl.multiple_of(j * TILE, TILE), TILE)
-            source = packed_rows[at, :]
-            grads = packed_grads[at, :]
+            source = packed[member, at, :width]
+            change = packed[member, at, width : 2 * width].astype(F32)
+            gate = slot_gate[member, at, 0:1]
+            grads = (change * gate).astype(BF)
             active, slope = gelu_both(dot_nn(source, up_part))
             active = active.astype(BF)
             out = dot_nn(active, down_part)
@@ -301,8 +302,16 @@
 
             @pl.when(part == parts - 1)
             def _():
-                out_low[member, at, :] = (out_sum[at, :] + out).astype(BF)
-                back_low[member, at, :] = (back_sum[at, :] + back).astype(BF)
+                total = (out_sum[at, :] + out).astype(BF).astype(F32)
+                change = packed[member, at, width : 2 * width].astype(F32)
+                dots = jnp.sum(total * change, -1, keepdims=True)
+                packed[member, at, :width] = (total * gate).astype(BF)
+                packed[member, at, width : 2 * width] = (back_sum[at, :] + back).astype(BF)
+                high = dots.astype(BF).astype(F32)
+                lane = lax.broadcasted_iota(jnp.int32, (1, LANES), 1)
+                both = jnp.where(lane == member, high, 0.0)
+                both += jnp.where(lane == member + owned, dots - high, 0.0)
+                packed[member, at, 2 * width :] = both.astype(BF)
 
             down_sum[...] += dot_tn(active, grads)
             up_sum[...] += dot_tn(source, pre_grad)
@@ -315,36 +324,26 @@
     @pl.when(step >= owned * parts)
     def _():
         tile = step - owned * parts
-        at = pl.ds(pl.multiple_of(tile * TILE, TILE), TILE)
+        bases, count = windows(tile)
         columns = info[tile].T
-        grads = upstream[at, :].astype(F32)
-        mixture[...] = jnp.zeros(mixture.shape, mixture.dtype)
-        lane = lax.broadcasted_iota(jnp.int32, (1, LANES), 1)
-        zero = jnp.zeros((TILE, width), F32)
-        mix, back, dots = zero, zero, jnp.zeros((TILE, LANES), F32)
-        for which in range(owned):
-            begin = meta[which * stride + tile]
-            end = meta[which * stride + tile + 1]
-            base = begin // 16 * 16
-            count = jnp.where(end > begin, (end - base + TILE - 1) // TILE, 0)
-            order = columns[:, which : which + 1]
-
-            def fetch(j, carry, which=which, base=base, order=order):
-                out, back = carry
-                origin = pl.multiple_of(base + j * TILE, 16)
-                wanted = lax.broadcasted_iota(jnp.int32, (1, TILE), 1) + origin
-                chosen = jnp.where(order == wanted.astype(F32), 1.0, 0.0).astype(BF)
-                source = pl.ds(origin, TILE)
-                out += dot_nn(chosen, out_low[which, source, :])
-                back += dot_nn(chosen, back_low[which, source, :])
-                return out, back
-
-            out, back = lax.fori_loop(0, count, fetch, (zero, back))
-            mix += out * columns[:, owned + which : owned + which + 1]
-            dots += jnp.where(lane == which, jnp.sum(out * grads, -1, keepdims=True), 0.0)
-        mixture[...] = mix.astype(BF)
-        row_grad[...] = back.astype(BF)
-        gate_grad[...] = dots.T[:8]
+
+        def fetch(j, total):
+            chosen, source = [], []
+            for which in range(owned):
+                origin = pl.multiple_of(bases[which] + j * SUB, 16)
+                wanted = lax.broadcasted_iota(jnp.int32, (1, SUB), 1) + origin
+                hit = columns[:, which : which + 1] == wanted.astype(F32)
+                chosen.append(jnp.where(hit, 1.0, 0.0).astype(BF))
+                source.append(packed[which, pl.ds(origin, SUB), :])
+            return total + dot_nn(jnp.concatenate(chosen, 1), jnp.concatenate(source, 0))
+
+        total = lax.fori_loop(0, count, fetch, jnp.zeros((TILE, packed.shape[2]), F32))
+        mixture[...] = total[:, :width].astype(BF)
+        row_grad[...] = total[:, width : 2 * width].astype(BF)
+        dots = total[:, 2 * width :].T
+        dots = dots[:owned] + dots[owned : 2 * owned]
+        gate_grad[...] = jnp.zeros(gate_grad.shape, F32)
+        gate_grad[:owned, :] = dots
 
 
 def expert_block(meta, info, up, down, rows, upstream, most):
@@ -355,7 +354,8 @@
     tiles = count // TILE
     parts = hidden_units // 512
     span = hidden_units // parts
-    room = ceil_to(most, TILE) + TILE
+    held = ceil_to(most, TILE)
+    room = ceil_to(most + 3 * SUB, TILE)
     shape = jax.ShapeDtypeStruct
     last = owned * parts - 1
 
@@ -389,12 +389,10 @@
                 down_spec,
             ],
             scratch_shapes=[
-                pltpu.VMEM((room, width), BF),
-                pltpu.VMEM((room, width), BF),
-                pltpu.VMEM((room, width), F32),
-                pltpu.VMEM((room, width), F32),
-                pltpu.VMEM((owned, room, width), BF),
-                pltpu.VMEM((owned, room, width), BF),
+                pltpu.VMEM((owned, room, LANES), F32),
+                pltpu.VMEM((held, width), F32),
+                pltpu.VMEM((held, width), F32),
+                pltpu.VMEM((owned, room, 2 * width + LANES), BF),
                 pltpu.VMEM((width, span), F32),
                 pltpu.VMEM((span, width), F32),
             ],

time: 364 us -> 341 us (0.937); the launches traced: 360 us -> 342 us
  Pallas kernels: 337 us -> 319 us
    pallas_call x1, Pallas kernels: 118 us -> 86.6 us  [expert_block(): pl.pallas_call(partial(expert_kernel, tiles, parts, room), grid_spec=pltp...]
    pallas_call x1, Pallas kernels: 129 us -> 143 us  [back(): pl.pallas_call(partial(back_kernel, experts), out_shape=(shape((real, wid...]
  transfers between devices with their start and end apart: 1 -> 1, of which waited for: 0 -> 0; matrix products, arithmetic and copies ran while one was open for 2% -> 2% of each run, Pallas kernels for 25% -> 26%
where the time goes in v5:
time: 341 us; the launch traced here: 342 us
  Pallas kernels  319 us (94%)
  local copies, waits for them, and re-layouts  16 us (5%)
  starting transfers between devices  4.12 us (1%)
    pallas_call x1, Pallas kernels, back(): pl.pallas_call(partial(back_kernel, experts), out_shape=(shape((real, wid...  143 us
    pallas_call x1, Pallas kernels, front(): pl.pallas_call(partial(front_kernel, experts), out_shape=(shape((rows, wi...  89.9 us
    pallas_call x1, Pallas kernels, expert_block(): pl.pallas_call(partial(expert_kernel, tiles, parts, room), grid_spec=pltp...  86.6 us
    unnamed x20, local copies, waits for them, and re-layouts  8.83 us
  transfers between devices with their start and end apart: 1, of which 0 were waited for; matrix products, arithmetic and copies ran while one was open for 2% of the time, Pallas kernels for 26%

profile of v5, /device:TPU:0, one launch (start us, length us, event | category | flops | bytes accessed | tf_op | source)
XLA Modules:
  0.0 342.2 jit_solution(10193494376925955705)
XLA Ops:
  0.6 0.7 pad_bitcast_fusion
  1.3 4.1 %collective-permute-start = (s32[2,896]{1,0:T(2,128)S(1)}, s32[2,896]{1,0:T(2,128)S(1)}, u32[]{:S(2)}, u32[]{:S(2)}) collective-permute-start(s32[2,896]{1,0:T(2,128)S(1)} %get-tuple-element.101.routes), channel_id=1, source_target_pairs={{0,16},{8,24},{16,0},{24,8},{1,17},{9,25},{17,1},{25,9},{2,18},{10... | collective-permute-start | bytes 21512 | tf_op jit(solution)/shard_map/ppermute | solution.py:1346
  5.5 0.7 copy.45
  6.2 0.7 copy.46
  7.0 0.7 copy.47
  7.7 0.7 copy.48
  8.5 0.8 copy.44
  9.2 0.7 pad_add_fusion.rest
  10.0 89.9 %front.1 = (bf16[896,512]{1,0:T(8,128)(2,1)}, bf16[896,512]{1,0:T(8,128)(2,1)}, bf16[8,2,32,2176]{3,2,1,0:T(8,128)(2,1)}, bf16[896,1536]{1,0:T(8,128)(2,1)}, bf1...) custom-call(bf16[788,512]{1,0:T(8,128)(2,1)} %tokens.1, ...), custom_call_target="tpu_custom_call" | custom-call | tf_op jit(solution)/shard_map/front/pallas_call | solution.py:935
  99.9 0.8 copy.58
  101.1 0.2 fusion.2
  101.4 0.1 copy.57
  101.6 0.6 convert_element_type.19.meta
  102.4 0.6 maximum_bitcast_fusion.info
  103.0 86.6 %experts.1 = (bf16[1792,512]{1,0:T(8,128)(2,1)}, bf16[1792,512]{1,0:T(8,128)(2,1)}, f32[8,1792]{1,0:T(8,128)}, bf16[2,8,2,64,2048]{4,3,2,1,0:T(8,128)(2,1)}, bf16[2,8,2,256,512]{4,3,2,1,0:T(8,128)(2,1)}) custom-call(s32[32]{0:T(128)} %convert_element_type.19.meta, f32[7,8,256]{2,1,0:T(8,128)} %maximum_bitcast_fusion.info, ...), custom_call_target="tpu_custom_call" | custom-call | tf_op jit(solution)/shard_map/experts/pallas_call | solution.py:378
  189.6 142.8 %back.1 = (bf16[788,512]{1,0:T(8,128)(2,1)}, f32[788,512]{1,0:T(8,128)}, f32[64,1536]{1,0:T(8,128)}, f32[64,512]{1,0:T(8,128)}, f32[64,128]{1,0:T(8,128)}, /*ind...) custom-call(bf16[896,512]{1,0:T(8,128)(2,1)} %get-tuple-element.36.tokens, bf16[896,512]{1,0:T(8,128)(2,1)} %get-tuple-element.37.cotangent, ...), custom_call_target="tpu_custom_call" | custom-call | tf_op jit(solution)/shard_map/back/pallas_call | solution.py:1187
  332.4 1.7 slice_reduce_fusion
  334.1 1.4 copy.56
  335.5 2.1 copy.72
  337.6 1.2 copy.73
  338.8 0.7 copy.74
  339.6 0.7 copy.75
  340.2 1.0 copy.76
  341.2 1.0 copy.77
  (31 shorter events, 0.7 us)
Async XLA Ops:
  1.3 8.6 %copy-start.5 = (s32[2,896]{1,0:T(2,128)}, s32[2,896]{1,0:T(2,128)S(1)}, u32[]{:S(2)}) copy-start(s32[2,896]{1,0:T(2,128)S(1)} %get-tuple-element.101.routes) | copy-start | bytes 21508
  1.3 99.6 %collective-permute-start = (s32[2,896]{1,0:T(2,128)S(1)}, s32[2,896]{1,0:T(2,128)S(1)}, u32[]{:S(2)}, u32[]{:S(2)}) collective-permute-start(s32[2,896]{1,0:T(2,128)S(1)} %get-tuple-element.101.routes), channel_id=1, source_target_pairs={{0,16},{8,24},{16,0},{24,8},{1,17},{9,25},{17,1},{25,9},{2,18},{10... | collective-permute-start | bytes 21512 | tf_op jit(solution)/shard_map/ppermute | solution.py:1346
  332.4 5.2 %copy-start = (f32[788,512]{1,0:T(8,128)S(1)}, f32[788,512]{1,0:T(8,128)}, u32[]{:S(2)}) copy-start(f32[788,512]{1,0:T(8,128)} %get-tuple-element.116) | copy-start | bytes 4841476
  337.6 1.2 copy-start.3
  337.6 2.0 copy-start.4
  337.6 2.6 copy-start.2
  338.8 2.4 copy-start.1

commit v6 on v5

--- a/solution.py
+++ b/solution.py
@@ -274,20 +274,25 @@
     def _():
         up_part = up[...].reshape(width, span)
         down_part = down[...].reshape(span, width)
-        chunks = (meta[member * stride + tiles] + TILE - 1) // TILE
+        held = (meta[member * stride + tiles] + SUB - 1) // SUB
+        chunks = held // 2
         up_sum[...] = jnp.zeros(up_sum.shape, F32)
         down_sum[...] = jnp.zeros(down_sum.shape, F32)
 
-        def chunk(j, carry):
-            at = pl.ds(pl.multiple_of(j * TILE, TILE), TILE)
+        def chunk(j, carry, size=TILE):
+            at = pl.ds(pl.multiple_of(j * TILE, TILE), size)
             source = packed[member, at, :width]
             change = packed[member, at, width : 2 * width].astype(F32)
             gate = slot_gate[member, at, 0:1]
             grads = (change * gate).astype(BF)
-            active, slope = gelu_both(dot_nn(source, up_part))
-            active = active.astype(BF)
+            pieces = []
+            for start in range(0, span, TILE):
+                piece = slice(start, start + TILE)
+                active, slope = gelu_both(dot_nn(source, up_part[:, piece]))
+                change = dot_nt(grads, down_part[piece])
+                pieces.append((active.astype(BF), (change * slope).astype(BF)))
+            active, pre_grad = [jnp.concatenate(piece, 1) for piece in zip(*pieces)]
             out = dot_nn(active, down_part)
-            pre_grad = (dot_nt(grads, down_part) * slope).astype(BF)
             back = dot_nt(pre_grad, up_part)
 
             @pl.when(part == 0)
@@ -318,6 +323,11 @@
             return carry
 
         lax.fori_loop(0, chunks, chunk, 0)
+
+        @pl.when(held % 2 == 1)
+        def _():
+            chunk(chunks, 0, SUB)
+
         up_grad[...] = up_sum[...].astype(BF).reshape(up_grad.shape)
         down_grad[...] = down_sum[...].astype(BF).reshape(down_grad.shape)
 
@@ -352,7 +362,7 @@
     owned = groups * members
     count, width = rows.shape
     tiles = count // TILE
-    parts = hidden_units // 512
+    parts = hidden_units // (1024 if count <= 4096 else 512)
     span = hidden_units // parts
     held = ceil_to(most, TILE)
     room = ceil_to(most + 3 * SUB, TILE)
@@ -1033,19 +1043,19 @@
         send_to(source, target, z_sent.at[i], z_arrived.at[i], place.to_far)
         for i, (source, target) in enumerate(pairs)
     ]
-    for copy in across:
+    for copy in across[:2]:
         copy.start()
     sources = (up.at[1], down.at[1], up.at[0], down.at[0], grads)
     folds = [
         Fold(place, source, *buffers[8 * i : 8 * i + 8]) for i, source in enumerate(sources)
     ]
     twins = [
-        send_to(low, other, z_sent.at[3 + i], z_arrived.at[3 + i], place.to_twin)
+        send_to(low, other, z_sent.at[4 + i], z_arrived.at[4 + i], place.to_twin)
         for i, (low, other) in enumerate(
             ((up_low, up_far), (down_low, down_far), (grads_low, grads_twin))
         )
     ]
-    last = send_to(grads_middle, grads_far, z_sent.at[6], z_arrived.at[6], place.to_far)
+    last = send_to(grads_middle, grads_far, z_sent.at[7], z_arrived.at[7], place.to_far)
     for fold in folds[:4]:
         fold.start()
     loads = (
@@ -1058,6 +1068,7 @@
     folds[0].outward()
     folds[1].outward()
     folds[0].inward()
+    folds[1].inward()
     folds[2].outward()
     folds[3].outward()
 
@@ -1075,19 +1086,19 @@
     loads[0].wait()
     across[0].wait_recv()
 
-    def middle_step():
-        folds[2].inward()
+    def early_step():
         folds[0].total(up_low)
         twins[0].start()
 
-    def late_step():
-        folds[3].inward()
+    def middle_step():
         folds[1].total(down_low)
         twins[1].start()
+        across[2].start()
+        folds[2].inward()
 
     retreat_kernel(
         experts,
-        (folds[1].inward, middle_step, late_step),
+        (early_step, middle_step, lambda: None),
         tokens,
         cotangent,
         hidden,
@@ -1113,26 +1124,9 @@
     tail.start()
     tail.outward()
     tail.inward()
+    folds[3].inward()
     tail.total(grads_low)
     twins[2].start()
-
-    loads[1].wait()
-    across[2].wait_recv()
-
-    def output(start, size):
-        part = pl.ds(start, size)
-        total = hidden[part, :] + mixture_near[part, :].astype(F32)
-        return (total + mixture_far[part, :].astype(F32)).astype(BF)
-
-    def output_loop(j, carry):
-        start = pl.multiple_of(j * STRIP, STRIP)
-        block_out[pl.ds(start, STRIP), :] = output(start, STRIP)
-        return carry
-
-    lax.fori_loop(0, real // STRIP, output_loop, 0)
-    done = real // STRIP * STRIP
-    if done < real:
-        block_out[done:real, :] = output(done, crossing - done)[: real - done]
 
     twins[2].wait_recv()
     for half in range(2):
@@ -1140,6 +1134,23 @@
     last.start()
     twins[0].wait_recv()
     folds[2].total(up_total, up_far)
+    loads[1].wait()
+    across[2].wait_recv()
+
+    def output(start, size):
+        part = pl.ds(start, size)
+        total = hidden[part, :] + mixture_near[part, :].astype(F32)
+        return (total + mixture_far[part, :].astype(F32)).astype(BF)
+
+    def output_loop(j, carry):
+        start = pl.multiple_of(j * STRIP, STRIP)
+        block_out[pl.ds(start, STRIP), :] = output(start, STRIP)
+        return carry
+
+    lax.fori_loop(0, real // STRIP, output_loop, 0)
+    done = real // STRIP * STRIP
+    if done < real:
+        block_out[done:real, :] = output(done, crossing - done)[: real - done]
     twins[1].wait_recv()
     folds[3].total(down_total, down_far)
     last.wait_recv()
@@ -1181,7 +1192,7 @@
     ]
     scratch += [pltpu.VMEM(packed.shape[1:], BF)] * 4
     scratch += [pltpu.VMEM((2, *half), BF) for half in halves[:4]]
-    scratch += [pltpu.SemaphoreType.DMA((7,))] * 2 + [pltpu.SemaphoreType.DMA((2,))]
+    scratch += [pltpu.SemaphoreType.DMA((8,))] * 2 + [pltpu.SemaphoreType.DMA((2,))]
     for half in halves:
         scratch += fold_scratch(half)
     return pl.pallas_call(

time: 341 us -> 313 us (0.918)
  Pallas kernels: 319 us -> 289 us
    pallas_call x1, Pallas kernels: 143 us -> 117 us  [back(): pl.pallas_call(partial(back_kernel, experts), out_shape=(shape((real, wid...]
    pallas_call x1, Pallas kernels: 86.6 us -> 81.5 us  [expert_block(): pl.pallas_call(partial(expert_kernel, tiles, parts, room), grid_spec=pltp...]
  transfers between devices with their start and end apart: 1 -> 1, of which waited for: 0 -> 0; matrix products, arithmetic and copies ran while one was open for 2% -> 2% of each run, Pallas kernels for 26% -> 29%
where the time goes in v6:
time: 313 us; the launch traced here: 312 us
  Pallas kernels  289 us (92%)
  local copies, waits for them, and re-layouts  16 us (5%)
  starting transfers between devices  4.12 us (1%)
    pallas_call x1, Pallas kernels, back(): pl.pallas_call(partial(back_kernel, experts), out_shape=(shape((real, wid...  117 us
    pallas_call x1, Pallas kernels, front(): pl.pallas_call(partial(front_kernel, experts), out_shape=(shape((rows, wi...  89.9 us
    pallas_call x1, Pallas kernels, expert_block(): pl.pallas_call(partial(expert_kernel, tiles, parts, room), grid_spec=pltp...  81.5 us
    unnamed x20, local copies, waits for them, and re-layouts  8.83 us
  transfers between devices with their start and end apart: 1, of which 0 were waited for; matrix products, arithmetic and copies ran while one was open for 2% of the time, Pallas kernels for 29%

profile of v6, /device:TPU:0, one launch (start us, length us, event | category | flops | bytes accessed | tf_op | source)
XLA Modules:
  0.0 311.8 jit_solution(16851170961921597930)
XLA Ops:
  0.6 0.7 pad_bitcast_fusion
  1.3 4.1 %collective-permute-start = (s32[2,896]{1,0:T(2,128)S(1)}, s32[2,896]{1,0:T(2,128)S(1)}, u32[]{:S(2)}, u32[]{:S(2)}) collective-permute-start(s32[2,896]{1,0:T(2,128)S(1)} %get-tuple-element.101.routes), channel_id=1, source_target_pairs={{0,16},{8,24},{16,0},{24,8},{1,17},{9,25},{17,1},{25,9},{2,18},{10... | collective-permute-start | bytes 21512 | tf_op jit(solution)/shard_map/ppermute | solution.py:1357
  5.5 0.7 copy.45
  6.2 0.7 copy.46
  7.0 0.7 copy.47
  7.7 0.7 copy.48
  8.5 0.8 copy.44
  9.2 0.7 pad_add_fusion.rest
  10.0 89.9 %front.1 = (bf16[896,512]{1,0:T(8,128)(2,1)}, bf16[896,512]{1,0:T(8,128)(2,1)}, bf16[8,2,32,2176]{3,2,1,0:T(8,128)(2,1)}, bf16[896,1536]{1,0:T(8,128)(2,1)}, bf1...) custom-call(bf16[788,512]{1,0:T(8,128)(2,1)} %tokens.1, ...), custom_call_target="tpu_custom_call" | custom-call | tf_op jit(solution)/shard_map/front/pallas_call | solution.py:945
  99.9 0.8 copy.58
  101.1 0.2 fusion.2
  101.4 0.1 copy.57
  101.6 0.6 convert_element_type.19.meta
  102.4 0.6 maximum_bitcast_fusion.info
  103.0 81.5 %experts.1 = (bf16[1792,512]{1,0:T(8,128)(2,1)}, bf16[1792,512]{1,0:T(8,128)(2,1)}, f32[8,1792]{1,0:T(8,128)}, bf16[2,8,2,64,2048]{4,3,2,1,0:T(8,128)(2,1)}, bf16[2,8,2,256,512]{4,3,2,1,0:T(8,128)(2,1)}) custom-call(s32[32]{0:T(128)} %convert_element_type.19.meta, f32[7,8,256]{2,1,0:T(8,128)} %maximum_bitcast_fusion.info, ...), custom_call_target="tpu_custom_call" | custom-call | tf_op jit(solution)/shard_map/experts/pallas_call | solution.py:388
  184.5 117.5 %back.1 = (bf16[788,512]{1,0:T(8,128)(2,1)}, f32[788,512]{1,0:T(8,128)}, f32[64,1536]{1,0:T(8,128)}, f32[64,512]{1,0:T(8,128)}, f32[64,128]{1,0:T(8,128)}, /*ind...) custom-call(bf16[896,512]{1,0:T(8,128)(2,1)} %get-tuple-element.36.tokens, bf16[896,512]{1,0:T(8,128)(2,1)} %get-tuple-element.37.cotangent, ...), custom_call_target="tpu_custom_call" | custom-call | tf_op jit(solution)/shard_map/back/pallas_call | solution.py:1198
  302.1 1.7 slice_reduce_fusion
  303.7 1.4 copy.56
  305.2 2.1 copy.72
  307.3 1.2 copy.73
  308.5 0.7 copy.74
  309.2 0.7 copy.75
  309.9 1.0 copy.76
  310.8 1.0 copy.77
  (31 shorter events, 0.7 us)
Async XLA Ops:
  1.3 8.6 %copy-start.5 = (s32[2,896]{1,0:T(2,128)}, s32[2,896]{1,0:T(2,128)S(1)}, u32[]{:S(2)}) copy-start(s32[2,896]{1,0:T(2,128)S(1)} %get-tuple-element.101.routes) | copy-start | bytes 21508
  1.3 99.6 %collective-permute-start = (s32[2,896]{1,0:T(2,128)S(1)}, s32[2,896]{1,0:T(2,128)S(1)}, u32[]{:S(2)}, u32[]{:S(2)}) collective-permute-start(s32[2,896]{1,0:T(2,128)S(1)} %get-tuple-element.101.routes), channel_id=1, source_target_pairs={{0,16},{8,24},{16,0},{24,8},{1,17},{9,25},{17,1},{25,9},{2,18},{10... | collective-permute-start | bytes 21512 | tf_op jit(solution)/shard_map/ppermute | solution.py:1357
  302.0 5.2 %copy-start = (f32[788,512]{1,0:T(8,128)S(1)}, f32[788,512]{1,0:T(8,128)}, u32[]{:S(2)}) copy-start(f32[788,512]{1,0:T(8,128)} %get-tuple-element.116) | copy-start | bytes 4841476
  307.2 1.2 copy-start.3
  307.2 2.0 copy-start.4
  307.3 2.6 copy-start.2
  308.5 2.4 copy-start.1
